TPU v7x, 256 devices: a whole 4x4x8 slice. The times are simulated.
256 devices in a mesh: dp: 4 (over y_lo, core), mp: 64 (over y_hi, z, x).
Axes of the slice: x: 4, y: 4 (y_hi: 2, y_lo: 2; y = y_hi * 2 + y_lo), z: 8, core: 2. Of those that a mesh axis runs over, the one named last changes fastest.
Arguments:
- table: bfloat16 [131072, 1024], P('mp'), may hold values from -200 to 200
- triples: int32 [32, 3], P('dp'), may hold values from 0 to 131071
- words: int32 [32, 61], P('dp'), may hold values from 0 to 131071
- labels: int32 [32], P('dp'), may hold values 0 or 1
- in_gain: float32 [1024], replicated, may hold values from 0.5 to 1.5
- up_weight: bfloat16 [1024, 4096], P(None, 'mp'), may hold values from -0.1875 to 0.1875
- down_weight: bfloat16 [4096, 1024], P('mp'), may hold values from -0.09375 to 0.09375
- out_gain: float32 [1024], P('mp'), may hold values from 0.5 to 1.5
- class_weight: float32 [1024], P('mp'), may hold values from -6 to 6
Outputs:
- encoded: bfloat16 [2048, 1024], P('dp', 'mp')
- scores: float32 [32], P('dp')
- class_grad: float32 [1024], P('mp')
All inputs are finite; a program needn't handle non-finite values. No bound on the sum of `labels` on one device may be relied on, other than what follows from the above.
Results may differ from a plain program's by a relative error of at most 0.0075.
Values may be sent and summed in bfloat16 or wider, within the bound.
No kernel may reach another device: no remote copies, remote signals or barrier semaphores. Data moves between devices by JAX's collectives and lax.ppermute only.
A program may use at most 64 MiB of HBM per device.

v0:
```python
import jax
import jax.numpy as jnp
from jax import lax
from jax.sharding import PartitionSpec as P


def in_blocks(array, dim, peers):
    shape = array.shape
    blocks = array.reshape(*shape[:dim], peers, shape[dim] // peers, *shape[dim + 1 :])
    return jnp.moveaxis(blocks, dim, 0)


def sent_and_summed(array, axis, dim):
    peers = lax.axis_size(axis)
    blocks = lax.all_to_all(in_blocks(array, dim, peers), axis, 0, 0, tiled=True)
    return jnp.sum(blocks, axis=0)


def from_everyone(array, axis):
    copies = jnp.broadcast_to(array, (lax.axis_size(axis), *array.shape))
    return lax.all_to_all(copies, axis, split_axis=0, concat_axis=0, tiled=True)


def over_copies(array, axis):
    return from_everyone(array, axis).sum(axis=0)


def in_one(arrays, axis):
    ends = [0]
    for a in arrays:
        ends.append(ends[-1] + a.size)
    running = over_copies(jnp.concatenate([a.ravel() for a in arrays]), axis)
    return tuple((running[b:e].reshape(a.shape) for a, b, e in zip(arrays, ends, ends[1:])))


def laid_out(blocks, dim):
    blocks = jnp.moveaxis(blocks, 0, dim)
    shape = blocks.shape
    return blocks.reshape(*shape[:dim], shape[dim] * shape[dim + 1], *shape[dim + 2 :])


def gathered_copies(array, axis, dim):
    return laid_out(from_everyone(array, axis), dim)


def normalize(values, first, second, width, gain):
    mean = first / width
    var = second / width - mean * mean
    return (values - mean[:, None]) * lax.rsqrt(var + 1e-05)[:, None] * gain


def own_rows(table, ids, place):
    entries = table.shape[0]
    local = ids - place * entries
    inside = (local >= 0) & (local < entries)
    picked = jnp.take(table, jnp.clip(local, 0, entries - 1), axis=0).astype(jnp.float32)
    return jnp.where(inside[:, None], picked, 0.0)


def on_device(
    table, triples, words, labels, in_gain, up_weight, down_weight, out_gain, class_weight
):
    ids = jnp.concatenate([triples, words], axis=1).reshape(-1)
    seq_len = triples.shape[1] + words.shape[1]
    tok_rows = ids.shape[0]
    width = table.shape[1]
    share = width // lax.axis_size("mp")
    place = lax.axis_index("mp")
    embed = sent_and_summed(own_rows(table, ids, place), "mp", 1)
    first, second = in_one((jnp.sum(embed, axis=1), jnp.sum(embed * embed, axis=1)), "mp")
    gain_cols = lax.dynamic_slice_in_dim(in_gain, place * share, share, 0)
    own = normalize(embed, first, second, width, gain_cols).astype(jnp.bfloat16)
    hidden = jnp.dot(gathered_copies(own, "mp", 1), up_weight, preferred_element_type=jnp.float32)
    active = jax.nn.gelu(hidden, approximate=False).astype(jnp.bfloat16)
    terms = jnp.dot(active, down_weight, preferred_element_type=jnp.float32)
    mixed = sent_and_summed(terms, "mp", 1)
    resid = own.astype(jnp.float32) + mixed
    first_out, second_out = in_one((jnp.sum(resid, axis=1), jnp.sum(resid * resid, axis=1)), "mp")
    encoded = normalize(resid, first_out, second_out, width, out_gain).astype(jnp.bfloat16)
    pooled = jnp.mean(
        encoded.astype(jnp.float32).reshape(tok_rows // seq_len, seq_len, share), axis=1
    )
    partial_score = jnp.dot(pooled, class_weight, precision=lax.Precision.HIGHEST)
    scores = over_copies(partial_score, "mp")
    diff = jax.nn.sigmoid(scores) - labels.astype(jnp.float32)
    class_grad = over_copies(jnp.dot(diff, pooled, precision=lax.Precision.HIGHEST), "dp")
    return (encoded, scores, class_grad)


def solution(mesh):
    return jax.shard_map(
        on_device,
        mesh=mesh,
        in_specs=(
            P("mp", None),
            P("dp", None),
            P("dp", None),
            P("dp"),
            P(),
            P(None, "mp"),
            P("mp", None),
            P("mp"),
            P("mp"),
        ),
        out_specs=(P("dp", "mp"), P("dp"), P("mp")),
        check_vma=False,
    )
```

profile of v0, /device:TPU:1, one launch (start us, length us, event | category | flops | bytes accessed | tf_op | source)
XLA Modules:
  0.0 238.9 jit_solution(10327107983273642680)
XLA Ops:
  0.6 0.8 copy.23
  1.4 0.8 broadcast_clamp_fusion
  2.4 0.8 compare_and_fusion
  3.1 5.5 %gather_fusion = bf16[512,1024]{1,0:T(8,128)(2,1)S(1)} fusion(bf16[2048,1024]{1,0:T(8,128)(2,1)} %param.9, s32[1024]{0:T(1024)S(1)} %pad_clamp_fusion), kind=kCustom, calls=%fused_computation | custom fusion | bytes 2099200 | tf_op jit(solution)/shard_map/jit(_take)/gather | solution.py:56
  8.6 0.5 copy.24
  9.3 0.3 select_bitcast_fusion
  9.6 64.0 %all_to_all.39 = f32[64,512,16]{1,2,0:T(8,128)S(1)} all-to-all(f32[64,512,16]{1,2,0:T(8,128)S(1)} %select_bitcast_fusion), channel_id=1, replica_groups=mesh['dp'=4,'mp'=64] {'mp'}, dimensions={0} | all-to-all | bytes 4194304 | tf_op jit(solution)/shard_map/all_to_all | solution.py:15
  73.5 0.2 fusion.86
  73.8 0.8 broadcast_in_dim.48
  74.6 9.1 %all-to-all-start.1 = ((f32[64,1,1024]{2,1,0:T(1,128)}), f32[64,1,1024]{2,1,0:T(1,128)S(1)}, u32[]{:S(2)}, u32[]{:S(2)}) async-start(f32[64,1,1024]{2,1,0:T(1,128)} %broadcast_in_dim.48), calls=%async_computation.1 | async-start | bytes 524288 | tf_op jit(solution)/shard_map/all_to_all | solution.py:21
  83.7 0.8 dynamic_slice.3
  84.5 11.5 %all-to-all-done.1 = f32[64,1,1024]{2,1,0:T(1,128)S(1)} async-done(((f32[64,1,1024]{2,1,0:T(1,128)}), f32[64,1,1024]{2,1,0:T(1,128)S(1)}, u32[]{:S(2)}, u32[]{:S(2)}) %all-to-all-start.1) | async-done | bytes 262176 | tf_op jit(solution)/shard_map/all_to_all | solution.py:21
  96.3 33.4 %all_to_all.40 = bf16[64,512,16]{1,2,0:T(8,128)(2,1)S(1)} all-to-all(bf16[64,512,16]{1,2,0:T(8,128)(2,1)S(1)} %broadcast_in_dim.49), channel_id=1, replica_groups=mesh['dp'=4,'mp'=64] {'mp'}, dimensions={0} | all-to-all | bytes 2097152 | tf_op jit(solution)/shard_map/all_to_all | solution.py:21
  129.7 2.3 fusion.10
  132.1 56.0 %all_to_all.41 = f32[64,512,16]{1,2,0:T(8,128)S(1)} all-to-all(f32[64,512,16]{1,2,0:T(8,128)} %bitcast.29), channel_id=1, replica_groups=mesh['dp'=4,'mp'=64] {'mp'}, dimensions={0} | all-to-all | bytes 4194304 | tf_op jit(solution)/shard_map/all_to_all | solution.py:15
  188.3 0.8 broadcast_in_dim.50
  189.1 8.6 %all-to-all-start.4 = ((f32[64,1,1024]{2,1,0:T(1,128)}), f32[64,1,1024]{2,1,0:T(1,128)S(1)}, u32[]{:S(2)}, u32[]{:S(2)}) async-start(f32[64,1,1024]{2,1,0:T(1,128)} %broadcast_in_dim.50), calls=%async_computation.4 | async-start | bytes 524288 | tf_op jit(solution)/shard_map/all_to_all | solution.py:21
  198.0 11.9 %all-to-all-done.4 = f32[64,1,1024]{2,1,0:T(1,128)S(1)} async-done(((f32[64,1,1024]{2,1,0:T(1,128)}), f32[64,1,1024]{2,1,0:T(1,128)S(1)}, u32[]{:S(2)}, u32[]{:S(2)}) %all-to-all-start.4) | async-done | bytes 262176 | tf_op jit(solution)/shard_map/all_to_all | solution.py:21
  210.6 15.5 %all_to_all.42 = f32[64,1,8]{2,1,0:T(1,128)S(1)} all-to-all(f32[64,1,8]{2,1,0:T(1,128)S(1)} %broadcast_in_dim.51), channel_id=1, replica_groups=mesh['dp'=4,'mp'=64] {'mp'}, dimensions={0} | all-to-all | bytes 4096 | tf_op jit(solution)/shard_map/all_to_all | solution.py:21
  226.4 0.6 broadcast_in_dim.52
  227.0 8.3 %all-to-all-start.6 = ((f32[4,1,16]{2,1,0:T(1,128)}), f32[4,1,16]{2,1,0:T(1,128)S(1)}, u32[]{:S(2)}, u32[]{:S(2)}) async-start(f32[4,1,16]{2,1,0:T(1,128)} %broadcast_in_dim.52), calls=%async_computation.6 | async-start | bytes 4096 | tf_op jit(solution)/shard_map/all_to_all | solution.py:21
  235.3 0.7 multiply_convert_fusion.2
  236.0 2.4 all-to-all-done.6
  238.3 0.5 reduce_sum.115
  (42 shorter events, 2.2 us)
Async XLA Ops:
  0.6 129.1 %copy-start = (bf16[64,1024]{1,0:T(8,128)(2,1)S(1)}, bf16[64,1024]{1,0:T(8,128)(2,1)}, u32[]{:S(2)}) copy-start(bf16[64,1024]{1,0:T(8,128)(2,1)} %param.15) | copy-start | bytes 393220
  73.8 56.0 %copy-start.4 = (bf16[1024,64]{0,1:T(8,128)(2,1)S(1)}, bf16[1024,64]{0,1:T(8,128)(2,1)}, u32[]{:S(2)}) copy-start(bf16[1024,64]{0,1:T(8,128)(2,1)} %param.14) | copy-start | bytes 393220
  74.6 21.3 %all-to-all-start.1 = ((f32[64,1,1024]{2,1,0:T(1,128)}), f32[64,1,1024]{2,1,0:T(1,128)S(1)}, u32[]{:S(2)}, u32[]{:S(2)}) async-start(f32[64,1,1024]{2,1,0:T(1,128)} %broadcast_in_dim.48), calls=%async_computation.1 | async-start | bytes 524288 | tf_op jit(solution)/shard_map/all_to_all | solution.py:21
  188.1 22.2 %copy-start.1 = (f32[16]{0:T(128)S(1)}, f32[16]{0:T(128)}, u32[]{:S(2)}) copy-start(f32[16]{0:T(128)} %param.16) | copy-start | bytes 196
  188.1 22.4 %copy-start.3 = (f32[16]{0:T(128)S(1)}, f32[16]{0:T(128)}, u32[]{:S(2)}) copy-start(f32[16]{0:T(128)} %param.17) | copy-start | bytes 196
  188.1 38.2 %copy-start.5 = (s32[8]{0:T(128)S(1)}, s32[8]{0:T(128)}, u32[]{:S(2)}) copy-start(s32[8]{0:T(128)} %param.12) | copy-start | bytes 100
  189.1 20.8 %all-to-all-start.4 = ((f32[64,1,1024]{2,1,0:T(1,128)}), f32[64,1,1024]{2,1,0:T(1,128)S(1)}, u32[]{:S(2)}, u32[]{:S(2)}) async-start(f32[64,1,1024]{2,1,0:T(1,128)} %broadcast_in_dim.50), calls=%async_computation.4 | async-start | bytes 524288 | tf_op jit(solution)/shard_map/all_to_all | solution.py:21
  226.2 12.6 %copy-start.2 = (f32[8]{0:T(128)}, f32[8]{0:T(128)S(1)}, u32[]{:S(2)}) copy-start(f32[8]{0:T(128)S(1)} %reduce_sum.114) | copy-start | bytes 100
  227.0 11.3 %all-to-all-start.6 = ((f32[4,1,16]{2,1,0:T(1,128)}), f32[4,1,16]{2,1,0:T(1,128)S(1)}, u32[]{:S(2)}, u32[]{:S(2)}) async-start(f32[4,1,16]{2,1,0:T(1,128)} %broadcast_in_dim.52), calls=%async_computation.6 | async-start | bytes 4096 | tf_op jit(solution)/shard_map/all_to_all | solution.py:21
where the time goes:
time: 239 us
  blocking collectives  169 us (71%)
  starting transfers between devices  25.9 us (11%)
  waiting for transfers between devices  25.7 us (11%)
  local copies, waits for them, and re-layouts  10.7 us (4%)
  other arithmetic  4.3 us (2%)
  matrix products  2.6 us (1%)
    all_to_all x2, blocking collectives, sent_and_summed(): lax.all_to_all(in_blocks(array, dim, peers), axis, 0, 0, tiled=True)  120 us
    all_to_all x2, blocking collectives, from_everyone(): return lax.all_to_all(copies, axis, split_axis=0, concat_axis=0, tiled=True)  48.9 us
    all_to_all x3, starting transfers between devices, from_everyone(): return lax.all_to_all(copies, axis, split_axis=0, concat_axis=0, tiled=True)  25.9 us
    all_to_all x3, waiting for transfers between devices, from_everyone(): return lax.all_to_all(copies, axis, split_axis=0, concat_axis=0, tiled=True)  25.7 us
    gather x2, local copies, waits for them, and re-layouts, own_rows(): jnp.take(table, jnp.clip(local, 0, entries - 1), axis=0).astype(jnp.float32)  6 us
  transfers between devices with their start and end apart: 3, of which 3 were waited for; matrix products, arithmetic and copies ran while one was open for 1% of the time, Pallas kernels for 0%

commit v1 on v0

v1 whole, which is shorter than its diff:
```python
import jax
import jax.numpy as jnp
from jax import lax
from jax.sharding import Mesh
from jax.sharding import PartitionSpec as P

MP = ("yh", "z", "x")
DP = ("yl", "core")
ACT = ("yl", "core", "yh", "x")


def exchange(blocks, axes):
    return lax.all_to_all(blocks, axes, split_axis=0, concat_axis=0, tiled=True)


def to_everyone(array, axes):
    return exchange(jnp.broadcast_to(array, (lax.axis_size(axes), *array.shape)), axes)


def rounded(x):
    return lax.reduce_precision(x, exponent_bits=8, mantissa_bits=7)


def thirds(x):
    high = rounded(x)
    middle = rounded(x - high)
    return high, middle, rounded(x - high - middle)


def standardize(values):
    width = values.shape[1]
    mean = jnp.sum(values, axis=1, keepdims=True) / width
    var = jnp.sum(values * values, axis=1, keepdims=True) / width - mean * mean
    return (values - mean) * lax.rsqrt(var + 1e-05)


def on_device(
    table, triples, words, labels, in_gain, up_weight, down_weight, out_gain, class_weight
):
    bf16, f32 = jnp.bfloat16, jnp.float32
    peers = lax.axis_size(MP)
    place = lax.axis_index(MP)
    ids = jnp.concatenate([triples, words], axis=1).reshape(-1)
    seq_len = triples.shape[1] + words.shape[1]
    tok_rows = ids.shape[0]
    width = table.shape[1]
    own_toks = tok_rows // peers
    share = width // peers

    parts = lax.axis_size(DP)
    part = lax.axis_index(DP)
    units = up_weight.shape[1] // parts
    up_part = lax.dynamic_slice_in_dim(up_weight.T, part * units, units, 0)
    down_part = lax.dynamic_slice_in_dim(down_weight, part * units, units, 0)
    weights = to_everyone(jnp.concatenate([up_part, down_part], axis=0), "z")
    up_rows = weights[:, :units].reshape(-1, width)
    down_rows = weights[:, units:].reshape(-1, width)

    entries = table.shape[0]
    local = ids - place * entries
    inside = (local >= 0) & (local < entries)
    picked = jnp.take(table, jnp.clip(local, 0, entries - 1), axis=0)
    picked = jnp.where(inside[:, None], picked, jnp.zeros((), bf16))
    lanes = 128
    per_row = lanes // share
    score_weight = jnp.tile(out_gain * class_weight, per_row)
    here = jnp.arange(lanes) // share == place % per_row
    score_weight = jnp.where(here, score_weight, 0.0)
    extra = jnp.zeros((own_toks, lanes), f32)
    for row, third in enumerate(thirds(score_weight)):
        extra = extra.at[row].set(third)
    extra = jnp.broadcast_to(extra.astype(bf16), (peers, own_toks, lanes))
    sent = jnp.concatenate([picked.reshape(peers, own_toks, width), extra], axis=2)
    got = exchange(sent, MP)
    embed = jnp.sum(got[:, :, :width].astype(f32), axis=0)
    score_weight = got[:, :, width:].astype(f32).reshape(-1, per_row, own_toks, lanes)
    score_weight = jnp.sum(score_weight, axis=(1, 2)).reshape(1, width)

    normed = (standardize(embed) * in_gain).astype(bf16)
    everyone = to_everyone(normed, ACT)
    hidden = lax.dot_general(
        everyone.reshape(-1, width), up_rows, (((1,), (1,)), ((), ())), preferred_element_type=f32
    )
    active = jax.nn.gelu(hidden, approximate=False).astype(bf16)
    terms = jnp.dot(active, down_rows, preferred_element_type=f32).astype(bf16)
    terms = exchange(terms.reshape(everyone.shape), ACT)
    resid = normed.astype(f32) + jnp.sum(terms.astype(f32), axis=0)
    level = standardize(resid)
    score = jnp.sum(level * score_weight) / seq_len

    blocks = level.reshape(own_toks, peers, share).transpose(1, 0, 2).reshape(peers, 1, -1)
    sent = jnp.concatenate([blocks, jnp.full_like(blocks, score)], axis=1)
    got = exchange(sent, MP)
    encoded = (got[:, 0].reshape(tok_rows, share) * out_gain).astype(bf16)
    scores = jnp.sum(got[:, 1, 0].reshape(tok_rows // seq_len, -1), axis=1)
    pooled = jnp.mean(
        encoded.astype(f32).reshape(tok_rows // seq_len, seq_len, share), axis=1
    )
    diff = jax.nn.sigmoid(scores) - labels.astype(f32)
    grad = jnp.sum(diff[:, None] * pooled, axis=0)
    grad = grad + lax.ppermute(grad, "core", [(0, 1), (1, 0)])
    grad = grad + lax.ppermute(grad, "yl", [(0, 1), (1, 0)])
    return encoded, scores, grad


def solution(mesh):
    parts = Mesh(mesh.devices.reshape(2, 2, 2, 8, 4), ("yl", "core", "yh", "z", "x"))
    return jax.shard_map(
        on_device,
        mesh=parts,
        in_specs=(
            P(MP, None),
            P(DP, None),
            P(DP, None),
            P(DP),
            P(),
            P(None, MP),
            P(MP, None),
            P(MP),
            P(MP),
        ),
        out_specs=(P(DP, MP), P(DP), P(MP)),
        check_vma=False,
    )
```

time: 239 us -> 140 us (0.59)
  blocking collectives: 169 us -> 15.4 us
  waiting for transfers between devices: 25.7 us -> 66.9 us
  starting transfers between devices: 25.9 us -> 35.8 us
    all_to_all x4 -> x1, blocking collectives: 169 us -> 15.4 us  [exchange(): return lax.all_to_all(blocks, axes, split_axis=0, concat_axis=0, tiled=True)]
    all_to_all x3 -> x4, waiting for transfers between devices: 25.7 us -> 65.5 us  [exchange(): return lax.all_to_all(blocks, axes, split_axis=0, concat_axis=0, tiled=True)]
    all_to_all x3 -> x4, starting transfers between devices: 25.9 us -> 32.9 us  [exchange(): return lax.all_to_all(blocks, axes, split_axis=0, concat_axis=0, tiled=True)]
    ppermute x0 -> x2, starting transfers between devices: none -> 2.88 us  [the longest x1 1.96 us: on_device(): grad = grad + lax.ppermute(grad, 'core', [(0, 1), (1, 0)])]
    gather x2 -> x1, local copies, waits for them, and re-layouts: 6 us -> 5.46 us  [on_device(): picked = jnp.take(table, jnp.clip(local, 0, entries - 1), axis=0)]
  transfers between devices with their start and end apart: 3 -> 6, of which waited for: 3 -> 6; matrix products, arithmetic and copies ran while one was open for 1% -> 2% of each run, Pallas kernels for 0% -> 0%
where the time goes in v1:
time: 140 us
  waiting for transfers between devices  66.9 us (48%)
  starting transfers between devices  35.8 us (26%)
  blocking collectives  15.4 us (11%)
  local copies, waits for them, and re-layouts  11.4 us (8%)
  other arithmetic  6.64 us (5%)
  matrix products  1.77 us (1%)
  between operations  1.61 us (1%)
    all_to_all x4, waiting for transfers between devices, exchange(): return lax.all_to_all(blocks, axes, split_axis=0, concat_axis=0, tiled=True)  65.5 us
    all_to_all x4, starting transfers between devices, exchange(): return lax.all_to_all(blocks, axes, split_axis=0, concat_axis=0, tiled=True)  32.9 us
    all_to_all x1, blocking collectives, exchange(): return lax.all_to_all(blocks, axes, split_axis=0, concat_axis=0, tiled=True)  15.4 us
    gather x1, local copies, waits for them, and re-layouts, on_device(): picked = jnp.take(table, jnp.clip(local, 0, entries - 1), axis=0)  5.46 us
  transfers between devices with their start and end apart: 6, of which 6 were waited for; matrix products, arithmetic and copies ran while one was open for 2% of the time, Pallas kernels for 0%

profile of v1, /device:TPU:1, one launch (start us, length us, event | category | flops | bytes accessed | tf_op | source)
XLA Modules:
  0.0 139.6 jit_solution(1016512632382992370)
XLA Ops:
  0.7 0.8 copy.24
  1.5 0.8 broadcast_clamp_fusion
  2.4 0.8 compare_and_fusion.1
  4.1 5.5 %gather_fusion = bf16[512,1024]{1,0:T(8,128)(2,1)S(1)} fusion(bf16[2048,1024]{1,0:T(8,128)(2,1)} %param.15, s32[1024]{0:T(1024)S(1)} %pad_clamp_fusion), kind=kCustom, calls=%fused_computation | custom fusion | bytes 2099200 | tf_op jit(solution)/shard_map/jit(_take)/gather | solution.py:62
  9.9 1.1 pad_maximum_fusion
  11.0 15.1 %all-to-all-start = ((bf16[64,8,1152]{2,1,0:T(8,128)(2,1)}), bf16[64,8,1152]{2,1,0:T(8,128)(2,1)S(1)}, u32[]{:S(2)}, u32[]{:S(2)}) async-start(bf16[64,8,1152]{2,1,0:T(8,128)(2,1)} %pad_maximum_fusion), calls=%async_computation | async-start | bytes 2359296 | tf_op jit(solution)/shard_map/all_to_all | solution.py:13
  26.1 0.8 dynamic-slice_bitcast_fusion
  26.9 29.9 %all-to-all-done = bf16[64,8,1152]{2,1,0:T(8,128)(2,1)S(1)} async-done(((bf16[64,8,1152]{2,1,0:T(8,128)(2,1)}), bf16[64,8,1152]{2,1,0:T(8,128)(2,1)S(1)}, u32[]{:S(2)}, u32[]{:S(2)}) %all-to-all-start) | async-done | bytes 1179680 | tf_op jit(solution)/shard_map/all_to_all | solution.py:13
  56.8 0.8 broadcast_in_dim.52
  57.6 4.4 %all-to-all-start.2 = ((bf16[8,32,1024]{2,1,0:T(8,128)(2,1)}), bf16[8,32,1024]{2,1,0:T(8,128)(2,1)S(1)}, u32[]{:S(2)}, u32[]{:S(2)}) async-start(bf16[8,32,1024]{2,1,0:T(8,128)(2,1)} %broadcast_in_dim.52), calls=%async_computation.2 | async-start | bytes 1048576 | tf_op jit(solution)/shard_map/all_to_all | solution.py:13
  62.0 0.8 convert_reduce_fusion
  63.1 13.7 %all-to-all-done.2 = bf16[8,32,1024]{2,1,0:T(8,128)(2,1)S(1)} async-done(((bf16[8,32,1024]{2,1,0:T(8,128)(2,1)}), bf16[8,32,1024]{2,1,0:T(8,128)(2,1)S(1)}, u32[]{:S(2)}, u32[]{:S(2)}) %all-to-all-start.2) | async-done | bytes 524320 | tf_op jit(solution)/shard_map/all_to_all | solution.py:13
  76.8 0.8 broadcast_in_dim.51
  77.6 8.5 %all-to-all-start.1 = ((bf16[32,8,1024]{2,1,0:T(8,128)(2,1)}), bf16[32,8,1024]{2,1,0:T(8,128)(2,1)S(1)}, u32[]{:S(2)}, u32[]{:S(2)}) async-start(bf16[32,8,1024]{2,1,0:T(8,128)(2,1)} %broadcast_in_dim.51), calls=%async_computation.1 | async-start | bytes 1048576 | tf_op jit(solution)/shard_map/all_to_all | solution.py:13
  86.2 11.1 %all-to-all-done.1 = bf16[32,8,1024]{2,1,0:T(8,128)(2,1)S(1)} async-done(((bf16[32,8,1024]{2,1,0:T(8,128)(2,1)}), bf16[32,8,1024]{2,1,0:T(8,128)(2,1)S(1)}, u32[]{:S(2)}, u32[]{:S(2)}) %all-to-all-start.1) | async-done | bytes 524320 | tf_op jit(solution)/shard_map/all_to_all | solution.py:13
  97.2 1.8 %fusion = bf16[32,8,1024]{2,1,0:T(8,128)(2,1)} fusion(bf16[128,1024]{1,0:T(8,128)(2,1)S(1)} %bitcast.29, bf16[128,1024]{1,0:T(8,128)(2,1)S(1)} %bitcast.28, bf16[32,8,1024]{2,1,0:T(8,128)(2,1)S(1)} %all-to-all-done.1), kind=kOutput, calls=%fused_computation.4 | convolution fusion | flops 136609792 | bytes 1572864 | tf_op jit(solution)/shard_map/dot_general | solution.py:85
  99.0 4.9 %all-to-all-start.3 = ((bf16[32,8,1024]{2,1,0:T(8,128)(2,1)}), bf16[32,8,1024]{2,1,0:T(8,128)(2,1)S(1)}, u32[]{:S(2)}, u32[]{:S(2)}) async-start(bf16[32,8,1024]{2,1,0:T(8,128)(2,1)} %fusion), calls=%async_computation.3 | async-start | bytes 1048576 | tf_op jit(solution)/shard_map/all_to_all | solution.py:13
  104.2 10.9 %all-to-all-done.3 = bf16[32,8,1024]{2,1,0:T(8,128)(2,1)S(1)} async-done(((bf16[32,8,1024]{2,1,0:T(8,128)(2,1)}), bf16[32,8,1024]{2,1,0:T(8,128)(2,1)S(1)}, u32[]{:S(2)}, u32[]{:S(2)}) %all-to-all-start.3) | async-done | bytes 524320 | tf_op jit(solution)/shard_map/all_to_all | solution.py:13
  115.6 0.7 multiply_reduce_fusion
  117.3 15.4 %all_to_all.25 = f32[64,2,128]{2,1,0:T(2,128)S(1)} all-to-all(f32[64,2,128]{2,1,0:T(2,128)S(1)} %concatenate.21.clone), channel_id=1, replica_groups=mesh['yl'=2,'core'=2,'yh'=2,'z'=8,'x'=4] {'yh','z','x'}, dimensions={0} | all-to-all | bytes 131072 | tf_op jit(solution)/shard_map/all_to_all | solution.py:13
  133.9 2.0 %collective-permute-start = (f32[16]{0:T(128)S(1)}, f32[16]{0:T(128)S(1)}, u32[]{:S(2)}, u32[]{:S(2)}) collective-permute-start(f32[16]{0:T(128)S(1)} %multiply_reduce_fusion.3), channel_id=1, source_target_pairs={{0,64},{64,0},{1,65},{65,1},{2,66},{66,2},{3,67},{67,3},{4,68},{68... | collective-permute-start | bytes 200 | tf_op jit(solution)/shard_map/ppermute | solution.py:101
  136.7 0.9 collective-permute-start.1
  137.6 0.7 copy.27
  138.3 0.8 collective-permute-done.1
  (57 shorter events, 5.1 us)
Async XLA Ops:
  0.6 25.5 %copy-start = (bf16[64,1024]{1,0:T(8,128)(2,1)S(1)}, bf16[64,1024]{1,0:T(8,128)(2,1)}, u32[]{:S(2)}) copy-start(bf16[64,1024]{1,0:T(8,128)(2,1)} %param.21) | copy-start | bytes 393220
  11.0 45.8 %all-to-all-start = ((bf16[64,8,1152]{2,1,0:T(8,128)(2,1)}), bf16[64,8,1152]{2,1,0:T(8,128)(2,1)S(1)}, u32[]{:S(2)}, u32[]{:S(2)}) async-start(bf16[64,8,1152]{2,1,0:T(8,128)(2,1)} %pad_maximum_fusion), calls=%async_computation | async-start | bytes 2359296 | tf_op jit(solution)/shard_map/all_to_all | solution.py:13
  57.6 5.4 %copy-start.1 = (f32[1024]{0:T(1024)S(1)}, f32[1024]{0:T(1024)}, u32[]{:S(2)}) copy-start(f32[1024]{0:T(1024)} %param.19) | copy-start | bytes 12292
  57.6 19.1 %all-to-all-start.2 = ((bf16[8,32,1024]{2,1,0:T(8,128)(2,1)}), bf16[8,32,1024]{2,1,0:T(8,128)(2,1)S(1)}, u32[]{:S(2)}, u32[]{:S(2)}) async-start(bf16[8,32,1024]{2,1,0:T(8,128)(2,1)} %broadcast_in_dim.52), calls=%async_computation.2 | async-start | bytes 1048576 | tf_op jit(solution)/shard_map/all_to_all | solution.py:13
  77.6 19.6 %all-to-all-start.1 = ((bf16[32,8,1024]{2,1,0:T(8,128)(2,1)}), bf16[32,8,1024]{2,1,0:T(8,128)(2,1)S(1)}, u32[]{:S(2)}, u32[]{:S(2)}) async-start(bf16[32,8,1024]{2,1,0:T(8,128)(2,1)} %broadcast_in_dim.51), calls=%async_computation.1 | async-start | bytes 1048576 | tf_op jit(solution)/shard_map/all_to_all | solution.py:13
  99.0 16.1 %all-to-all-start.3 = ((bf16[32,8,1024]{2,1,0:T(8,128)(2,1)}), bf16[32,8,1024]{2,1,0:T(8,128)(2,1)S(1)}, u32[]{:S(2)}, u32[]{:S(2)}) async-start(bf16[32,8,1024]{2,1,0:T(8,128)(2,1)} %fusion), calls=%async_computation.3 | async-start | bytes 1048576 | tf_op jit(solution)/shard_map/all_to_all | solution.py:13
  115.2 17.8 %copy-start.2 = (f32[16]{0:T(128)S(1)}, f32[16]{0:T(128)}, u32[]{:S(2)}) copy-start(f32[16]{0:T(128)} %param.22) | copy-start | bytes 196
  115.6 18.2 %copy-start.4 = (s32[8]{0:T(128)S(1)}, s32[8]{0:T(128)}, u32[]{:S(2)}) copy-start(s32[8]{0:T(128)} %param.18) | copy-start | bytes 100
  133.8 5.8 %copy-start.3 = (f32[8]{0:T(128)}, f32[8]{0:T(128)S(1)}, u32[]{:S(2)}) copy-start(f32[8]{0:T(128)S(1)} %reduce_sum.122) | copy-start | bytes 100
  133.9 2.8 %collective-permute-start = (f32[16]{0:T(128)S(1)}, f32[16]{0:T(128)S(1)}, u32[]{:S(2)}, u32[]{:S(2)}) collective-permute-start(f32[16]{0:T(128)S(1)} %multiply_reduce_fusion.3), channel_id=1, source_target_pairs={{0,64},{64,0},{1,65},{65,1},{2,66},{66,2},{3,67},{67,3},{4,68},{68... | collective-permute-start | bytes 200 | tf_op jit(solution)/shard_map/ppermute | solution.py:101
  136.7 2.4 %collective-permute-start.1 = (f32[16]{0:T(128)S(1)}, f32[16]{0:T(128)S(1)}, u32[]{:S(2)}, u32[]{:S(2)}) collective-permute-start(f32[16]{0:T(128)S(1)} %add.100), channel_id=1, source_target_pairs={{0,128},{128,0},{1,129},{129,1},{2,130},{130,2},{3,131},{131,3},{4... | collective-permute-start | bytes 200 | tf_op jit(solution)/shard_map/ppermute | solution.py:102

commit v2 on v1

v2 whole, which is shorter than its diff:
```python
import jax
import jax.numpy as jnp
from jax import lax
from jax.sharding import Mesh
from jax.sharding import PartitionSpec as P

MP = ("yh", "z", "x")
DP = ("yl", "core")
ACT = ("yl", "core", "yh", "x")
LANES = 128


def exchange(blocks, axes):
    return lax.all_to_all(blocks, axes, split_axis=0, concat_axis=0, tiled=True)


def to_everyone(array, axes):
    return exchange(jnp.broadcast_to(array, (lax.axis_size(axes), *array.shape)), axes)


def shifted(array, axis):
    peers = lax.axis_size(axis)
    return [array] + [
        lax.ppermute(array, axis, [(i, (i + step) % peers) for i in range(peers)])
        for step in range(1, peers)
    ]


def swapped(array, axis):
    return lax.ppermute(array, axis, [(0, 1), (1, 0)])


def rounded(x):
    return lax.reduce_precision(x, exponent_bits=8, mantissa_bits=7)


def thirds(x):
    high = rounded(x)
    middle = rounded(x - high)
    return high, middle, rounded(x - high - middle)


def standardize(values):
    width = values.shape[1]
    mean = jnp.sum(values, axis=1, keepdims=True) / width
    var = jnp.sum(values * values, axis=1, keepdims=True) / width - mean * mean
    return (values - mean) * lax.rsqrt(var + 1e-05)


def on_device(
    table, triples, words, labels, in_gain, up_weight, down_weight, out_gain, class_weight
):
    bf16, f32 = jnp.bfloat16, jnp.float32
    peers = lax.axis_size(MP)
    place = lax.axis_index(MP)
    ids = jnp.concatenate([triples, words], axis=1).reshape(1, -1)
    seq_len = triples.shape[1] + words.shape[1]
    toks = ids.shape[1]
    entries, width = table.shape
    slots = toks // peers
    share = width // peers

    owner = ids // entries
    key = owner * toks + jnp.arange(toks)[None]
    spot = jnp.sum(key.reshape(-1, 1) < key, axis=0, keepdims=True)
    first = jnp.sum(owner.reshape(-1, 1) < owner, axis=0, keepdims=True)
    trip = (spot - first) // peers
    trips = jnp.max(trip) + 1
    trips = jnp.maximum(trips, swapped(trips, "core"))
    trips = jnp.maximum(trips, swapped(trips, "yl"))
    mine = owner == place
    to_peer = (spot % peers == jnp.arange(peers)[:, None]) & mine
    kept = spot == jnp.arange(slots)[:, None] * peers + place
    sender = jnp.sum(jnp.where(kept, owner, 0), axis=1, keepdims=True)
    sent_in = jnp.sum(jnp.where(kept, trip, 0), axis=1, keepdims=True)
    from_peer = sender == jnp.arange(peers)[None]

    def rows_of(now):
        chosen = to_peer & (trip == now)
        local = jnp.sum(jnp.where(chosen, ids - place * entries, 0), axis=1)
        return jnp.take(table, local, axis=0, mode="clip").reshape(peers, 1, width)

    def taken(now, rows):
        picks = (from_peer & (sent_in == now)).astype(bf16)
        return jnp.dot(picks, rows, preferred_element_type=f32)

    score_weight = jnp.concatenate(thirds(out_gain * class_weight)).astype(bf16)
    score_weight = jnp.pad(score_weight, (0, width - score_weight.size))
    extra = jnp.broadcast_to(score_weight, (peers, 1, width))
    got = exchange(jnp.concatenate([rows_of(0), extra], axis=1), MP)
    embed = taken(0, got[:, 0])
    score_weight = got[:, 1, : 3 * share].astype(f32).reshape(peers, 3, share)
    score_weight = jnp.sum(score_weight, axis=1).reshape(1, width)

    parts = lax.axis_size(DP)
    part = lax.axis_index(DP)
    units = up_weight.shape[1] // parts
    up_part = lax.dynamic_slice_in_dim(up_weight.T, part * units, units, 0)
    down_part = lax.dynamic_slice_in_dim(down_weight, part * units, units, 0)
    weights = shifted(jnp.concatenate([up_part, down_part], axis=0), "z")
    up_rows = jnp.concatenate([w[:units] for w in weights], axis=0)
    down_rows = jnp.concatenate([w[units:] for w in weights], axis=0)

    def another(state):
        now, embed = state
        return now + 1, embed + taken(now, exchange(rows_of(now), MP)[:, 0])

    _, embed = lax.while_loop(lambda state: state[0] < trips, another, (jnp.int32(1), embed))

    normed = (standardize(embed) * in_gain).astype(bf16)
    everyone = to_everyone(normed, ACT)
    hidden = lax.dot_general(
        everyone.reshape(-1, width), up_rows, (((1,), (1,)), ((), ())), preferred_element_type=f32
    )
    active = jax.nn.gelu(hidden, approximate=False).astype(bf16)
    terms = jnp.dot(active, down_rows, preferred_element_type=f32).astype(bf16)
    terms = exchange(terms.reshape(everyone.shape), ACT)
    resid = normed.astype(f32) + jnp.sum(terms.astype(f32), axis=0)
    level = standardize(resid)
    score = jnp.sum(level * score_weight, axis=1)

    blocks = level.reshape(slots, peers, share).transpose(1, 0, 2).reshape(peers, 1, -1)
    score = jnp.broadcast_to(jnp.pad(score, (0, LANES - slots)), (peers, 1, LANES))
    got = exchange(jnp.concatenate([blocks, score], axis=2), MP)
    level = got[:, 0, : slots * share].reshape(peers, slots, share)
    by_spot = (level * out_gain).astype(bf16).transpose(1, 0, 2).reshape(toks, share)
    score = got[:, 0, slots * share :][:, :slots].T.reshape(1, toks)
    where = spot == jnp.arange(toks)[:, None]
    encoded = lax.dot_general(
        by_spot, where.astype(bf16), (((0,), (0,)), ((), ())), preferred_element_type=f32
    )
    triple = jnp.arange(toks // seq_len)[:, None]
    of_triple = jnp.sum(jnp.where(where, jnp.arange(toks)[None] // seq_len, 0), axis=1)
    scores = jnp.sum(jnp.where(of_triple[None] == triple, score, 0.0), axis=1) / seq_len
    diff = jax.nn.sigmoid(scores) - labels.astype(f32)
    pooled = jnp.mean(encoded.reshape(share, toks // seq_len, seq_len), axis=2)
    grad = jnp.sum(diff[None] * pooled, axis=1)
    grad = grad + swapped(grad, "core")
    grad = grad + swapped(grad, "yl")
    return encoded.T.astype(bf16), scores, grad


def solution(mesh):
    parts = Mesh(mesh.devices.reshape(2, 2, 2, 8, 4), ("yl", "core", "yh", "z", "x"))
    return jax.shard_map(
        on_device,
        mesh=parts,
        in_specs=(
            P(MP, None),
            P(DP, None),
            P(DP, None),
            P(DP),
            P(),
            P(None, MP),
            P(MP, None),
            P(MP),
            P(MP),
        ),
        out_specs=(P(DP, MP), P(DP), P(MP)),
        check_vma=False,
    )
```

time: 140 us -> 119 us (0.85)
  waiting for transfers between devices: 66.9 us -> 46.9 us
  starting transfers between devices: 35.8 us -> 51.5 us
  blocking collectives: 15.4 us -> 0 us
  local copies, waits for them, and re-layouts: 11.4 us -> 9.41 us
    ppermute x2 -> x11, starting transfers between devices: 2.88 us -> 25.1 us  [the longest x7 17.7 us: shifted(): lax.ppermute(array, axis, [(i, (i + step) % peers) for i in range(peers)])]
    all_to_all x4, waiting for transfers between devices: 65.5 us -> 45 us  [exchange(): return lax.all_to_all(blocks, axes, split_axis=0, concat_axis=0, tiled=True)]
    all_to_all x1 -> x0, blocking collectives: 15.4 us -> none  [exchange(): return lax.all_to_all(blocks, axes, split_axis=0, concat_axis=0, tiled=True)]
    all_to_all x4, starting transfers between devices: 32.9 us -> 26.3 us  [exchange(): return lax.all_to_all(blocks, axes, split_axis=0, concat_axis=0, tiled=True)]
    gather x1, local copies, waits for them, and re-layouts: 5.46 us -> 3.52 us  [rows_of(): return jnp.take(table, local, axis=0, mode='clip').reshape(peers, 1, width)]
    concatenate x1 -> x3, local copies, waits for them, and re-layouts: 0.03 us -> 1.68 us  [the longest x1 0.96 us: on_device(): got = exchange(jnp.concatenate([rows_of(0), extra], axis=1), MP)]
  transfers between devices with their start and end apart: 6 -> 15, of which waited for: 6 -> 7; matrix products, arithmetic and copies ran while one was open for 2% -> 9% of each run, Pallas kernels for 0% -> 0%
where the time goes in v2:
time: 119 us
  starting transfers between devices  51.5 us (43%)
  waiting for transfers between devices  46.9 us (39%)
  local copies, waits for them, and re-layouts  9.41 us (8%)
  other arithmetic  5.94 us (5%)
  between operations  2.84 us (2%)
  matrix products  2.24 us (2%)
    all_to_all x4, waiting for transfers between devices, exchange(): return lax.all_to_all(blocks, axes, split_axis=0, concat_axis=0, tiled=True)  45 us
    all_to_all x4, starting transfers between devices, exchange(): return lax.all_to_all(blocks, axes, split_axis=0, concat_axis=0, tiled=True)  26.3 us
    ppermute x7, starting transfers between devices, shifted(): lax.ppermute(array, axis, [(i, (i + step) % peers) for i in range(peers)])  17.7 us
    ppermute x4, starting transfers between devices, swapped(): return lax.ppermute(array, axis, [(0, 1), (1, 0)])  7.47 us
    gather x1, local copies, waits for them, and re-layouts, rows_of(): return jnp.take(table, local, axis=0, mode='clip').reshape(peers, 1, width)  3.52 us
  transfers between devices with their start and end apart: 15, of which 7 were waited for; matrix products, arithmetic and copies ran while one was open for 9% of the time, Pallas kernels for 0%

profile of v2, /device:TPU:1, one launch (start us, length us, event | category | flops | bytes accessed | tf_op | source)
XLA Modules:
  0.0 118.8 jit_solution(13259876524514519889)
XLA Ops:
  0.6 0.8 constant_dynamic-update-slice_fusion
  1.4 2.5 %collective-permute-start.2 = (bf16[32,1024]{1,0:T(8,128)(2,1)S(1)}, bf16[32,1024]{1,0:T(8,128)(2,1)S(1)}, u32[]{:S(2)}, u32[]{:S(2)}) collective-permute-start(bf16[32,1024]{1,0:T(8,128)(2,1)S(1)} %pad_maximum_fusion.2), channel_id=1, source_target_pairs={{0,4},{4,8},{8,12},{12,16},{16,20},{20,24},{24,28},{28,0},{1,5},{5... | collective-permute-start | bytes 196616 | tf_op jit(solution)/shard_map/ppermute | solution.py:24
  4.0 3.0 %collective-permute-start.3 = (bf16[32,1024]{1,0:T(8,128)(2,1)S(1)}, bf16[32,1024]{1,0:T(8,128)(2,1)S(1)}, u32[]{:S(2)}, u32[]{:S(2)}) collective-permute-start(bf16[32,1024]{1,0:T(8,128)(2,1)S(1)} %pad_maximum_fusion.2), channel_id=1, source_target_pairs={{0,8},{4,12},{8,16},{12,20},{16,24},{20,28},{24,0},{28,4},{1,9},{5... | collective-permute-start | bytes 196616 | tf_op jit(solution)/shard_map/ppermute | solution.py:24
  7.0 3.8 %collective-permute-start.4 = (bf16[32,1024]{1,0:T(8,128)(2,1)S(1)}, bf16[32,1024]{1,0:T(8,128)(2,1)S(1)}, u32[]{:S(2)}, u32[]{:S(2)}) collective-permute-start(bf16[32,1024]{1,0:T(8,128)(2,1)S(1)} %pad_maximum_fusion.2), channel_id=1, source_target_pairs={{0,12},{4,16},{8,20},{12,24},{16,28},{20,0},{24,4},{28,8},{1,13},{... | collective-permute-start | bytes 196616 | tf_op jit(solution)/shard_map/ppermute | solution.py:24
  14.4 2.5 %collective-permute-start = (s32[]{:T(128)}, s32[]{:T(128)}, u32[]{:S(2)}, u32[]{:S(2)}) collective-permute-start(s32[]{:T(128)} %add.137), channel_id=1, source_target_pairs={{0,64},{64,0},{1,65},{65,1},{2,66},{66,2},{3,67},{67,3},{4,68},{68... | collective-permute-start | bytes 20 | tf_op jit(solution)/shard_map/ppermute | solution.py:30
  18.0 3.5 %gather_fusion.1 = bf16[64,1024]{1,0:T(8,128)(2,1)S(1)} fusion(bf16[2048,1024]{1,0:T(8,128)(2,1)} %param.11, s32[1024]{0:T(1024)S(1)} %pad_clamp_fusion.1), kind=kCustom, calls=%fused_computation.1 | custom fusion | bytes 262400 | tf_op jit(solution)/shard_map/jit(_take)/gather | solution.py:81
  21.7 1.0 copy.63
  23.3 2.1 %collective-permute-start.1 = (s32[]{:T(128)}, s32[]{:T(128)}, u32[]{:S(2)}, u32[]{:S(2)}) collective-permute-start(s32[]{:T(128)} %max.6), channel_id=1, source_target_pairs={{0,128},{128,0},{1,129},{129,1},{2,130},{130,2},{3,131},{131,3},{4... | collective-permute-start | bytes 20 | tf_op jit(solution)/shard_map/ppermute | solution.py:30
  25.9 4.7 %collective-permute-start.6 = (bf16[32,1024]{1,0:T(8,128)(2,1)S(1)}, bf16[32,1024]{1,0:T(8,128)(2,1)S(1)}, u32[]{:S(2)}, u32[]{:S(2)}) collective-permute-start(bf16[32,1024]{1,0:T(8,128)(2,1)S(1)} %pad_maximum_fusion.2), channel_id=1, source_target_pairs={{0,20},{4,24},{8,28},{12,0},{16,4},{20,8},{24,12},{28,16},{1,21},{... | collective-permute-start | bytes 196616 | tf_op jit(solution)/shard_map/ppermute | solution.py:24
  31.2 2.5 %collective-permute-start.7 = (bf16[32,1024]{1,0:T(8,128)(2,1)S(1)}, bf16[32,1024]{1,0:T(8,128)(2,1)S(1)}, u32[]{:S(2)}, u32[]{:S(2)}) collective-permute-start(bf16[32,1024]{1,0:T(8,128)(2,1)S(1)} %pad_maximum_fusion.2), channel_id=1, source_target_pairs={{0,24},{4,28},{8,0},{12,4},{16,8},{20,12},{24,16},{28,20},{1,25},{... | collective-permute-start | bytes 196616 | tf_op jit(solution)/shard_map/ppermute | solution.py:24
  33.6 0.8 collective-permute-start.8
  34.5 8.5 %all-to-all-start.1 = ((bf16[64,2,1024]{2,1,0:T(2,128)(2,1)}), bf16[64,2,1024]{2,1,0:T(2,128)(2,1)S(1)}, u32[]{:S(2)}, u32[]{:S(2)}) async-start(bf16[64,2,1024]{2,1,0:T(2,128)(2,1)} %copy.63), calls=%async_computation.1 | async-start | bytes 524288 | tf_op jit(solution)/shard_map/all_to_all | solution.py:14
  43.1 12.1 %all-to-all-done.1 = bf16[64,2,1024]{2,1,0:T(2,128)(2,1)S(1)} async-done(((bf16[64,2,1024]{2,1,0:T(2,128)(2,1)}), bf16[64,2,1024]{2,1,0:T(2,128)(2,1)S(1)}, u32[]{:S(2)}, u32[]{:S(2)}) %all-to-all-start.1) | async-done | bytes 262176 | tf_op jit(solution)/shard_map/all_to_all | solution.py:14
  56.2 0.9 broadcast_in_dim.118
  57.0 7.4 %all-to-all-start.2 = ((bf16[32,8,1024]{2,1,0:T(8,128)(2,1)}), bf16[32,8,1024]{2,1,0:T(8,128)(2,1)S(1)}, u32[]{:S(2)}, u32[]{:S(2)}) async-start(bf16[32,8,1024]{2,1,0:T(8,128)(2,1)} %broadcast_in_dim.118), calls=%async_computation.2 | async-start | bytes 1048576 | tf_op jit(solution)/shard_map/all_to_all | solution.py:14
  64.5 11.1 %all-to-all-done.2 = bf16[32,8,1024]{2,1,0:T(8,128)(2,1)S(1)} async-done(((bf16[32,8,1024]{2,1,0:T(8,128)(2,1)}), bf16[32,8,1024]{2,1,0:T(8,128)(2,1)S(1)}, u32[]{:S(2)}, u32[]{:S(2)}) %all-to-all-start.2) | async-done | bytes 524320 | tf_op jit(solution)/shard_map/all_to_all | solution.py:14
  75.6 1.8 %fusion.12 = bf16[32,8,1024]{2,1,0:T(8,128)(2,1)} fusion(bf16[128,1024]{1,0:T(8,128)(2,1)S(1)} %get-tuple-element.196, bf16[128,1024]{1,0:T(8,128)(2,1)S(1)} %get-tuple-element.195, bf16[32,8,1024]{2,1,0:T(8,128)(2,1)S(1)} %all-to-all-done.2), kind=kOutput, calls=%fused_computation.20 | convolution fusion | flops 136609792 | bytes 1572864 | tf_op jit(solution)/shard_map/dot_general | solution.py:116
  77.3 4.9 %all-to-all-start.3 = ((bf16[32,8,1024]{2,1,0:T(8,128)(2,1)}), bf16[32,8,1024]{2,1,0:T(8,128)(2,1)S(1)}, u32[]{:S(2)}, u32[]{:S(2)}) async-start(bf16[32,8,1024]{2,1,0:T(8,128)(2,1)} %fusion.12), calls=%async_computation.3 | async-start | bytes 1048576 | tf_op jit(solution)/shard_map/all_to_all | solution.py:14
  82.6 10.8 %all-to-all-done.3 = bf16[32,8,1024]{2,1,0:T(8,128)(2,1)S(1)} async-done(((bf16[32,8,1024]{2,1,0:T(8,128)(2,1)}), bf16[32,8,1024]{2,1,0:T(8,128)(2,1)S(1)}, u32[]{:S(2)}, u32[]{:S(2)}) %all-to-all-start.3) | async-done | bytes 524320 | tf_op jit(solution)/shard_map/all_to_all | solution.py:14
  95.0 5.5 %all-to-all-start.4 = ((f32[64,1,256]{2,1,0:T(1,128)}), f32[64,1,256]{2,1,0:T(1,128)S(1)}, u32[]{:S(2)}, u32[]{:S(2)}) async-start(f32[64,1,256]{2,1,0:T(1,128)} %copy.68), calls=%async_computation.4 | async-start | bytes 131072 | tf_op jit(solution)/shard_map/all_to_all | solution.py:14
  100.7 11.0 %all-to-all-done.4 = f32[64,1,256]{2,1,0:T(1,128)S(1)} async-done(((f32[64,1,256]{2,1,0:T(1,128)}), f32[64,1,256]{2,1,0:T(1,128)S(1)}, u32[]{:S(2)}, u32[]{:S(2)}) %all-to-all-start.4) | async-done | bytes 65568 | tf_op jit(solution)/shard_map/all_to_all | solution.py:14
  113.4 1.7 %collective-permute-start.9 = (f32[16]{0:T(128)S(1)}, f32[16]{0:T(128)S(1)}, u32[]{:S(2)}, u32[]{:S(2)}) collective-permute-start(f32[16]{0:T(128)S(1)} %multiply_reduce_fusion.3), channel_id=1, source_target_pairs={{0,64},{64,0},{1,65},{65,1},{2,66},{66,2},{3,67},{67,3},{4,68},{68... | collective-permute-start | bytes 200 | tf_op jit(solution)/shard_map/ppermute | solution.py:30
  115.1 0.8 collective-permute-done.9
  115.9 1.2 collective-permute-start.10
  (84 shorter events, 11.3 us)
Async XLA Ops:
  1.4 29.7 %collective-permute-start.2 = (bf16[32,1024]{1,0:T(8,128)(2,1)S(1)}, bf16[32,1024]{1,0:T(8,128)(2,1)S(1)}, u32[]{:S(2)}, u32[]{:S(2)}) collective-permute-start(bf16[32,1024]{1,0:T(8,128)(2,1)S(1)} %pad_maximum_fusion.2), channel_id=1, source_target_pairs={{0,4},{4,8},{8,12},{12,16},{16,20},{20,24},{24,28},{28,0},{1,5},{5... | collective-permute-start | bytes 196616 | tf_op jit(solution)/shard_map/ppermute | solution.py:24
  4.0 29.7 %collective-permute-start.3 = (bf16[32,1024]{1,0:T(8,128)(2,1)S(1)}, bf16[32,1024]{1,0:T(8,128)(2,1)S(1)}, u32[]{:S(2)}, u32[]{:S(2)}) collective-permute-start(bf16[32,1024]{1,0:T(8,128)(2,1)S(1)} %pad_maximum_fusion.2), channel_id=1, source_target_pairs={{0,8},{4,12},{8,16},{12,20},{16,24},{20,28},{24,0},{28,4},{1,9},{5... | collective-permute-start | bytes 196616 | tf_op jit(solution)/shard_map/ppermute | solution.py:24
  7.0 36.0 %collective-permute-start.4 = (bf16[32,1024]{1,0:T(8,128)(2,1)S(1)}, bf16[32,1024]{1,0:T(8,128)(2,1)S(1)}, u32[]{:S(2)}, u32[]{:S(2)}) collective-permute-start(bf16[32,1024]{1,0:T(8,128)(2,1)S(1)} %pad_maximum_fusion.2), channel_id=1, source_target_pairs={{0,12},{4,16},{8,20},{12,24},{16,28},{20,0},{24,4},{28,8},{1,13},{... | collective-permute-start | bytes 196616 | tf_op jit(solution)/shard_map/ppermute | solution.py:24
  10.7 32.3 %collective-permute-start.5 = (bf16[32,1024]{1,0:T(8,128)(2,1)S(1)}, bf16[32,1024]{1,0:T(8,128)(2,1)S(1)}, u32[]{:S(2)}, u32[]{:S(2)}) collective-permute-start(bf16[32,1024]{1,0:T(8,128)(2,1)S(1)} %pad_maximum_fusion.2), channel_id=1, source_target_pairs={{0,16},{4,20},{8,24},{12,28},{16,0},{20,4},{24,8},{28,12},{1,17},{... | collective-permute-start | bytes 196616 | tf_op jit(solution)/shard_map/ppermute | solution.py:24
  14.4 8.3 %collective-permute-start = (s32[]{:T(128)}, s32[]{:T(128)}, u32[]{:S(2)}, u32[]{:S(2)}) collective-permute-start(s32[]{:T(128)} %add.137), channel_id=1, source_target_pairs={{0,64},{64,0},{1,65},{65,1},{2,66},{66,2},{3,67},{67,3},{4,68},{68... | collective-permute-start | bytes 20 | tf_op jit(solution)/shard_map/ppermute | solution.py:30
  23.3 2.6 %collective-permute-start.1 = (s32[]{:T(128)}, s32[]{:T(128)}, u32[]{:S(2)}, u32[]{:S(2)}) collective-permute-start(s32[]{:T(128)} %max.6), channel_id=1, source_target_pairs={{0,128},{128,0},{1,129},{129,1},{2,130},{130,2},{3,131},{131,3},{4... | collective-permute-start | bytes 20 | tf_op jit(solution)/shard_map/ppermute | solution.py:30
  25.9 38.5 %collective-permute-start.6 = (bf16[32,1024]{1,0:T(8,128)(2,1)S(1)}, bf16[32,1024]{1,0:T(8,128)(2,1)S(1)}, u32[]{:S(2)}, u32[]{:S(2)}) collective-permute-start(bf16[32,1024]{1,0:T(8,128)(2,1)S(1)} %pad_maximum_fusion.2), channel_id=1, source_target_pairs={{0,20},{4,24},{8,28},{12,0},{16,4},{20,8},{24,12},{28,16},{1,21},{... | collective-permute-start | bytes 196616 | tf_op jit(solution)/shard_map/ppermute | solution.py:24
  31.2 33.3 %collective-permute-start.7 = (bf16[32,1024]{1,0:T(8,128)(2,1)S(1)}, bf16[32,1024]{1,0:T(8,128)(2,1)S(1)}, u32[]{:S(2)}, u32[]{:S(2)}) collective-permute-start(bf16[32,1024]{1,0:T(8,128)(2,1)S(1)} %pad_maximum_fusion.2), channel_id=1, source_target_pairs={{0,24},{4,28},{8,0},{12,4},{16,8},{20,12},{24,16},{28,20},{1,25},{... | collective-permute-start | bytes 196616 | tf_op jit(solution)/shard_map/ppermute | solution.py:24
  33.6 30.8 %collective-permute-start.8 = (bf16[32,1024]{1,0:T(8,128)(2,1)S(1)}, bf16[32,1024]{1,0:T(8,128)(2,1)S(1)}, u32[]{:S(2)}, u32[]{:S(2)}) collective-permute-start(bf16[32,1024]{1,0:T(8,128)(2,1)S(1)} %pad_maximum_fusion.2), channel_id=1, source_target_pairs={{0,28},{4,0},{8,4},{12,8},{16,12},{20,16},{24,20},{28,24},{1,29},{... | collective-permute-start | bytes 196616 | tf_op jit(solution)/shard_map/ppermute | solution.py:24
  34.5 20.8 %all-to-all-start.1 = ((bf16[64,2,1024]{2,1,0:T(2,128)(2,1)}), bf16[64,2,1024]{2,1,0:T(2,128)(2,1)S(1)}, u32[]{:S(2)}, u32[]{:S(2)}) async-start(bf16[64,2,1024]{2,1,0:T(2,128)(2,1)} %copy.63), calls=%async_computation.1 | async-start | bytes 524288 | tf_op jit(solution)/shard_map/all_to_all | solution.py:14
  55.4 0.7 copy-start
  57.0 54.8 %copy-start.1 = (f32[16]{0:T(128)S(1)}, f32[16]{0:T(128)}, u32[]{:S(2)}) copy-start(f32[16]{0:T(128)} %param.18) | copy-start | bytes 196
  57.0 18.5 %all-to-all-start.2 = ((bf16[32,8,1024]{2,1,0:T(8,128)(2,1)}), bf16[32,8,1024]{2,1,0:T(8,128)(2,1)S(1)}, u32[]{:S(2)}, u32[]{:S(2)}) async-start(bf16[32,8,1024]{2,1,0:T(8,128)(2,1)} %broadcast_in_dim.118), calls=%async_computation.2 | async-start | bytes 1048576 | tf_op jit(solution)/shard_map/all_to_all | solution.py:14
  64.4 48.4 %copy-start.2 = (s32[8]{0:T(128)S(1)}, s32[8]{0:T(128)}, u32[]{:S(2)}) copy-start(s32[8]{0:T(128)} %param.14) | copy-start | bytes 100
  77.3 16.1 %all-to-all-start.3 = ((bf16[32,8,1024]{2,1,0:T(8,128)(2,1)}), bf16[32,8,1024]{2,1,0:T(8,128)(2,1)S(1)}, u32[]{:S(2)}, u32[]{:S(2)}) async-start(bf16[32,8,1024]{2,1,0:T(8,128)(2,1)} %fusion.12), calls=%async_computation.3 | async-start | bytes 1048576 | tf_op jit(solution)/shard_map/all_to_all | solution.py:14
  95.0 16.7 %all-to-all-start.4 = ((f32[64,1,256]{2,1,0:T(1,128)}), f32[64,1,256]{2,1,0:T(1,128)S(1)}, u32[]{:S(2)}, u32[]{:S(2)}) async-start(f32[64,1,256]{2,1,0:T(1,128)} %copy.68), calls=%async_computation.4 | async-start | bytes 131072 | tf_op jit(solution)/shard_map/all_to_all | solution.py:14
  113.4 2.5 %collective-permute-start.9 = (f32[16]{0:T(128)S(1)}, f32[16]{0:T(128)S(1)}, u32[]{:S(2)}, u32[]{:S(2)}) collective-permute-start(f32[16]{0:T(128)S(1)} %multiply_reduce_fusion.3), channel_id=1, source_target_pairs={{0,64},{64,0},{1,65},{65,1},{2,66},{66,2},{3,67},{67,3},{4,68},{68... | collective-permute-start | bytes 200 | tf_op jit(solution)/shard_map/ppermute | solution.py:30
  115.9 2.4 %collective-permute-start.10 = (f32[16]{0:T(128)S(1)}, f32[16]{0:T(128)S(1)}, u32[]{:S(2)}, u32[]{:S(2)}) collective-permute-start(f32[16]{0:T(128)S(1)} %add.144), channel_id=1, source_target_pairs={{0,128},{128,0},{1,129},{129,1},{2,130},{130,2},{3,131},{131,3},{4... | collective-permute-start | bytes 200 | tf_op jit(solution)/shard_map/ppermute | solution.py:30

commit v3 on v2

--- a/solution.py
+++ b/solution.py
@@ -6,7 +6,7 @@
 
 MP = ("yh", "z", "x")
 DP = ("yl", "core")
-ACT = ("yl", "core", "yh", "x")
+ACT = ("core", "yh", "x")
 LANES = 128
 
 
@@ -16,14 +16,6 @@
 
 def to_everyone(array, axes):
     return exchange(jnp.broadcast_to(array, (lax.axis_size(axes), *array.shape)), axes)
-
-
-def shifted(array, axis):
-    peers = lax.axis_size(axis)
-    return [array] + [
-        lax.ppermute(array, axis, [(i, (i + step) % peers) for i in range(peers)])
-        for step in range(1, peers)
-    ]
 
 
 def swapped(array, axis):
@@ -92,14 +84,14 @@
     score_weight = got[:, 1, : 3 * share].astype(f32).reshape(peers, 3, share)
     score_weight = jnp.sum(score_weight, axis=1).reshape(1, width)
 
-    parts = lax.axis_size(DP)
-    part = lax.axis_index(DP)
-    units = up_weight.shape[1] // parts
-    up_part = lax.dynamic_slice_in_dim(up_weight.T, part * units, units, 0)
-    down_part = lax.dynamic_slice_in_dim(down_weight, part * units, units, 0)
-    weights = shifted(jnp.concatenate([up_part, down_part], axis=0), "z")
-    up_rows = jnp.concatenate([w[:units] for w in weights], axis=0)
-    down_rows = jnp.concatenate([w[units:] for w in weights], axis=0)
+    halves = lax.axis_size("core")
+    half = lax.axis_index("core")
+    units = up_weight.shape[1] // halves
+    up_part = lax.dynamic_slice_in_dim(up_weight.T, half * units, units, 0)
+    down_part = lax.dynamic_slice_in_dim(down_weight, half * units, units, 0)
+    weights = lax.all_gather(jnp.concatenate([up_part, down_part], axis=0), "z", axis=0)
+    up_rows = weights[:, :units].reshape(-1, width)
+    down_rows = weights[:, units:].reshape(-1, width)
 
     def another(state):
         now, embed = state

time: 119 us -> 113 us (0.950)
  starting transfers between devices: 51.5 us -> 34.2 us
  between operations: 2.84 us -> 16.2 us
  waiting for transfers between devices: 46.9 us -> 42.9 us
  local copies, waits for them, and re-layouts: 9.41 us -> 10.7 us
    ppermute x7 -> x0, starting transfers between devices: 17.7 us -> none  [shifted(): lax.ppermute(array, axis, [(i, (i + step) % peers) for i in range(peers)])]
    all_to_all x4, waiting for transfers between devices: 45 us -> 39.1 us  [exchange(): return lax.all_to_all(blocks, axes, split_axis=0, concat_axis=0, tiled=True)]
    ppermute x4, waiting for transfers between devices: 1.9 us -> 3.79 us  [swapped(): return lax.ppermute(array, axis, [(0, 1), (1, 0)])]
    slice x0 -> x1, local copies, waits for them, and re-layouts: none -> 1.3 us  [on_device(): up_rows = weights[:, :units].reshape(-1, width)]
  transfers between devices with their start and end apart: 15 -> 9, of which waited for: 7 -> 7; matrix products, arithmetic and copies ran while one was open for 9% -> 10% of each run, Pallas kernels for 0% -> 0%
where the time goes in v3:
time: 113 us; the launch traced here: 112 us
  waiting for transfers between devices  42.9 us (38%)
  starting transfers between devices  34.2 us (30%)
  between operations  16.2 us (14%)
  local copies, waits for them, and re-layouts  10.7 us (9%)
  other arithmetic  6.54 us (6%)
  matrix products  2.02 us (2%)
    all_to_all x4, waiting for transfers between devices, exchange(): return lax.all_to_all(blocks, axes, split_axis=0, concat_axis=0, tiled=True)  39.1 us
    all_to_all x4, starting transfers between devices, exchange(): return lax.all_to_all(blocks, axes, split_axis=0, concat_axis=0, tiled=True)  26.5 us
    ppermute x4, starting transfers between devices, swapped(): return lax.ppermute(array, axis, [(0, 1), (1, 0)])  7.66 us
    ppermute x4, waiting for transfers between devices, swapped(): return lax.ppermute(array, axis, [(0, 1), (1, 0)])  3.79 us
    gather x1, local copies, waits for them, and re-layouts, rows_of(): return jnp.take(table, local, axis=0, mode='clip').reshape(peers, 1, width)  3.52 us
  transfers between devices with their start and end apart: 9, of which 7 were waited for; matrix products, arithmetic and copies ran while one was open for 10% of the time, Pallas kernels for 0%

profile of v3, /device:TPU:1, one launch (start us, length us, event | category | flops | bytes accessed | tf_op | source)
XLA Modules:
  0.0 112.5 jit_solution(4368117261645768043)
XLA Ops:
  7.2 0.8 copy.62
  8.0 0.8 pad_add_fusion
  10.4 4.3 %collective-permute-start = (s32[]{:T(128)}, s32[]{:T(128)}, u32[]{:S(2)}, u32[]{:S(2)}) collective-permute-start(s32[]{:T(128)} %add.134), channel_id=1, source_target_pairs={{0,64},{64,0},{1,65},{65,1},{2,66},{66,2},{3,67},{67,3},{4,68},{68... | collective-permute-start | bytes 20 | tf_op jit(solution)/shard_map/ppermute | solution.py:22
  14.7 0.8 constant_dynamic-slice_fusion
  16.5 0.7 reduce-precision_convert_fusion.1
  17.2 3.5 %gather_fusion.1 = bf16[64,1024]{1,0:T(8,128)(2,1)S(1)} fusion(bf16[2048,1024]{1,0:T(8,128)(2,1)} %param.11, s32[1024]{0:T(1024)S(1)} %pad_clamp_fusion.1), kind=kCustom, calls=%fused_computation.1 | custom fusion | bytes 262400 | tf_op jit(solution)/shard_map/jit(_take)/gather | solution.py:73
  20.8 1.0 copy.63
  21.8 12.6 %all-to-all-start.1 = ((bf16[64,2,1024]{2,1,0:T(2,128)(2,1)}), bf16[64,2,1024]{2,1,0:T(2,128)(2,1)S(1)}, u32[]{:S(2)}, u32[]{:S(2)}) async-start(bf16[64,2,1024]{2,1,0:T(2,128)(2,1)} %copy.63), calls=%async_computation.1 | async-start | bytes 524288 | tf_op jit(solution)/shard_map/all_to_all | solution.py:14
  35.2 1.2 %collective-permute-start.1 = (s32[]{:T(128)}, s32[]{:T(128)}, u32[]{:S(2)}, u32[]{:S(2)}) collective-permute-start(s32[]{:T(128)} %max.6), channel_id=1, source_target_pairs={{0,128},{128,0},{1,129},{129,1},{2,130},{130,2},{3,131},{131,3},{4... | collective-permute-start | bytes 20 | tf_op jit(solution)/shard_map/ppermute | solution.py:22
  36.4 1.6 %collective-permute-done.1 = s32[]{:T(128)} collective-permute-done((s32[]{:T(128)}, s32[]{:T(128)}, u32[]{:S(2)}, u32[]{:S(2)}) %collective-permute-start.1) | collective-permute-done | bytes 36 | tf_op jit(solution)/shard_map/ppermute | solution.py:22
  38.7 11.3 %all-to-all-done.1 = bf16[64,2,1024]{2,1,0:T(2,128)(2,1)S(1)} async-done(((bf16[64,2,1024]{2,1,0:T(2,128)(2,1)}), bf16[64,2,1024]{2,1,0:T(2,128)(2,1)S(1)}, u32[]{:S(2)}, u32[]{:S(2)}) %all-to-all-start.1) | async-done | bytes 262176 | tf_op jit(solution)/shard_map/all_to_all | solution.py:14
  50.9 0.7 broadcast_in_dim.118
  51.6 5.7 %all-to-all-start.2 = ((bf16[16,8,1024]{2,1,0:T(8,128)(2,1)}), bf16[16,8,1024]{2,1,0:T(8,128)(2,1)S(1)}, u32[]{:S(2)}, u32[]{:S(2)}) async-start(bf16[16,8,1024]{2,1,0:T(8,128)(2,1)} %broadcast_in_dim.118), calls=%async_computation.2 | async-start | bytes 524288 | tf_op jit(solution)/shard_map/all_to_all | solution.py:14
  57.4 1.3 %fusion.120 = (bf16[8,32,1024]{2,1,0:T(8,128)(2,1)S(1)}, bf16[8,32,1024]{2,1,0:T(8,128)(2,1)S(1)}) fusion(bf16[8,64,1024]{2,1,0:T(8,128)(2,1)} %bitcast.55), kind=kLoop, calls=%fused_computation.202 | loop fusion | bytes 2097152 | tf_op jit(solution)/shard_map/slice | solution.py:93
  58.7 7.9 %all-to-all-done.2 = bf16[16,8,1024]{2,1,0:T(8,128)(2,1)S(1)} async-done(((bf16[16,8,1024]{2,1,0:T(8,128)(2,1)}), bf16[16,8,1024]{2,1,0:T(8,128)(2,1)S(1)}, u32[]{:S(2)}, u32[]{:S(2)}) %all-to-all-start.2) | async-done | bytes 262176 | tf_op jit(solution)/shard_map/all_to_all | solution.py:14
  66.6 1.5 %fusion.12 = bf16[16,8,1024]{2,1,0:T(8,128)(2,1)} fusion(bf16[256,1024]{1,0:T(8,128)(2,1)S(1)} %bitcast.58, bf16[256,1024]{1,0:T(8,128)(2,1)S(1)} %bitcast.57, bf16[16,8,1024]{2,1,0:T(8,128)(2,1)S(1)} %all-to-all-done.2), kind=kOutput, calls=%fused_computation.20 | convolution fusion | flops 136478720 | bytes 1572864 | tf_op jit(solution)/shard_map/dot_general | solution.py:108
  68.2 3.6 %all-to-all-start.3 = ((bf16[16,8,1024]{2,1,0:T(8,128)(2,1)}), bf16[16,8,1024]{2,1,0:T(8,128)(2,1)S(1)}, u32[]{:S(2)}, u32[]{:S(2)}) async-start(bf16[16,8,1024]{2,1,0:T(8,128)(2,1)} %fusion.12), calls=%async_computation.3 | async-start | bytes 524288 | tf_op jit(solution)/shard_map/all_to_all | solution.py:14
  72.1 8.9 %all-to-all-done.3 = bf16[16,8,1024]{2,1,0:T(8,128)(2,1)S(1)} async-done(((bf16[16,8,1024]{2,1,0:T(8,128)(2,1)}), bf16[16,8,1024]{2,1,0:T(8,128)(2,1)S(1)}, u32[]{:S(2)}, u32[]{:S(2)}) %all-to-all-start.3) | async-done | bytes 262176 | tf_op jit(solution)/shard_map/all_to_all | solution.py:14
  81.9 0.7 copy.68
  82.6 4.6 %all-to-all-start.4 = ((f32[64,1,256]{2,1,0:T(1,128)}), f32[64,1,256]{2,1,0:T(1,128)S(1)}, u32[]{:S(2)}, u32[]{:S(2)}) async-start(f32[64,1,256]{2,1,0:T(1,128)} %copy.68), calls=%async_computation.4 | async-start | bytes 131072 | tf_op jit(solution)/shard_map/all_to_all | solution.py:14
  87.4 10.9 %all-to-all-done.4 = f32[64,1,256]{2,1,0:T(1,128)S(1)} async-done(((f32[64,1,256]{2,1,0:T(1,128)}), f32[64,1,256]{2,1,0:T(1,128)S(1)}, u32[]{:S(2)}, u32[]{:S(2)}) %all-to-all-start.4) | async-done | bytes 65568 | tf_op jit(solution)/shard_map/all_to_all | solution.py:14
  100.1 1.8 %collective-permute-start.2 = (f32[16]{0:T(128)S(1)}, f32[16]{0:T(128)S(1)}, u32[]{:S(2)}, u32[]{:S(2)}) collective-permute-start(f32[16]{0:T(128)S(1)} %multiply_reduce_fusion.3), channel_id=1, source_target_pairs={{0,64},{64,0},{1,65},{65,1},{2,66},{66,2},{3,67},{67,3},{4,68},{68... | collective-permute-start | bytes 200 | tf_op jit(solution)/shard_map/ppermute | solution.py:22
  101.9 0.8 collective-permute-done.2
  103.7 1.4 %collective-permute-done.3 = f32[16]{0:T(128)S(1)} collective-permute-done((f32[16]{0:T(128)S(1)}, f32[16]{0:T(128)S(1)}, u32[]{:S(2)}, u32[]{:S(2)}) %collective-permute-start.3) | collective-permute-done | bytes 96 | tf_op jit(solution)/shard_map/ppermute | solution.py:22
  (70 shorter events, 7.8 us)
Async XLA Ops:
  7.2 7.6 %copy-start = (bf16[1024,64]{0,1:T(8,128)(2,1)S(1)}, bf16[1024,64]{0,1:T(8,128)(2,1)}, u32[]{:S(2)}) copy-start(bf16[1024,64]{0,1:T(8,128)(2,1)} %param.16) | copy-start | bytes 393220
  7.2 50.2 %all-gather.3.cloned.1.call-start = ((), (), s32[]{:S(2)}) async-start(), calls=%async_computation.5 | async-start | bytes 1179648 | tf_op jit(solution)/shard_map/all_gather | solution.py:92
  10.4 24.2 %collective-permute-start = (s32[]{:T(128)}, s32[]{:T(128)}, u32[]{:S(2)}, u32[]{:S(2)}) collective-permute-start(s32[]{:T(128)} %add.134), channel_id=1, source_target_pairs={{0,64},{64,0},{1,65},{65,1},{2,66},{66,2},{3,67},{67,3},{4,68},{68... | collective-permute-start | bytes 20 | tf_op jit(solution)/shard_map/ppermute | solution.py:22
  21.8 28.1 %all-to-all-start.1 = ((bf16[64,2,1024]{2,1,0:T(2,128)(2,1)}), bf16[64,2,1024]{2,1,0:T(2,128)(2,1)S(1)}, u32[]{:S(2)}, u32[]{:S(2)}) async-start(bf16[64,2,1024]{2,1,0:T(2,128)(2,1)} %copy.63), calls=%async_computation.1 | async-start | bytes 524288 | tf_op jit(solution)/shard_map/all_to_all | solution.py:14
  35.2 2.8 %collective-permute-start.1 = (s32[]{:T(128)}, s32[]{:T(128)}, u32[]{:S(2)}, u32[]{:S(2)}) collective-permute-start(s32[]{:T(128)} %max.6), channel_id=1, source_target_pairs={{0,128},{128,0},{1,129},{129,1},{2,130},{130,2},{3,131},{131,3},{4... | collective-permute-start | bytes 20 | tf_op jit(solution)/shard_map/ppermute | solution.py:22
  50.1 0.7 copy-start.1
  51.6 15.0 %all-to-all-start.2 = ((bf16[16,8,1024]{2,1,0:T(8,128)(2,1)}), bf16[16,8,1024]{2,1,0:T(8,128)(2,1)S(1)}, u32[]{:S(2)}, u32[]{:S(2)}) async-start(bf16[16,8,1024]{2,1,0:T(8,128)(2,1)} %broadcast_in_dim.118), calls=%async_computation.2 | async-start | bytes 524288 | tf_op jit(solution)/shard_map/all_to_all | solution.py:14
  57.4 41.3 %copy-start.2 = (f32[16]{0:T(128)S(1)}, f32[16]{0:T(128)}, u32[]{:S(2)}) copy-start(f32[16]{0:T(128)} %param.18) | copy-start | bytes 196
  58.7 40.8 %copy-start.3 = (s32[8]{0:T(128)S(1)}, s32[8]{0:T(128)}, u32[]{:S(2)}) copy-start(s32[8]{0:T(128)} %param.14) | copy-start | bytes 100
  68.2 12.9 %all-to-all-start.3 = ((bf16[16,8,1024]{2,1,0:T(8,128)(2,1)}), bf16[16,8,1024]{2,1,0:T(8,128)(2,1)S(1)}, u32[]{:S(2)}, u32[]{:S(2)}) async-start(bf16[16,8,1024]{2,1,0:T(8,128)(2,1)} %fusion.12), calls=%async_computation.3 | async-start | bytes 524288 | tf_op jit(solution)/shard_map/all_to_all | solution.py:14
  82.6 15.7 %all-to-all-start.4 = ((f32[64,1,256]{2,1,0:T(1,128)}), f32[64,1,256]{2,1,0:T(1,128)S(1)}, u32[]{:S(2)}, u32[]{:S(2)}) async-start(f32[64,1,256]{2,1,0:T(1,128)} %copy.68), calls=%async_computation.4 | async-start | bytes 131072 | tf_op jit(solution)/shard_map/all_to_all | solution.py:14
  100.1 2.6 %collective-permute-start.2 = (f32[16]{0:T(128)S(1)}, f32[16]{0:T(128)S(1)}, u32[]{:S(2)}, u32[]{:S(2)}) collective-permute-start(f32[16]{0:T(128)S(1)} %multiply_reduce_fusion.3), channel_id=1, source_target_pairs={{0,64},{64,0},{1,65},{65,1},{2,66},{66,2},{3,67},{67,3},{4,68},{68... | collective-permute-start | bytes 200 | tf_op jit(solution)/shard_map/ppermute | solution.py:22
  102.7 2.4 %collective-permute-start.3 = (f32[16]{0:T(128)S(1)}, f32[16]{0:T(128)S(1)}, u32[]{:S(2)}, u32[]{:S(2)}) collective-permute-start(f32[16]{0:T(128)S(1)} %add.140), channel_id=1, source_target_pairs={{0,128},{128,0},{1,129},{129,1},{2,130},{130,2},{3,131},{131,3},{4... | collective-permute-start | bytes 200 | tf_op jit(solution)/shard_map/ppermute | solution.py:22
Sparse Core Ops, SparseCore 0:
  16.4 38.4 all-gather.2

commit v4 on v3

--- a/solution.py
+++ b/solution.py
@@ -4,9 +4,9 @@
 from jax.sharding import Mesh
 from jax.sharding import PartitionSpec as P
 
-MP = ("yh", "z", "x")
+MP = ("yh", "zh", "zl", "x")
 DP = ("yl", "core")
-ACT = ("core", "yh", "x")
+ACT = ("yh", "zl", "x")
 LANES = 128
 
 
@@ -16,6 +16,14 @@
 
 def to_everyone(array, axes):
     return exchange(jnp.broadcast_to(array, (lax.axis_size(axes), *array.shape)), axes)
+
+
+def from_column(array):
+    steps, places = lax.axis_size("zh"), lax.axis_size(DP)
+    moves = [
+        (d * steps + (i + d) % steps, d * steps + i) for d in range(places) for i in range(steps)
+    ]
+    return lax.ppermute(array, (*DP, "zh"), moves)
 
 
 def swapped(array, axis):
@@ -76,6 +84,9 @@
         picks = (from_peer & (sent_in == now)).astype(bf16)
         return jnp.dot(picks, rows, preferred_element_type=f32)
 
+    units = up_weight.shape[1]
+    weights = from_column(jnp.concatenate([up_weight.T, down_weight], axis=0))
+
     score_weight = jnp.concatenate(thirds(out_gain * class_weight)).astype(bf16)
     score_weight = jnp.pad(score_weight, (0, width - score_weight.size))
     extra = jnp.broadcast_to(score_weight, (peers, 1, width))
@@ -84,20 +95,17 @@
     score_weight = got[:, 1, : 3 * share].astype(f32).reshape(peers, 3, share)
     score_weight = jnp.sum(score_weight, axis=1).reshape(1, width)
 
-    halves = lax.axis_size("core")
-    half = lax.axis_index("core")
-    units = up_weight.shape[1] // halves
-    up_part = lax.dynamic_slice_in_dim(up_weight.T, half * units, units, 0)
-    down_part = lax.dynamic_slice_in_dim(down_weight, half * units, units, 0)
-    weights = lax.all_gather(jnp.concatenate([up_part, down_part], axis=0), "z", axis=0)
-    up_rows = weights[:, :units].reshape(-1, width)
-    down_rows = weights[:, units:].reshape(-1, width)
-
     def another(state):
         now, embed = state
         return now + 1, embed + taken(now, exchange(rows_of(now), MP)[:, 0])
 
     _, embed = lax.while_loop(lambda state: state[0] < trips, another, (jnp.int32(1), embed))
+
+    weights = jnp.where(embed[0, 0] < jnp.inf, weights, 0)[None]
+    weights = jnp.concatenate([weights, swapped(weights, "core")], axis=0)
+    weights = jnp.concatenate([weights, swapped(weights, "yl")], axis=0)
+    up_rows = weights[:, :units].reshape(-1, width)
+    down_rows = weights[:, units:].reshape(-1, width)
 
     normed = (standardize(embed) * in_gain).astype(bf16)
     everyone = to_everyone(normed, ACT)
@@ -133,7 +141,7 @@
 
 
 def solution(mesh):
-    parts = Mesh(mesh.devices.reshape(2, 2, 2, 8, 4), ("yl", "core", "yh", "z", "x"))
+    parts = Mesh(mesh.devices.reshape(2, 2, 2, 4, 2, 4), (*DP, *MP))
     return jax.shard_map(
         on_device,
         mesh=parts,

time: 113 us -> 108 us (0.956)
  between operations: 16.2 us -> 3.42 us
  starting transfers between devices: 34.2 us -> 46.4 us
  waiting for transfers between devices: 42.9 us -> 39.9 us
  local copies, waits for them, and re-layouts: 10.7 us -> 8.55 us
    all_to_all x4, waiting for transfers between devices: 39.1 us -> 26.4 us  [exchange(): return lax.all_to_all(blocks, axes, split_axis=0, concat_axis=0, tiled=True)]
    ppermute x4 -> x6, waiting for transfers between devices: 3.79 us -> 13.5 us  [swapped(): return lax.ppermute(array, axis, [(0, 1), (1, 0)])]
    ppermute x0 -> x1, starting transfers between devices: none -> 8.76 us  [from_column(): return lax.ppermute(array, (*DP, 'zh'), moves)]
    ppermute x4 -> x6, starting transfers between devices: 7.66 us -> 14.4 us  [swapped(): return lax.ppermute(array, axis, [(0, 1), (1, 0)])]
    all_to_all x4, starting transfers between devices: 26.5 us -> 23.2 us  [exchange(): return lax.all_to_all(blocks, axes, split_axis=0, concat_axis=0, tiled=True)]
    slice x1, local copies, waits for them, and re-layouts: 1.3 us -> 0.1 us  [on_device(): up_rows = weights[:, :units].reshape(-1, width)]
  transfers between devices with their start and end apart: 9 -> 11, of which waited for: 7 -> 9; matrix products, arithmetic and copies ran while one was open for 10% -> 10% of each run, Pallas kernels for 0% -> 0%
where the time goes in v4:
time: 108 us; the launch traced here: 107 us
  starting transfers between devices  46.4 us (43%)
  waiting for transfers between devices  39.9 us (37%)
  local copies, waits for them, and re-layouts  8.55 us (8%)
  other arithmetic  7.05 us (7%)
  between operations  3.42 us (3%)
  matrix products  2.02 us (2%)
    all_to_all x4, waiting for transfers between devices, exchange(): return lax.all_to_all(blocks, axes, split_axis=0, concat_axis=0, tiled=True)  26.4 us
    all_to_all x4, starting transfers between devices, exchange(): return lax.all_to_all(blocks, axes, split_axis=0, concat_axis=0, tiled=True)  23.2 us
    ppermute x6, starting transfers between devices, swapped(): return lax.ppermute(array, axis, [(0, 1), (1, 0)])  14.4 us
    ppermute x6, waiting for transfers between devices, swapped(): return lax.ppermute(array, axis, [(0, 1), (1, 0)])  13.5 us
    ppermute x1, starting transfers between devices, from_column(): return lax.ppermute(array, (*DP, 'zh'), moves)  8.76 us
    gather x1, local copies, waits for them, and re-layouts, rows_of(): return jnp.take(table, local, axis=0, mode='clip').reshape(peers, 1, width)  3.52 us
  transfers between devices with their start and end apart: 11, of which 9 were waited for; matrix products, arithmetic and copies ran while one was open for 10% of the time, Pallas kernels for 0%

profile of v4, /device:TPU:1, one launch (start us, length us, event | category | flops | bytes accessed | tf_op | source)
XLA Modules:
  0.0 107.4 jit_solution(16831357307849569887)
XLA Ops:
  0.6 1.0 pad_maximum_fusion.3
  1.6 8.8 %collective-permute-start.2 = (bf16[128,1024]{1,0:T(8,128)(2,1)S(1)}, bf16[128,1024]{1,0:T(8,128)(2,1)S(1)}, u32[]{:S(2)}, u32[]{:S(2)}) collective-permute-start(bf16[128,1024]{1,0:T(8,128)(2,1)S(1)} %pad_maximum_fusion.3), channel_id=1, source_target_pairs={{0,0},{8,8},{16,16},{24,24},{72,64},{80,72},{88,80},{64,88},{144,1... | collective-permute-start | bytes 786440 | tf_op jit(solution)/shard_map/ppermute | solution.py:26
  10.4 0.8 copy.62
  11.1 0.8 pad_add_fusion
  13.6 0.9 collective-permute-start
  15.4 3.5 %gather_fusion.1 = bf16[64,1024]{1,0:T(8,128)(2,1)S(1)} fusion(bf16[2048,1024]{1,0:T(8,128)(2,1)} %param.11, s32[1024]{0:T(1024)S(1)} %pad_clamp_fusion.1), kind=kCustom, calls=%fused_computation.1 | custom fusion | bytes 262400 | tf_op jit(solution)/shard_map/jit(_take)/gather | solution.py:81
  19.1 1.0 copy.63
  20.0 8.5 %all-to-all-start.1 = ((bf16[64,2,1024]{2,1,0:T(2,128)(2,1)}), bf16[64,2,1024]{2,1,0:T(2,128)(2,1)S(1)}, u32[]{:S(2)}, u32[]{:S(2)}) async-start(bf16[64,2,1024]{2,1,0:T(2,128)(2,1)} %copy.63), calls=%async_computation.1 | async-start | bytes 524288 | tf_op jit(solution)/shard_map/all_to_all | solution.py:14
  29.4 3.5 %collective-permute-start.1 = (s32[]{:T(128)}, s32[]{:T(128)}, u32[]{:S(2)}, u32[]{:S(2)}) collective-permute-start(s32[]{:T(128)} %max.6), channel_id=1, source_target_pairs={{0,128},{128,0},{1,129},{129,1},{2,130},{130,2},{3,131},{131,3},{4... | collective-permute-start | bytes 20 | tf_op jit(solution)/shard_map/ppermute | solution.py:30
  34.1 6.8 %all-to-all-done.1 = bf16[64,2,1024]{2,1,0:T(2,128)(2,1)S(1)} async-done(((bf16[64,2,1024]{2,1,0:T(2,128)(2,1)}), bf16[64,2,1024]{2,1,0:T(2,128)(2,1)S(1)}, u32[]{:S(2)}, u32[]{:S(2)}) %all-to-all-start.1) | async-done | bytes 262176 | tf_op jit(solution)/shard_map/all_to_all | solution.py:14
  42.3 3.4 %collective-permute-start.3 = (bf16[1,128,1024]{2,1,0:T(8,128)(2,1)S(1)}, bf16[1,128,1024]{2,1,0:T(8,128)(2,1)S(1)}, u32[]{:S(2)}, u32[]{:S(2)}) collective-permute-start(bf16[1,128,1024]{2,1,0:T(8,128)(2,1)S(1)} %select_bitcast_fusion), channel_id=1, source_target_pairs={{0,64},{64,0},{1,65},{65,1},{2,66},{66,2},{3,67},{67,3},{4,68},{68... | collective-permute-start | bytes 786440 | tf_op jit(solution)/shard_map/ppermute | solution.py:30
  45.9 1.0 collective-permute-done.3
  47.0 2.5 %collective-permute-start.4 = (bf16[2,128,1024]{2,1,0:T(8,128)(2,1)S(1)}, bf16[2,128,1024]{2,1,0:T(8,128)(2,1)S(1)}, u32[]{:S(2)}, u32[]{:S(2)}) collective-permute-start(bf16[2,128,1024]{2,1,0:T(8,128)(2,1)S(1)} %pad_maximum_fusion.1), channel_id=1, source_target_pairs={{0,128},{128,0},{1,129},{129,1},{2,130},{130,2},{3,131},{131,3},{4... | collective-permute-start | bytes 1572872 | tf_op jit(solution)/shard_map/ppermute | solution.py:30
  49.5 0.7 broadcast_in_dim.125
  50.3 4.3 %all-to-all-start.2 = ((bf16[16,8,1024]{2,1,0:T(8,128)(2,1)}), bf16[16,8,1024]{2,1,0:T(8,128)(2,1)S(1)}, u32[]{:S(2)}, u32[]{:S(2)}) async-start(bf16[16,8,1024]{2,1,0:T(8,128)(2,1)} %broadcast_in_dim.125), calls=%async_computation.2 | async-start | bytes 524288 | tf_op jit(solution)/shard_map/all_to_all | solution.py:14
  54.5 9.4 %collective-permute-done.4 = bf16[2,128,1024]{2,1,0:T(8,128)(2,1)S(1)} collective-permute-done((bf16[2,128,1024]{2,1,0:T(8,128)(2,1)S(1)}, bf16[2,128,1024]{2,1,0:T(8,128)(2,1)S(1)}, u32[]{:S(2)}, u32[]{:S(2)}) %collective-permute-start.4) | collective-permute-done | bytes 524320 | tf_op jit(solution)/shard_map/ppermute | solution.py:30
  64.4 1.5 %fusion.12 = bf16[16,8,1024]{2,1,0:T(8,128)(2,1)} fusion(bf16[256,1024]{1,0:T(8,128)(2,1)S(1)} %bitcast.58, bf16[256,1024]{1,0:T(8,128)(2,1)S(1)} %bitcast.57, bf16[16,8,1024]{2,1,0:T(8,128)(2,1)S(1)} %all-to-all-done.2), kind=kOutput, calls=%fused_computation.20 | convolution fusion | flops 136478720 | bytes 1572864 | tf_op jit(solution)/shard_map/dot_general | solution.py:116
  65.9 5.8 %all-to-all-start.3 = ((bf16[16,8,1024]{2,1,0:T(8,128)(2,1)}), bf16[16,8,1024]{2,1,0:T(8,128)(2,1)S(1)}, u32[]{:S(2)}, u32[]{:S(2)}) async-start(bf16[16,8,1024]{2,1,0:T(8,128)(2,1)} %fusion.12), calls=%async_computation.3 | async-start | bytes 524288 | tf_op jit(solution)/shard_map/all_to_all | solution.py:14
  72.1 8.4 %all-to-all-done.3 = bf16[16,8,1024]{2,1,0:T(8,128)(2,1)S(1)} async-done(((bf16[16,8,1024]{2,1,0:T(8,128)(2,1)}), bf16[16,8,1024]{2,1,0:T(8,128)(2,1)S(1)}, u32[]{:S(2)}, u32[]{:S(2)}) %all-to-all-start.3) | async-done | bytes 262176 | tf_op jit(solution)/shard_map/all_to_all | solution.py:14
  82.1 4.6 %all-to-all-start.4 = ((f32[64,1,256]{2,1,0:T(1,128)}), f32[64,1,256]{2,1,0:T(1,128)S(1)}, u32[]{:S(2)}, u32[]{:S(2)}) async-start(f32[64,1,256]{2,1,0:T(1,128)} %copy.68), calls=%async_computation.4 | async-start | bytes 131072 | tf_op jit(solution)/shard_map/all_to_all | solution.py:14
  86.9 10.9 %all-to-all-done.4 = f32[64,1,256]{2,1,0:T(1,128)S(1)} async-done(((f32[64,1,256]{2,1,0:T(1,128)}), f32[64,1,256]{2,1,0:T(1,128)S(1)}, u32[]{:S(2)}, u32[]{:S(2)}) %all-to-all-start.4) | async-done | bytes 65568 | tf_op jit(solution)/shard_map/all_to_all | solution.py:14
  99.6 4.1 %collective-permute-start.5 = (f32[16]{0:T(128)S(1)}, f32[16]{0:T(128)S(1)}, u32[]{:S(2)}, u32[]{:S(2)}) collective-permute-start(f32[16]{0:T(128)S(1)} %multiply_reduce_fusion.3), channel_id=1, source_target_pairs={{0,64},{64,0},{1,65},{65,1},{2,66},{66,2},{3,67},{67,3},{4,68},{68... | collective-permute-start | bytes 200 | tf_op jit(solution)/shard_map/ppermute | solution.py:30
  103.6 0.8 collective-permute-done.5
  105.1 1.8 %collective-permute-done.6 = f32[16]{0:T(128)S(1)} collective-permute-done((f32[16]{0:T(128)S(1)}, f32[16]{0:T(128)S(1)}, u32[]{:S(2)}, u32[]{:S(2)}) %collective-permute-start.6) | collective-permute-done | bytes 96 | tf_op jit(solution)/shard_map/ppermute | solution.py:30
  (73 shorter events, 9.1 us)
Async XLA Ops:
  1.6 40.7 %collective-permute-start.2 = (bf16[128,1024]{1,0:T(8,128)(2,1)S(1)}, bf16[128,1024]{1,0:T(8,128)(2,1)S(1)}, u32[]{:S(2)}, u32[]{:S(2)}) collective-permute-start(bf16[128,1024]{1,0:T(8,128)(2,1)S(1)} %pad_maximum_fusion.3), channel_id=1, source_target_pairs={{0,0},{8,8},{16,16},{24,24},{72,64},{80,72},{88,80},{64,88},{144,1... | collective-permute-start | bytes 786440 | tf_op jit(solution)/shard_map/ppermute | solution.py:26
  13.6 15.2 %collective-permute-start = (s32[]{:T(128)}, s32[]{:T(128)}, u32[]{:S(2)}, u32[]{:S(2)}) collective-permute-start(s32[]{:T(128)} %add.134), channel_id=1, source_target_pairs={{0,64},{64,0},{1,65},{65,1},{2,66},{66,2},{3,67},{67,3},{4,68},{68... | collective-permute-start | bytes 20 | tf_op jit(solution)/shard_map/ppermute | solution.py:30
  20.0 20.9 %all-to-all-start.1 = ((bf16[64,2,1024]{2,1,0:T(2,128)(2,1)}), bf16[64,2,1024]{2,1,0:T(2,128)(2,1)S(1)}, u32[]{:S(2)}, u32[]{:S(2)}) async-start(bf16[64,2,1024]{2,1,0:T(2,128)(2,1)} %copy.63), calls=%async_computation.1 | async-start | bytes 524288 | tf_op jit(solution)/shard_map/all_to_all | solution.py:14
  29.4 4.0 %collective-permute-start.1 = (s32[]{:T(128)}, s32[]{:T(128)}, u32[]{:S(2)}, u32[]{:S(2)}) collective-permute-start(s32[]{:T(128)} %max.6), channel_id=1, source_target_pairs={{0,128},{128,0},{1,129},{129,1},{2,130},{130,2},{3,131},{131,3},{4... | collective-permute-start | bytes 20 | tf_op jit(solution)/shard_map/ppermute | solution.py:30
  41.1 8.3 %copy-start = (f32[1024]{0:T(1024)S(1)}, f32[1024]{0:T(1024)}, u32[]{:S(2)}) copy-start(f32[1024]{0:T(1024)} %param.15) | copy-start | bytes 12292
  42.3 4.6 %collective-permute-start.3 = (bf16[1,128,1024]{2,1,0:T(8,128)(2,1)S(1)}, bf16[1,128,1024]{2,1,0:T(8,128)(2,1)S(1)}, u32[]{:S(2)}, u32[]{:S(2)}) collective-permute-start(bf16[1,128,1024]{2,1,0:T(8,128)(2,1)S(1)} %select_bitcast_fusion), channel_id=1, source_target_pairs={{0,64},{64,0},{1,65},{65,1},{2,66},{66,2},{3,67},{67,3},{4,68},{68... | collective-permute-start | bytes 786440 | tf_op jit(solution)/shard_map/ppermute | solution.py:30
  47.0 16.9 %collective-permute-start.4 = (bf16[2,128,1024]{2,1,0:T(8,128)(2,1)S(1)}, bf16[2,128,1024]{2,1,0:T(8,128)(2,1)S(1)}, u32[]{:S(2)}, u32[]{:S(2)}) collective-permute-start(bf16[2,128,1024]{2,1,0:T(8,128)(2,1)S(1)} %pad_maximum_fusion.1), channel_id=1, source_target_pairs={{0,128},{128,0},{1,129},{129,1},{2,130},{130,2},{3,131},{131,3},{4... | collective-permute-start | bytes 1572872 | tf_op jit(solution)/shard_map/ppermute | solution.py:30
  50.3 14.1 %all-to-all-start.2 = ((bf16[16,8,1024]{2,1,0:T(8,128)(2,1)}), bf16[16,8,1024]{2,1,0:T(8,128)(2,1)S(1)}, u32[]{:S(2)}, u32[]{:S(2)}) async-start(bf16[16,8,1024]{2,1,0:T(8,128)(2,1)} %broadcast_in_dim.125), calls=%async_computation.2 | async-start | bytes 524288 | tf_op jit(solution)/shard_map/all_to_all | solution.py:14
  64.0 34.0 %copy-start.1 = (f32[16]{0:T(128)S(1)}, f32[16]{0:T(128)}, u32[]{:S(2)}) copy-start(f32[16]{0:T(128)} %param.18) | copy-start | bytes 196
  64.1 34.8 %copy-start.2 = (s32[8]{0:T(128)S(1)}, s32[8]{0:T(128)}, u32[]{:S(2)}) copy-start(s32[8]{0:T(128)} %param.14) | copy-start | bytes 100
  65.9 14.6 %all-to-all-start.3 = ((bf16[16,8,1024]{2,1,0:T(8,128)(2,1)}), bf16[16,8,1024]{2,1,0:T(8,128)(2,1)S(1)}, u32[]{:S(2)}, u32[]{:S(2)}) async-start(bf16[16,8,1024]{2,1,0:T(8,128)(2,1)} %fusion.12), calls=%async_computation.3 | async-start | bytes 524288 | tf_op jit(solution)/shard_map/all_to_all | solution.py:14
  82.1 15.7 %all-to-all-start.4 = ((f32[64,1,256]{2,1,0:T(1,128)}), f32[64,1,256]{2,1,0:T(1,128)S(1)}, u32[]{:S(2)}, u32[]{:S(2)}) async-start(f32[64,1,256]{2,1,0:T(1,128)} %copy.68), calls=%async_computation.4 | async-start | bytes 131072 | tf_op jit(solution)/shard_map/all_to_all | solution.py:14
  99.6 4.9 %collective-permute-start.5 = (f32[16]{0:T(128)S(1)}, f32[16]{0:T(128)S(1)}, u32[]{:S(2)}, u32[]{:S(2)}) collective-permute-start(f32[16]{0:T(128)S(1)} %multiply_reduce_fusion.3), channel_id=1, source_target_pairs={{0,64},{64,0},{1,65},{65,1},{2,66},{66,2},{3,67},{67,3},{4,68},{68... | collective-permute-start | bytes 200 | tf_op jit(solution)/shard_map/ppermute | solution.py:30
  104.5 2.4 %collective-permute-start.6 = (f32[16]{0:T(128)S(1)}, f32[16]{0:T(128)S(1)}, u32[]{:S(2)}, u32[]{:S(2)}) collective-permute-start(f32[16]{0:T(128)S(1)} %add.139), channel_id=1, source_target_pairs={{0,128},{128,0},{1,129},{129,1},{2,130},{130,2},{3,131},{131,3},{4... | collective-permute-start | bytes 200 | tf_op jit(solution)/shard_map/ppermute | solution.py:30

commit v5 on v4

--- a/solution.py
+++ b/solution.py
@@ -18,12 +18,12 @@
     return exchange(jnp.broadcast_to(array, (lax.axis_size(axes), *array.shape)), axes)
 
 
-def from_column(array):
-    steps, places = lax.axis_size("zh"), lax.axis_size(DP)
-    moves = [
-        (d * steps + (i + d) % steps, d * steps + i) for d in range(places) for i in range(steps)
+def from_column(array, axis):
+    peers = lax.axis_size(axis)
+    return [array] + [
+        lax.ppermute(array, axis, [((i + step) % peers, i) for i in range(peers)])
+        for step in range(1, peers)
     ]
-    return lax.ppermute(array, (*DP, "zh"), moves)
 
 
 def swapped(array, axis):
@@ -85,7 +85,9 @@
         return jnp.dot(picks, rows, preferred_element_type=f32)
 
     units = up_weight.shape[1]
-    weights = from_column(jnp.concatenate([up_weight.T, down_weight], axis=0))
+    weights = from_column(jnp.concatenate([up_weight.T, down_weight], axis=0), "zh")
+    up_rows = jnp.concatenate([w[:units] for w in weights], axis=0)
+    down_rows = jnp.concatenate([w[units:] for w in weights], axis=0)
 
     score_weight = jnp.concatenate(thirds(out_gain * class_weight)).astype(bf16)
     score_weight = jnp.pad(score_weight, (0, width - score_weight.size))
@@ -100,12 +102,6 @@
         return now + 1, embed + taken(now, exchange(rows_of(now), MP)[:, 0])
 
     _, embed = lax.while_loop(lambda state: state[0] < trips, another, (jnp.int32(1), embed))
-
-    weights = jnp.where(embed[0, 0] < jnp.inf, weights, 0)[None]
-    weights = jnp.concatenate([weights, swapped(weights, "core")], axis=0)
-    weights = jnp.concatenate([weights, swapped(weights, "yl")], axis=0)
-    up_rows = weights[:, :units].reshape(-1, width)
-    down_rows = weights[:, units:].reshape(-1, width)
 
     normed = (standardize(embed) * in_gain).astype(bf16)
     everyone = to_everyone(normed, ACT)

time: 108 us -> 104 us (0.963)
  starting transfers between devices: 46.4 us -> 42.5 us
    all_to_all x4, waiting for transfers between devices: 26.4 us -> 36.7 us  [exchange(): return lax.all_to_all(blocks, axes, split_axis=0, concat_axis=0, tiled=True)]
    ppermute x6 -> x4, waiting for transfers between devices: 13.5 us -> 3.68 us  [swapped(): return lax.ppermute(array, axis, [(0, 1), (1, 0)])]
    ppermute x6 -> x4, starting transfers between devices: 14.4 us -> 8.49 us  [swapped(): return lax.ppermute(array, axis, [(0, 1), (1, 0)])]
    ppermute x1 -> x3, starting transfers between devices: 8.76 us -> 11.4 us  [from_column(): lax.ppermute(array, axis, [((i + step) % peers, i) for i in range(peers)])]
  transfers between devices with their start and end apart: 11 -> 11, of which waited for: 9 -> 7; matrix products, arithmetic and copies ran while one was open for 10% -> 10% of each run, Pallas kernels for 0% -> 0%
where the time goes in v5:
time: 104 us; the launch traced here: 103 us
  starting transfers between devices  42.5 us (41%)
  waiting for transfers between devices  40.4 us (39%)
  local copies, waits for them, and re-layouts  8.49 us (8%)
  other arithmetic  6.88 us (7%)
  between operations  2.77 us (3%)
  matrix products  2.02 us (2%)
    all_to_all x4, waiting for transfers between devices, exchange(): return lax.all_to_all(blocks, axes, split_axis=0, concat_axis=0, tiled=True)  36.7 us
    all_to_all x4, starting transfers between devices, exchange(): return lax.all_to_all(blocks, axes, split_axis=0, concat_axis=0, tiled=True)  22.6 us
    ppermute x3, starting transfers between devices, from_column(): lax.ppermute(array, axis, [((i + step) % peers, i) for i in range(peers)])  11.4 us
    ppermute x4, starting transfers between devices, swapped(): return lax.ppermute(array, axis, [(0, 1), (1, 0)])  8.49 us
    ppermute x4, waiting for transfers between devices, swapped(): return lax.ppermute(array, axis, [(0, 1), (1, 0)])  3.68 us
    gather x1, local copies, waits for them, and re-layouts, rows_of(): return jnp.take(table, local, axis=0, mode='clip').reshape(peers, 1, width)  3.52 us
  transfers between devices with their start and end apart: 11, of which 7 were waited for; matrix products, arithmetic and copies ran while one was open for 10% of the time, Pallas kernels for 0%

profile of v5, /device:TPU:1, one launch (start us, length us, event | category | flops | bytes accessed | tf_op | source)
XLA Modules:
  0.0 103.0 jit_solution(4209262483692586391)
XLA Ops:
  0.6 1.0 pad_maximum_fusion.1
  1.6 3.9 %collective-permute-start.4 = (bf16[128,1024]{1,0:T(8,128)(2,1)S(1)}, bf16[128,1024]{1,0:T(8,128)(2,1)S(1)}, u32[]{:S(2)}, u32[]{:S(2)}) collective-permute-start(bf16[128,1024]{1,0:T(8,128)(2,1)S(1)} %pad_maximum_fusion.1), channel_id=1, source_target_pairs={{24,0},{0,8},{8,16},{16,24},{25,1},{1,9},{9,17},{17,25},{26,2},{2,... | collective-permute-start | bytes 786440 | tf_op jit(solution)/shard_map/ppermute | solution.py:24
  5.5 5.1 %collective-permute-start.3 = (bf16[128,1024]{1,0:T(8,128)(2,1)S(1)}, bf16[128,1024]{1,0:T(8,128)(2,1)S(1)}, u32[]{:S(2)}, u32[]{:S(2)}) collective-permute-start(bf16[128,1024]{1,0:T(8,128)(2,1)S(1)} %pad_maximum_fusion.1), channel_id=1, source_target_pairs={{16,0},{24,8},{0,16},{8,24},{17,1},{25,9},{1,17},{9,25},{18,2},{26... | collective-permute-start | bytes 786440 | tf_op jit(solution)/shard_map/ppermute | solution.py:24
  10.6 2.4 %collective-permute-start.2 = (bf16[128,1024]{1,0:T(8,128)(2,1)S(1)}, bf16[128,1024]{1,0:T(8,128)(2,1)S(1)}, u32[]{:S(2)}, u32[]{:S(2)}) collective-permute-start(bf16[128,1024]{1,0:T(8,128)(2,1)S(1)} %pad_maximum_fusion.1), channel_id=1, source_target_pairs={{8,0},{16,8},{24,16},{0,24},{9,1},{17,9},{25,17},{1,25},{10,2},{18... | collective-permute-start | bytes 786440 | tf_op jit(solution)/shard_map/ppermute | solution.py:24
  13.0 0.8 copy.62
  13.8 0.8 pad_add_fusion
  16.2 2.4 %collective-permute-start = (s32[]{:T(128)}, s32[]{:T(128)}, u32[]{:S(2)}, u32[]{:S(2)}) collective-permute-start(s32[]{:T(128)} %add.134), channel_id=1, source_target_pairs={{0,64},{64,0},{1,65},{65,1},{2,66},{66,2},{3,67},{67,3},{4,68},{68... | collective-permute-start | bytes 20 | tf_op jit(solution)/shard_map/ppermute | solution.py:30
  19.6 3.5 %gather_fusion.1 = bf16[64,1024]{1,0:T(8,128)(2,1)S(1)} fusion(bf16[2048,1024]{1,0:T(8,128)(2,1)} %param.11, s32[1024]{0:T(1024)S(1)} %pad_clamp_fusion.1), kind=kCustom, calls=%fused_computation.1 | custom fusion | bytes 262400 | tf_op jit(solution)/shard_map/jit(_take)/gather | solution.py:81
  23.2 1.0 copy.63
  24.2 8.1 %all-to-all-start.1 = ((bf16[64,2,1024]{2,1,0:T(2,128)(2,1)}), bf16[64,2,1024]{2,1,0:T(2,128)(2,1)S(1)}, u32[]{:S(2)}, u32[]{:S(2)}) async-start(bf16[64,2,1024]{2,1,0:T(2,128)(2,1)} %copy.63), calls=%async_computation.1 | async-start | bytes 524288 | tf_op jit(solution)/shard_map/all_to_all | solution.py:14
  33.1 1.2 %collective-permute-start.1 = (s32[]{:T(128)}, s32[]{:T(128)}, u32[]{:S(2)}, u32[]{:S(2)}) collective-permute-start(s32[]{:T(128)} %max.6), channel_id=1, source_target_pairs={{0,128},{128,0},{1,129},{129,1},{2,130},{130,2},{3,131},{131,3},{4... | collective-permute-start | bytes 20 | tf_op jit(solution)/shard_map/ppermute | solution.py:30
  34.3 1.6 %collective-permute-done.1 = s32[]{:T(128)} collective-permute-done((s32[]{:T(128)}, s32[]{:T(128)}, u32[]{:S(2)}, u32[]{:S(2)}) %collective-permute-start.1) | collective-permute-done | bytes 36 | tf_op jit(solution)/shard_map/ppermute | solution.py:30
  36.5 8.7 %all-to-all-done.1 = bf16[64,2,1024]{2,1,0:T(2,128)(2,1)S(1)} async-done(((bf16[64,2,1024]{2,1,0:T(2,128)(2,1)}), bf16[64,2,1024]{2,1,0:T(2,128)(2,1)S(1)}, u32[]{:S(2)}, u32[]{:S(2)}) %all-to-all-start.1) | async-done | bytes 262176 | tf_op jit(solution)/shard_map/all_to_all | solution.py:14
  46.2 0.7 broadcast_in_dim.118
  46.9 5.3 %all-to-all-start.2 = ((bf16[16,8,1024]{2,1,0:T(8,128)(2,1)}), bf16[16,8,1024]{2,1,0:T(8,128)(2,1)S(1)}, u32[]{:S(2)}, u32[]{:S(2)}) async-start(bf16[16,8,1024]{2,1,0:T(8,128)(2,1)} %broadcast_in_dim.118), calls=%async_computation.2 | async-start | bytes 524288 | tf_op jit(solution)/shard_map/all_to_all | solution.py:14
  52.3 8.7 %all-to-all-done.2 = bf16[16,8,1024]{2,1,0:T(8,128)(2,1)S(1)} async-done(((bf16[16,8,1024]{2,1,0:T(8,128)(2,1)}), bf16[16,8,1024]{2,1,0:T(8,128)(2,1)S(1)}, u32[]{:S(2)}, u32[]{:S(2)}) %all-to-all-start.2) | async-done | bytes 262176 | tf_op jit(solution)/shard_map/all_to_all | solution.py:14
  61.1 1.6 %fusion.12 = bf16[16,8,1024]{2,1,0:T(8,128)(2,1)} fusion(bf16[64,1024]{1,0:T(8,128)(2,1)S(1)} %get-tuple-element.194, bf16[64,1024]{1,0:T(8,128)(2,1)S(1)} %get-tuple-element.192, bf16[64,1024]{1,0:T(8,128)(2,1)S(1)} %get-tuple-element.190, bf16[64,1024]{1,0:T(8,128)(2,1)S(1)} %copy-done, bf16[64,1024]{1,0:T(8,128)(2,1)S(1)} %get-tuple-element.193, ...), kind=kOutput, calls=%fused_computation.20 | convolution fusion | flops 140673024 | bytes 1572864 | tf_op jit(solution)/shard_map/dot_general | solution.py:112
  62.6 3.5 %all-to-all-start.3 = ((bf16[16,8,1024]{2,1,0:T(8,128)(2,1)}), bf16[16,8,1024]{2,1,0:T(8,128)(2,1)S(1)}, u32[]{:S(2)}, u32[]{:S(2)}) async-start(bf16[16,8,1024]{2,1,0:T(8,128)(2,1)} %fusion.12), calls=%async_computation.3 | async-start | bytes 524288 | tf_op jit(solution)/shard_map/all_to_all | solution.py:14
  66.5 8.4 %all-to-all-done.3 = bf16[16,8,1024]{2,1,0:T(8,128)(2,1)S(1)} async-done(((bf16[16,8,1024]{2,1,0:T(8,128)(2,1)}), bf16[16,8,1024]{2,1,0:T(8,128)(2,1)S(1)}, u32[]{:S(2)}, u32[]{:S(2)}) %all-to-all-start.3) | async-done | bytes 262176 | tf_op jit(solution)/shard_map/all_to_all | solution.py:14
  76.4 5.6 %all-to-all-start.4 = ((f32[64,1,256]{2,1,0:T(1,128)}), f32[64,1,256]{2,1,0:T(1,128)S(1)}, u32[]{:S(2)}, u32[]{:S(2)}) async-start(f32[64,1,256]{2,1,0:T(1,128)} %copy.68), calls=%async_computation.4 | async-start | bytes 131072 | tf_op jit(solution)/shard_map/all_to_all | solution.py:14
  82.2 10.9 %all-to-all-done.4 = f32[64,1,256]{2,1,0:T(1,128)S(1)} async-done(((f32[64,1,256]{2,1,0:T(1,128)}), f32[64,1,256]{2,1,0:T(1,128)S(1)}, u32[]{:S(2)}, u32[]{:S(2)}) %all-to-all-start.4) | async-done | bytes 65568 | tf_op jit(solution)/shard_map/all_to_all | solution.py:14
  94.9 4.4 %collective-permute-start.5 = (f32[16]{0:T(128)S(1)}, f32[16]{0:T(128)S(1)}, u32[]{:S(2)}, u32[]{:S(2)}) collective-permute-start(f32[16]{0:T(128)S(1)} %multiply_reduce_fusion.3), channel_id=1, source_target_pairs={{0,64},{64,0},{1,65},{65,1},{2,66},{66,2},{3,67},{67,3},{4,68},{68... | collective-permute-start | bytes 200 | tf_op jit(solution)/shard_map/ppermute | solution.py:30
  99.3 0.8 collective-permute-done.5
  101.2 1.3 %collective-permute-done.6 = f32[16]{0:T(128)S(1)} collective-permute-done((f32[16]{0:T(128)S(1)}, f32[16]{0:T(128)S(1)}, u32[]{:S(2)}, u32[]{:S(2)}) %collective-permute-start.6) | collective-permute-done | bytes 96 | tf_op jit(solution)/shard_map/ppermute | solution.py:30
  (75 shorter events, 8.6 us)
Async XLA Ops:
  1.6 50.6 %collective-permute-start.4 = (bf16[128,1024]{1,0:T(8,128)(2,1)S(1)}, bf16[128,1024]{1,0:T(8,128)(2,1)S(1)}, u32[]{:S(2)}, u32[]{:S(2)}) collective-permute-start(bf16[128,1024]{1,0:T(8,128)(2,1)S(1)} %pad_maximum_fusion.1), channel_id=1, source_target_pairs={{24,0},{0,8},{8,16},{16,24},{25,1},{1,9},{9,17},{17,25},{26,2},{2,... | collective-permute-start | bytes 786440 | tf_op jit(solution)/shard_map/ppermute | solution.py:24
  5.5 46.7 %collective-permute-start.3 = (bf16[128,1024]{1,0:T(8,128)(2,1)S(1)}, bf16[128,1024]{1,0:T(8,128)(2,1)S(1)}, u32[]{:S(2)}, u32[]{:S(2)}) collective-permute-start(bf16[128,1024]{1,0:T(8,128)(2,1)S(1)} %pad_maximum_fusion.1), channel_id=1, source_target_pairs={{16,0},{24,8},{0,16},{8,24},{17,1},{25,9},{1,17},{9,25},{18,2},{26... | collective-permute-start | bytes 786440 | tf_op jit(solution)/shard_map/ppermute | solution.py:24
  10.6 41.7 %collective-permute-start.2 = (bf16[128,1024]{1,0:T(8,128)(2,1)S(1)}, bf16[128,1024]{1,0:T(8,128)(2,1)S(1)}, u32[]{:S(2)}, u32[]{:S(2)}) collective-permute-start(bf16[128,1024]{1,0:T(8,128)(2,1)S(1)} %pad_maximum_fusion.1), channel_id=1, source_target_pairs={{8,0},{16,8},{24,16},{0,24},{9,1},{17,9},{25,17},{1,25},{10,2},{18... | collective-permute-start | bytes 786440 | tf_op jit(solution)/shard_map/ppermute | solution.py:24
  16.2 16.3 %collective-permute-start = (s32[]{:T(128)}, s32[]{:T(128)}, u32[]{:S(2)}, u32[]{:S(2)}) collective-permute-start(s32[]{:T(128)} %add.134), channel_id=1, source_target_pairs={{0,64},{64,0},{1,65},{65,1},{2,66},{66,2},{3,67},{67,3},{4,68},{68... | collective-permute-start | bytes 20 | tf_op jit(solution)/shard_map/ppermute | solution.py:30
  24.2 21.1 %all-to-all-start.1 = ((bf16[64,2,1024]{2,1,0:T(2,128)(2,1)}), bf16[64,2,1024]{2,1,0:T(2,128)(2,1)S(1)}, u32[]{:S(2)}, u32[]{:S(2)}) async-start(bf16[64,2,1024]{2,1,0:T(2,128)(2,1)} %copy.63), calls=%async_computation.1 | async-start | bytes 524288 | tf_op jit(solution)/shard_map/all_to_all | solution.py:14
  33.1 2.8 %collective-permute-start.1 = (s32[]{:T(128)}, s32[]{:T(128)}, u32[]{:S(2)}, u32[]{:S(2)}) collective-permute-start(s32[]{:T(128)} %max.6), channel_id=1, source_target_pairs={{0,128},{128,0},{1,129},{129,1},{2,130},{130,2},{3,131},{131,3},{4... | collective-permute-start | bytes 20 | tf_op jit(solution)/shard_map/ppermute | solution.py:30
  45.4 0.7 copy-start.2
  45.4 15.6 %copy-start = (bf16[64,1024]{1,0:T(8,128)(2,1)S(1)}, bf16[64,1024]{1,0:T(8,128)(2,1)}, u32[]{:S(2)}) copy-start(bf16[64,1024]{1,0:T(8,128)(2,1)} %param.17) | copy-start | bytes 393220
  45.4 15.6 %copy-start.1 = (bf16[1024,64]{0,1:T(8,128)(2,1)S(1)}, bf16[1024,64]{0,1:T(8,128)(2,1)}, u32[]{:S(2)}) copy-start(bf16[1024,64]{0,1:T(8,128)(2,1)} %param.16) | copy-start | bytes 393220
  46.9 14.1 %all-to-all-start.2 = ((bf16[16,8,1024]{2,1,0:T(8,128)(2,1)}), bf16[16,8,1024]{2,1,0:T(8,128)(2,1)S(1)}, u32[]{:S(2)}, u32[]{:S(2)}) async-start(bf16[16,8,1024]{2,1,0:T(8,128)(2,1)} %broadcast_in_dim.118), calls=%async_computation.2 | async-start | bytes 524288 | tf_op jit(solution)/shard_map/all_to_all | solution.py:14
  61.1 32.3 %copy-start.3 = (f32[16]{0:T(128)S(1)}, f32[16]{0:T(128)}, u32[]{:S(2)}) copy-start(f32[16]{0:T(128)} %param.18) | copy-start | bytes 196
  61.1 33.3 %copy-start.4 = (s32[8]{0:T(128)S(1)}, s32[8]{0:T(128)}, u32[]{:S(2)}) copy-start(s32[8]{0:T(128)} %param.14) | copy-start | bytes 100
  62.6 12.2 %all-to-all-start.3 = ((bf16[16,8,1024]{2,1,0:T(8,128)(2,1)}), bf16[16,8,1024]{2,1,0:T(8,128)(2,1)S(1)}, u32[]{:S(2)}, u32[]{:S(2)}) async-start(bf16[16,8,1024]{2,1,0:T(8,128)(2,1)} %fusion.12), calls=%async_computation.3 | async-start | bytes 524288 | tf_op jit(solution)/shard_map/all_to_all | solution.py:14
  76.4 16.8 %all-to-all-start.4 = ((f32[64,1,256]{2,1,0:T(1,128)}), f32[64,1,256]{2,1,0:T(1,128)S(1)}, u32[]{:S(2)}, u32[]{:S(2)}) async-start(f32[64,1,256]{2,1,0:T(1,128)} %copy.68), calls=%async_computation.4 | async-start | bytes 131072 | tf_op jit(solution)/shard_map/all_to_all | solution.py:14
  94.9 5.2 %collective-permute-start.5 = (f32[16]{0:T(128)S(1)}, f32[16]{0:T(128)S(1)}, u32[]{:S(2)}, u32[]{:S(2)}) collective-permute-start(f32[16]{0:T(128)S(1)} %multiply_reduce_fusion.3), channel_id=1, source_target_pairs={{0,64},{64,0},{1,65},{65,1},{2,66},{66,2},{3,67},{67,3},{4,68},{68... | collective-permute-start | bytes 200 | tf_op jit(solution)/shard_map/ppermute | solution.py:30
  100.1 2.4 %collective-permute-start.6 = (f32[16]{0:T(128)S(1)}, f32[16]{0:T(128)S(1)}, u32[]{:S(2)}, u32[]{:S(2)}) collective-permute-start(f32[16]{0:T(128)S(1)} %add.139), channel_id=1, source_target_pairs={{0,128},{128,0},{1,129},{129,1},{2,130},{130,2},{3,131},{131,3},{4... | collective-permute-start | bytes 200 | tf_op jit(solution)/shard_map/ppermute | solution.py:30

commit v6 on v5

--- a/solution.py
+++ b/solution.py
@@ -1,6 +1,10 @@
+import functools
+
 import jax
 import jax.numpy as jnp
 from jax import lax
+from jax.experimental import pallas as pl
+from jax.experimental.pallas import tpu as pltpu
 from jax.sharding import Mesh
 from jax.sharding import PartitionSpec as P
 
@@ -30,14 +34,102 @@
     return lax.ppermute(array, axis, [(0, 1), (1, 0)])
 
 
-def rounded(x):
-    return lax.reduce_precision(x, exponent_bits=8, mantissa_bits=7)
-
-
-def thirds(x):
-    high = rounded(x)
-    middle = rounded(x - high)
-    return high, middle, rounded(x - high - middle)
+def gather_kernel(
+    peers, place_ref, triples, words, triples_v, words_v, gain, weight, table,
+    sent, spot_ref, tiles, ids, lanes, rows, sems,
+):
+    place = place_ref[0]
+    n_triples, seq_len = ids.shape
+    lead = triples.shape[1]
+    toks = n_triples * seq_len
+    entries, width = table.shape
+    half = width // 2
+    shift = entries.bit_length() - 1
+    low = place * entries
+
+    lanes[...] = jnp.zeros_like(lanes)
+    share = gain.shape[1]
+    lanes[0:1, 0:share] = gain[...] * weight[...]
+    exact = lanes[...]
+    high = exact.astype(jnp.bfloat16).astype(jnp.float32)
+    middle = (exact - high).astype(jnp.bfloat16).astype(jnp.float32)
+    least = (exact - high - middle).astype(jnp.bfloat16).astype(jnp.float32)
+    parts = high + pltpu.roll(middle, share, 1) + pltpu.roll(least, 2 * share, 1)
+    sent[:, :, 0:half] = jnp.zeros((peers, 2, half), sent.dtype)
+    sent[:, :, half:] = jnp.broadcast_to(parts[None, 0:2], (peers, 2, LANES)).astype(sent.dtype)
+
+    ids[:, 0:lead] = triples_v[...]
+    ids[:, lead:] = words_v[...]
+    order = lax.broadcasted_iota(jnp.int32, ids.shape, 0) * seq_len
+    order = order + lax.broadcasted_iota(jnp.int32, ids.shape, 1)
+    keys = (ids[...] >> shift) * toks + order
+
+    def copy(number, local):
+        start = pl.multiple_of((local >> 3) * 8, 8)
+        return pltpu.make_async_copy(
+            table.at[pl.ds(start, 8), :], tiles.at[number], sems.at[number]
+        )
+
+    def scan(i, carry):
+        spot, first, held = carry
+        for j in range(seq_len):
+            token = triples[i, j] if j < lead else words[i, j - lead]
+            key = (token >> shift) * toks + (i * seq_len + j)
+            spot = spot + (key < keys).astype(jnp.int32)
+            local = token - low
+            mine = (local >= 0) & (local < entries)
+
+            @pl.when(mine & (held < peers))
+            def _(local=local, held=held):
+                rows[held] = local
+                copy(held, local).start()
+
+            first = first + (local < 0).astype(jnp.int32)
+            held = held + mine.astype(jnp.int32)
+        return spot, first, held
+
+    zero = jnp.int32(0)
+    spot, first, held = lax.fori_loop(
+        0, n_triples, scan, (jnp.zeros(ids.shape, jnp.int32), zero, zero)
+    )
+    spot_ref[...] = spot
+
+    def place_row(number, carry):
+        local = rows[number]
+        copy(number, local).wait()
+        tile = tiles[number].astype(jnp.float32)
+        here = lax.broadcasted_iota(jnp.int32, tile.shape, 0) == (local & 7)
+        row = jnp.sum(jnp.where(here, tile, 0.0), axis=0, keepdims=True)
+        peer = (first + number) & (peers - 1)
+        pair = jnp.concatenate([row[:, :half], row[:, half:]], axis=0)
+        sent[peer, :, 0:half] = pair.astype(sent.dtype)
+        return carry
+
+    lax.fori_loop(0, jnp.minimum(held, peers), place_row, zero)
+
+
+def gathered(place, triples, words, gain, weight, table, peers):
+    n_triples, seq_len = triples.shape[0], triples.shape[1] + words.shape[1]
+    width = table.shape[1]
+    vmem = pl.BlockSpec(memory_space=pltpu.VMEM)
+    smem = pl.BlockSpec(memory_space=pltpu.SMEM)
+    return pl.pallas_call(
+        functools.partial(gather_kernel, peers),
+        out_shape=(
+            jax.ShapeDtypeStruct((peers, 2, width // 2 + LANES), table.dtype),
+            jax.ShapeDtypeStruct((n_triples, seq_len), jnp.int32),
+        ),
+        in_specs=[smem] * 3 + [vmem] * 4 + [pl.BlockSpec(memory_space=pl.ANY)],
+        out_specs=(vmem, vmem),
+        scratch_shapes=[
+            pltpu.VMEM((peers, 8, width), table.dtype),
+            pltpu.VMEM((n_triples, seq_len), jnp.int32),
+            pltpu.VMEM((8, LANES), jnp.float32),
+            pltpu.SMEM((peers,), jnp.int32),
+            pltpu.SemaphoreType.DMA((peers,)),
+        ],
+        name="gather_rows",
+    )(place, triples, words, triples, words, gain, weight, table)
 
 
 def standardize(values):
@@ -60,13 +152,30 @@
     slots = toks // peers
     share = width // peers
 
+    sent, spot = gathered(
+        place.reshape(1),
+        triples,
+        words,
+        out_gain.reshape(1, -1),
+        class_weight.reshape(1, -1),
+        table,
+        peers,
+    )
+    got = exchange(sent, MP)
+
     owner = ids // entries
-    key = owner * toks + jnp.arange(toks)[None]
-    spot = jnp.sum(key.reshape(-1, 1) < key, axis=0, keepdims=True)
+    spot = spot.reshape(1, toks)
     first = jnp.sum(owner.reshape(-1, 1) < owner, axis=0, keepdims=True)
     trip = (spot - first) // peers
     trips = jnp.max(trip) + 1
     trips = jnp.maximum(trips, swapped(trips, "core"))
+
+    units = up_weight.shape[1]
+    weights = jnp.concatenate([up_weight.T, down_weight], axis=0)
+    weights = from_column(jnp.where(trips <= toks, weights, 0), "zh")
+    up_rows = jnp.concatenate([w[:units] for w in weights], axis=0)
+    down_rows = jnp.concatenate([w[units:] for w in weights], axis=0)
+
     trips = jnp.maximum(trips, swapped(trips, "yl"))
     mine = owner == place
     to_peer = (spot % peers == jnp.arange(peers)[:, None]) & mine
@@ -84,17 +193,9 @@
         picks = (from_peer & (sent_in == now)).astype(bf16)
         return jnp.dot(picks, rows, preferred_element_type=f32)
 
-    units = up_weight.shape[1]
-    weights = from_column(jnp.concatenate([up_weight.T, down_weight], axis=0), "zh")
-    up_rows = jnp.concatenate([w[:units] for w in weights], axis=0)
-    down_rows = jnp.concatenate([w[units:] for w in weights], axis=0)
-
-    score_weight = jnp.concatenate(thirds(out_gain * class_weight)).astype(bf16)
-    score_weight = jnp.pad(score_weight, (0, width - score_weight.size))
-    extra = jnp.broadcast_to(score_weight, (peers, 1, width))
-    got = exchange(jnp.concatenate([rows_of(0), extra], axis=1), MP)
-    embed = taken(0, got[:, 0])
-    score_weight = got[:, 1, : 3 * share].astype(f32).reshape(peers, 3, share)
+    half = width // 2
+    embed = taken(0, jnp.concatenate([got[:, 0, :half], got[:, 1, :half]], axis=1))
+    score_weight = got[:, 0, half : half + 3 * share].astype(f32).reshape(peers, 3, share)
     score_weight = jnp.sum(score_weight, axis=1).reshape(1, width)
 
     def another(state):

time: 104 us -> 110 us (1.058)
  Pallas kernels: 0 us -> 7.41 us
  starting transfers between devices: 42.5 us -> 47.2 us
  local copies, waits for them, and re-layouts: 8.49 us -> 5.79 us
  waiting for transfers between devices: 40.4 us -> 38.6 us
  other arithmetic: 6.88 us -> 5.61 us
    all_to_all x4, waiting for transfers between devices: 36.7 us -> 24.3 us  [exchange(): return lax.all_to_all(blocks, axes, split_axis=0, concat_axis=0, tiled=True)]
    ppermute x3, waiting for transfers between devices: 0.01 us -> 10.2 us  [from_column(): lax.ppermute(array, axis, [((i + step) % peers, i) for i in range(peers)])]
    pallas_call x0 -> x1, Pallas kernels: none -> 7.41 us  [gathered(): pl.pallas_call(functools.partial(gather_kernel, peers), out_shape=(jax.Sh...]
    all_to_all x4, starting transfers between devices: 22.6 us -> 29.9 us  [exchange(): return lax.all_to_all(blocks, axes, split_axis=0, concat_axis=0, tiled=True)]
    gather x1 -> x0, local copies, waits for them, and re-layouts: 3.52 us -> none  [rows_of(): return jnp.take(table, local, axis=0, mode='clip').reshape(peers, 1, width)]
    ppermute x3, starting transfers between devices: 11.4 us -> 8.58 us  [from_column(): lax.ppermute(array, axis, [((i + step) % peers, i) for i in range(peers)])]
  transfers between devices with their start and end apart: 11 -> 11, of which waited for: 7 -> 8; matrix products, arithmetic and copies ran while one was open for 10% -> 4% of each run, Pallas kernels for 0% -> 0%
where the time goes in v6:
time: 110 us; the launch traced here: 109 us
  starting transfers between devices  47.2 us (43%)
  waiting for transfers between devices  38.6 us (35%)
  Pallas kernels  7.41 us (7%)
  local copies, waits for them, and re-layouts  5.79 us (5%)
  other arithmetic  5.61 us (5%)
  between operations  2.81 us (3%)
  matrix products  2.02 us (2%)
    all_to_all x4, starting transfers between devices, exchange(): return lax.all_to_all(blocks, axes, split_axis=0, concat_axis=0, tiled=True)  29.9 us
    all_to_all x4, waiting for transfers between devices, exchange(): return lax.all_to_all(blocks, axes, split_axis=0, concat_axis=0, tiled=True)  24.3 us
    ppermute x3, waiting for transfers between devices, from_column(): lax.ppermute(array, axis, [((i + step) % peers, i) for i in range(peers)])  10.2 us
    ppermute x4, starting transfers between devices, swapped(): return lax.ppermute(array, axis, [(0, 1), (1, 0)])  8.68 us
    ppermute x3, starting transfers between devices, from_column(): lax.ppermute(array, axis, [((i + step) % peers, i) for i in range(peers)])  8.58 us
    pallas_call x1, Pallas kernels, gathered(): pl.pallas_call(functools.partial(gather_kernel, peers), out_shape=(jax.Sh...  7.41 us
    ppermute x4, waiting for transfers between devices, swapped(): return lax.ppermute(array, axis, [(0, 1), (1, 0)])  4.19 us
  transfers between devices with their start and end apart: 11, of which 8 were waited for; matrix products, arithmetic and copies ran while one was open for 4% of the time, Pallas kernels for 0%

profile of v6, /device:TPU:1, one launch (start us, length us, event | category | flops | bytes accessed | tf_op | source)
XLA Modules:
  0.0 109.4 jit_solution(1412707439134630862)
XLA Ops:
  0.7 0.8 copy.74.triples.triples_v
  1.5 0.8 pad_add_fusion
  2.6 7.4 %gather_rows.1 = (bf16[64,2,640]{2,1,0:T(2,128)(2,1)}, s32[8,64]{1,0:T(8,128)}) custom-call(s32[1]{0:T(128)} %bitcast.place_ref, s32[8,3]{1,0:T(8,128)} %copy-done.2, s32[8,61]{1,0:T(8,128)} %words_v.1, s32[8,3]{1,0:T(8,128)} %copy-done.2, s32[8,61]{1,0:T(8,128)} %words_v.1, f32[1,16]{1,0:T(1,128)} %bitcast.57, f32[1,16]{1,0:T(1,128)} %bitcast.58, ...), custom_call_target="tpu_custom_call" | custom-call | tf_op jit(solution)/shard_map/gather_rows/pallas_call | solution.py:116
  10.0 1.3 %fusion.88 = s32[]{:T(128)} fusion(s32[8,64]{1,0:T(8,128)} %get-tuple-element.124, s32[8,64]{1,0:T(8,128)S(1)} %reduce_sum.146), kind=kLoop, calls=%fused_computation.126 | loop fusion | flops 8703 | bytes 4100 | tf_op jit(solution)/shard_map/reduce_max | solution.py:170
  12.0 4.3 %collective-permute-start = (s32[]{:T(128)}, s32[]{:T(128)}, u32[]{:S(2)}, u32[]{:S(2)}) collective-permute-start(s32[]{:T(128)} %add.109), channel_id=1, source_target_pairs={{0,64},{64,0},{1,65},{65,1},{2,66},{66,2},{3,67},{67,3},{4,68},{68... | collective-permute-start | bytes 20 | tf_op jit(solution)/shard_map/ppermute | solution.py:34
  17.0 0.7 reshape.392
  18.7 12.5 %all-to-all-start.1 = ((bf16[64,2,640]{2,1,0:T(2,128)(2,1)}), bf16[64,2,640]{2,1,0:T(2,128)(2,1)S(1)}, u32[]{:S(2)}, u32[]{:S(2)}) async-start(bf16[64,2,640]{2,1,0:T(2,128)(2,1)} %get-tuple-element.125), calls=%async_computation.1 | async-start | bytes 327680 | tf_op jit(solution)/shard_map/all_to_all | solution.py:18
  31.3 2.0 %collective-permute-start.4 = (bf16[128,1024]{1,0:T(8,128)(2,1)S(1)}, bf16[128,1024]{1,0:T(8,128)(2,1)S(1)}, u32[]{:S(2)}, u32[]{:S(2)}) collective-permute-start(bf16[128,1024]{1,0:T(8,128)(2,1)S(1)} %maximum_select_fusion), channel_id=1, source_target_pairs={{24,0},{0,8},{8,16},{16,24},{25,1},{1,9},{9,17},{17,25},{26,2},{2,... | collective-permute-start | bytes 786440 | tf_op jit(solution)/shard_map/ppermute | solution.py:28
  33.3 3.3 %collective-permute-start.3 = (bf16[128,1024]{1,0:T(8,128)(2,1)S(1)}, bf16[128,1024]{1,0:T(8,128)(2,1)S(1)}, u32[]{:S(2)}, u32[]{:S(2)}) collective-permute-start(bf16[128,1024]{1,0:T(8,128)(2,1)S(1)} %maximum_select_fusion), channel_id=1, source_target_pairs={{16,0},{24,8},{0,16},{8,24},{17,1},{25,9},{1,17},{9,25},{18,2},{26... | collective-permute-start | bytes 786440 | tf_op jit(solution)/shard_map/ppermute | solution.py:28
  36.6 3.3 %collective-permute-start.2 = (bf16[128,1024]{1,0:T(8,128)(2,1)S(1)}, bf16[128,1024]{1,0:T(8,128)(2,1)S(1)}, u32[]{:S(2)}, u32[]{:S(2)}) collective-permute-start(bf16[128,1024]{1,0:T(8,128)(2,1)S(1)} %maximum_select_fusion), channel_id=1, source_target_pairs={{8,0},{16,8},{24,16},{0,24},{9,1},{17,9},{25,17},{1,25},{10,2},{18... | collective-permute-start | bytes 786440 | tf_op jit(solution)/shard_map/ppermute | solution.py:28
  39.9 0.9 collective-permute-start.1
  40.8 1.8 %collective-permute-done.1 = s32[]{:T(128)} collective-permute-done((s32[]{:T(128)}, s32[]{:T(128)}, u32[]{:S(2)}, u32[]{:S(2)}) %collective-permute-start.1) | collective-permute-done | bytes 36 | tf_op jit(solution)/shard_map/ppermute | solution.py:34
  45.1 6.7 %all-to-all-start.2 = ((bf16[16,8,1024]{2,1,0:T(8,128)(2,1)}), bf16[16,8,1024]{2,1,0:T(8,128)(2,1)S(1)}, u32[]{:S(2)}, u32[]{:S(2)}) async-start(bf16[16,8,1024]{2,1,0:T(8,128)(2,1)} %broadcast_in_dim.97), calls=%async_computation.2 | async-start | bytes 524288 | tf_op jit(solution)/shard_map/all_to_all | solution.py:18
  51.9 9.2 %collective-permute-done.3 = bf16[128,1024]{1,0:T(8,128)(2,1)S(1)} collective-permute-done((bf16[128,1024]{1,0:T(8,128)(2,1)S(1)}, bf16[128,1024]{1,0:T(8,128)(2,1)S(1)}, u32[]{:S(2)}, u32[]{:S(2)}) %collective-permute-start.3) | collective-permute-done | bytes 262176 | tf_op jit(solution)/shard_map/ppermute | solution.py:28
  61.0 1.0 collective-permute-done.2
  62.1 4.9 %all-to-all-done.2 = bf16[16,8,1024]{2,1,0:T(8,128)(2,1)S(1)} async-done(((bf16[16,8,1024]{2,1,0:T(8,128)(2,1)}), bf16[16,8,1024]{2,1,0:T(8,128)(2,1)S(1)}, u32[]{:S(2)}, u32[]{:S(2)}) %all-to-all-start.2) | async-done | bytes 262176 | tf_op jit(solution)/shard_map/all_to_all | solution.py:18
  67.0 1.5 %fusion.12 = bf16[16,8,1024]{2,1,0:T(8,128)(2,1)} fusion(bf16[64,1024]{1,0:T(8,128)(2,1)S(1)} %get-tuple-element.197, bf16[64,1024]{1,0:T(8,128)(2,1)S(1)} %get-tuple-element.195, bf16[64,1024]{1,0:T(8,128)(2,1)S(1)} %get-tuple-element.193, bf16[64,1024]{1,0:T(8,128)(2,1)S(1)} %get-tuple-element.191, bf16[64,1024]{1,0:T(8,128)(2,1)S(1)} %get-tuple-element.196, ...), kind=kOutput, calls=%fused_computation.19 | convolution fusion | flops 140673024 | bytes 1572864 | tf_op jit(solution)/shard_map/dot_general | solution.py:213
  68.5 3.5 %all-to-all-start.3 = ((bf16[16,8,1024]{2,1,0:T(8,128)(2,1)}), bf16[16,8,1024]{2,1,0:T(8,128)(2,1)S(1)}, u32[]{:S(2)}, u32[]{:S(2)}) async-start(bf16[16,8,1024]{2,1,0:T(8,128)(2,1)} %fusion.12), calls=%async_computation.3 | async-start | bytes 524288 | tf_op jit(solution)/shard_map/all_to_all | solution.py:18
  72.4 8.4 %all-to-all-done.3 = bf16[16,8,1024]{2,1,0:T(8,128)(2,1)S(1)} async-done(((bf16[16,8,1024]{2,1,0:T(8,128)(2,1)}), bf16[16,8,1024]{2,1,0:T(8,128)(2,1)S(1)}, u32[]{:S(2)}, u32[]{:S(2)}) %all-to-all-start.3) | async-done | bytes 262176 | tf_op jit(solution)/shard_map/all_to_all | solution.py:18
  82.3 7.2 %all-to-all-start.4 = ((f32[64,1,256]{2,1,0:T(1,128)}), f32[64,1,256]{2,1,0:T(1,128)S(1)}, u32[]{:S(2)}, u32[]{:S(2)}) async-start(f32[64,1,256]{2,1,0:T(1,128)} %copy.80), calls=%async_computation.4 | async-start | bytes 131072 | tf_op jit(solution)/shard_map/all_to_all | solution.py:18
  89.7 10.9 %all-to-all-done.4 = f32[64,1,256]{2,1,0:T(1,128)S(1)} async-done(((f32[64,1,256]{2,1,0:T(1,128)}), f32[64,1,256]{2,1,0:T(1,128)S(1)}, u32[]{:S(2)}, u32[]{:S(2)}) %all-to-all-start.4) | async-done | bytes 65568 | tf_op jit(solution)/shard_map/all_to_all | solution.py:18
  102.4 3.3 %collective-permute-start.5 = (f32[16]{0:T(128)S(1)}, f32[16]{0:T(128)S(1)}, u32[]{:S(2)}, u32[]{:S(2)}) collective-permute-start(f32[16]{0:T(128)S(1)} %multiply_reduce_fusion.3), channel_id=1, source_target_pairs={{0,64},{64,0},{1,65},{65,1},{2,66},{66,2},{3,67},{67,3},{4,68},{68... | collective-permute-start | bytes 200 | tf_op jit(solution)/shard_map/ppermute | solution.py:34
  105.7 0.8 collective-permute-done.5
  107.3 1.6 %collective-permute-done.6 = f32[16]{0:T(128)S(1)} collective-permute-done((f32[16]{0:T(128)S(1)}, f32[16]{0:T(128)S(1)}, u32[]{:S(2)}, u32[]{:S(2)}) %collective-permute-start.6) | collective-permute-done | bytes 96 | tf_op jit(solution)/shard_map/ppermute | solution.py:34
  (74 shorter events, 8.4 us)
Async XLA Ops:
  0.6 30.6 %copy-start = (bf16[64,1024]{1,0:T(8,128)(2,1)S(1)}, bf16[64,1024]{1,0:T(8,128)(2,1)}, u32[]{:S(2)}) copy-start(bf16[64,1024]{1,0:T(8,128)(2,1)} %param.17) | copy-start | bytes 393220
  0.6 30.6 %copy-start.1 = (bf16[1024,64]{0,1:T(8,128)(2,1)S(1)}, bf16[1024,64]{0,1:T(8,128)(2,1)}, u32[]{:S(2)}) copy-start(bf16[1024,64]{0,1:T(8,128)(2,1)} %param.16) | copy-start | bytes 393220
  1.5 1.1 %copy-start.2 = (s32[8,3]{1,0:T(8,128)}, s32[8,3]{1,0:T(8,128)S(1)}, u32[]{:S(2)}) copy-start(s32[8,3]{1,0:T(8,128)S(1)} %copy.74.triples.triples_v) | copy-start | bytes 292
  12.0 6.1 %collective-permute-start = (s32[]{:T(128)}, s32[]{:T(128)}, u32[]{:S(2)}, u32[]{:S(2)}) collective-permute-start(s32[]{:T(128)} %add.109), channel_id=1, source_target_pairs={{0,64},{64,0},{1,65},{65,1},{2,66},{66,2},{3,67},{67,3},{4,68},{68... | collective-permute-start | bytes 20 | tf_op jit(solution)/shard_map/ppermute | solution.py:34
  18.7 24.5 %all-to-all-start.1 = ((bf16[64,2,640]{2,1,0:T(2,128)(2,1)}), bf16[64,2,640]{2,1,0:T(2,128)(2,1)S(1)}, u32[]{:S(2)}, u32[]{:S(2)}) async-start(bf16[64,2,640]{2,1,0:T(2,128)(2,1)} %get-tuple-element.125), calls=%async_computation.1 | async-start | bytes 327680 | tf_op jit(solution)/shard_map/all_to_all | solution.py:18
  31.3 20.5 %collective-permute-start.4 = (bf16[128,1024]{1,0:T(8,128)(2,1)S(1)}, bf16[128,1024]{1,0:T(8,128)(2,1)S(1)}, u32[]{:S(2)}, u32[]{:S(2)}) collective-permute-start(bf16[128,1024]{1,0:T(8,128)(2,1)S(1)} %maximum_select_fusion), channel_id=1, source_target_pairs={{24,0},{0,8},{8,16},{16,24},{25,1},{1,9},{9,17},{17,25},{26,2},{2,... | collective-permute-start | bytes 786440 | tf_op jit(solution)/shard_map/ppermute | solution.py:28
  33.3 27.8 %collective-permute-start.3 = (bf16[128,1024]{1,0:T(8,128)(2,1)S(1)}, bf16[128,1024]{1,0:T(8,128)(2,1)S(1)}, u32[]{:S(2)}, u32[]{:S(2)}) collective-permute-start(bf16[128,1024]{1,0:T(8,128)(2,1)S(1)} %maximum_select_fusion), channel_id=1, source_target_pairs={{16,0},{24,8},{0,16},{8,24},{17,1},{25,9},{1,17},{9,25},{18,2},{26... | collective-permute-start | bytes 786440 | tf_op jit(solution)/shard_map/ppermute | solution.py:28
  36.6 25.4 %collective-permute-start.2 = (bf16[128,1024]{1,0:T(8,128)(2,1)S(1)}, bf16[128,1024]{1,0:T(8,128)(2,1)S(1)}, u32[]{:S(2)}, u32[]{:S(2)}) collective-permute-start(bf16[128,1024]{1,0:T(8,128)(2,1)S(1)} %maximum_select_fusion), channel_id=1, source_target_pairs={{8,0},{16,8},{24,16},{0,24},{9,1},{17,9},{25,17},{1,25},{10,2},{18... | collective-permute-start | bytes 786440 | tf_op jit(solution)/shard_map/ppermute | solution.py:28
  39.9 2.7 %collective-permute-start.1 = (s32[]{:T(128)}, s32[]{:T(128)}, u32[]{:S(2)}, u32[]{:S(2)}) collective-permute-start(s32[]{:T(128)} %max.6), channel_id=1, source_target_pairs={{0,128},{128,0},{1,129},{129,1},{2,130},{130,2},{3,131},{131,3},{4... | collective-permute-start | bytes 20 | tf_op jit(solution)/shard_map/ppermute | solution.py:34
  43.6 0.7 copy-start.3
  45.1 21.9 %all-to-all-start.2 = ((bf16[16,8,1024]{2,1,0:T(8,128)(2,1)}), bf16[16,8,1024]{2,1,0:T(8,128)(2,1)S(1)}, u32[]{:S(2)}, u32[]{:S(2)}) async-start(bf16[16,8,1024]{2,1,0:T(8,128)(2,1)} %broadcast_in_dim.97), calls=%async_computation.2 | async-start | bytes 524288 | tf_op jit(solution)/shard_map/all_to_all | solution.py:18
  67.0 33.8 %copy-start.4 = (f32[16]{0:T(128)S(1)}, f32[16]{0:T(128)}, u32[]{:S(2)}) copy-start(f32[16]{0:T(128)} %param.18) | copy-start | bytes 196
  67.0 34.8 %copy-start.5 = (s32[8]{0:T(128)S(1)}, s32[8]{0:T(128)}, u32[]{:S(2)}) copy-start(s32[8]{0:T(128)} %param.14) | copy-start | bytes 100
  68.5 12.2 %all-to-all-start.3 = ((bf16[16,8,1024]{2,1,0:T(8,128)(2,1)}), bf16[16,8,1024]{2,1,0:T(8,128)(2,1)S(1)}, u32[]{:S(2)}, u32[]{:S(2)}) async-start(bf16[16,8,1024]{2,1,0:T(8,128)(2,1)} %fusion.12), calls=%async_computation.3 | async-start | bytes 524288 | tf_op jit(solution)/shard_map/all_to_all | solution.py:18
  82.3 18.3 %all-to-all-start.4 = ((f32[64,1,256]{2,1,0:T(1,128)}), f32[64,1,256]{2,1,0:T(1,128)S(1)}, u32[]{:S(2)}, u32[]{:S(2)}) async-start(f32[64,1,256]{2,1,0:T(1,128)} %copy.80), calls=%async_computation.4 | async-start | bytes 131072 | tf_op jit(solution)/shard_map/all_to_all | solution.py:18
  102.4 4.1 %collective-permute-start.5 = (f32[16]{0:T(128)S(1)}, f32[16]{0:T(128)S(1)}, u32[]{:S(2)}, u32[]{:S(2)}) collective-permute-start(f32[16]{0:T(128)S(1)} %multiply_reduce_fusion.3), channel_id=1, source_target_pairs={{0,64},{64,0},{1,65},{65,1},{2,66},{66,2},{3,67},{67,3},{4,68},{68... | collective-permute-start | bytes 200 | tf_op jit(solution)/shard_map/ppermute | solution.py:34
  106.5 2.4 %collective-permute-start.6 = (f32[16]{0:T(128)S(1)}, f32[16]{0:T(128)S(1)}, u32[]{:S(2)}, u32[]{:S(2)}) collective-permute-start(f32[16]{0:T(128)S(1)} %add.115), channel_id=1, source_target_pairs={{0,128},{128,0},{1,129},{129,1},{2,130},{130,2},{3,131},{131,3},{4... | collective-permute-start | bytes 200 | tf_op jit(solution)/shard_map/ppermute | solution.py:34

commit v7 on v5

--- a/solution.py
+++ b/solution.py
@@ -1,6 +1,10 @@
+import functools
+
 import jax
 import jax.numpy as jnp
 from jax import lax
+from jax.experimental import pallas as pl
+from jax.experimental.pallas import tpu as pltpu
 from jax.sharding import Mesh
 from jax.sharding import PartitionSpec as P
 
@@ -30,14 +34,145 @@
     return lax.ppermute(array, axis, [(0, 1), (1, 0)])
 
 
-def rounded(x):
-    return lax.reduce_precision(x, exponent_bits=8, mantissa_bits=7)
-
-
-def thirds(x):
-    high = rounded(x)
-    middle = rounded(x - high)
-    return high, middle, rounded(x - high - middle)
+def send_kernel(
+    peers, where_ref, triples, words, gain, weight, table, sent, tiles, lanes, rows, held, sems
+):
+    lead, n_triples = triples.shape
+    seq_len = lead + words.shape[1]
+    entries, width = table.shape
+    half = width // 2
+    low = where_ref[0] * entries
+    skipped = where_ref[1] * peers
+    group = 8
+
+    def copy(number, local):
+        start = pl.multiple_of((local >> 3) * 8, 8)
+        return pltpu.make_async_copy(
+            table.at[pl.ds(start, 8), :], tiles.at[number], sems.at[number]
+        )
+
+    held[0] = 0
+
+    def scan(i, below):
+        for g in range(0, seq_len, group):
+            locals_ = [
+                (triples[j, i] if j < lead else words[i, j - lead]) - low
+                for j in range(g, g + group)
+            ]
+            outside = [local & -entries for local in locals_]
+            any_mine = outside[0] == 0
+            for out in outside[1:]:
+                any_mine = any_mine | (out == 0)
+            for local in locals_:
+                below = below - (local >> 31)
+
+            @pl.when(any_mine)
+            def _(locals_=locals_, outside=outside):
+                for local, out in zip(locals_, outside):
+                    @pl.when(out == 0)
+                    def _(local=local):
+                        number = held[0] - skipped
+                        held[0] = held[0] + 1
+
+                        @pl.when((number >= 0) & (number < peers))
+                        def _():
+                            rows[number] = local
+                            copy(number, local).start()
+
+        return below
+
+    below = lax.fori_loop(0, n_triples, scan, jnp.int32(0))
+
+    lanes[...] = jnp.zeros_like(lanes)
+    share = gain.shape[1]
+    lanes[0:1, 0:share] = gain[...] * weight[...]
+    exact = lanes[...]
+    high = exact.astype(jnp.bfloat16).astype(jnp.float32)
+    middle = (exact - high).astype(jnp.bfloat16).astype(jnp.float32)
+    least = (exact - high - middle).astype(jnp.bfloat16).astype(jnp.float32)
+    parts = high + pltpu.roll(middle, share, 1) + pltpu.roll(least, 2 * share, 1)
+    trips = ((held[0] + peers - 1) // peers).astype(jnp.float32)
+    row_of = lax.broadcasted_iota(jnp.int32, parts.shape, 0)
+    lane = lax.broadcasted_iota(jnp.int32, parts.shape, 1)
+    parts = jnp.where((row_of == 1) & (lane == 1), trips, parts)
+    slot_at = (row_of == 1) & (lane == 0)
+    blank = jnp.where(slot_at, -1.0, parts)[0:2]
+    sent[:, :, 0:half] = jnp.zeros((peers, 2, half), sent.dtype)
+    sent[:, :, half:] = jnp.broadcast_to(blank[None], (peers, 2, LANES)).astype(sent.dtype)
+
+    def place_row(number, carry):
+        local = rows[number]
+        copy(number, local).wait()
+        tile = tiles[number].astype(jnp.float32)
+        picked = lax.broadcasted_iota(jnp.int32, tile.shape, 0) == (local & 7)
+        row = jnp.sum(jnp.where(picked, tile, 0.0), axis=0, keepdims=True)
+        pair = jnp.concatenate([row[:, :half], row[:, half:]], axis=0)
+        spot = below + skipped + number
+        peer = spot & (peers - 1)
+        slot = (spot // peers).astype(jnp.float32)
+        sent[peer, :, 0:half] = pair.astype(sent.dtype)
+        sent[peer, :, half:] = jnp.where(slot_at, slot, parts)[0:2].astype(sent.dtype)
+        return carry
+
+    here = jnp.clip(held[0] - skipped, 0, peers)
+    lax.fori_loop(0, here, place_row, jnp.int32(0))
+
+
+def to_send(place, trip, triples, words, gain, weight, table, peers):
+    width = table.shape[1]
+    vmem = pl.BlockSpec(memory_space=pltpu.VMEM)
+    smem = pl.BlockSpec(memory_space=pltpu.SMEM)
+    return pl.pallas_call(
+        functools.partial(send_kernel, peers),
+        out_shape=jax.ShapeDtypeStruct((peers, 2, width // 2 + LANES), table.dtype),
+        in_specs=[smem] * 3 + [vmem] * 2 + [pl.BlockSpec(memory_space=pl.ANY)],
+        out_specs=vmem,
+        scratch_shapes=[
+            pltpu.VMEM((peers, 8, width), table.dtype),
+            pltpu.VMEM((8, LANES), jnp.float32),
+            pltpu.SMEM((peers,), jnp.int32),
+            pltpu.SMEM((1,), jnp.int32),
+            pltpu.SemaphoreType.DMA((peers,)),
+        ],
+        name="send_rows",
+    )(jnp.stack([place, trip]), triples.T, words, gain, weight, table)
+
+
+def position_kernel(entries, triples, words, words_v, spot_ref, ids_ref):
+    n_triples, seq_len = spot_ref.shape
+    lead = triples.shape[0]
+    toks = n_triples * seq_len
+    shift = entries.bit_length() - 1
+    for j in range(lead):
+        for i in range(n_triples):
+            ids_ref[i : i + 1, j : j + 1] = jnp.full((1, 1), triples[j, i], jnp.int32)
+    ids_ref[:, lead:] = words_v[...]
+    keys = (ids_ref[...] >> shift) * toks
+    keys = keys + lax.broadcasted_iota(jnp.int32, keys.shape, 0) * seq_len
+    keys = keys + lax.broadcasted_iota(jnp.int32, keys.shape, 1)
+
+    def scan(i, spot):
+        for j in range(seq_len):
+            token = triples[j, i] if j < lead else words[i, j - lead]
+            key = (token >> shift) * toks + (i * seq_len + j)
+            spot = spot + (key < keys).astype(jnp.int32)
+        return spot
+
+    spot_ref[...] = lax.fori_loop(0, n_triples, scan, jnp.zeros(keys.shape, jnp.int32))
+
+
+def positions(triples, words, entries):
+    shape = (triples.shape[0], triples.shape[1] + words.shape[1])
+    smem = pl.BlockSpec(memory_space=pltpu.SMEM)
+    vmem = pl.BlockSpec(memory_space=pltpu.VMEM)
+    return pl.pallas_call(
+        functools.partial(position_kernel, entries),
+        out_shape=jax.ShapeDtypeStruct(shape, jnp.int32),
+        in_specs=[smem, smem, vmem],
+        out_specs=vmem,
+        scratch_shapes=[pltpu.VMEM(shape, jnp.int32)],
+        name="positions",
+    )(triples.T, words, words)
 
 
 def standardize(values):
@@ -53,55 +188,41 @@
     bf16, f32 = jnp.bfloat16, jnp.float32
     peers = lax.axis_size(MP)
     place = lax.axis_index(MP)
-    ids = jnp.concatenate([triples, words], axis=1).reshape(1, -1)
     seq_len = triples.shape[1] + words.shape[1]
-    toks = ids.shape[1]
+    toks = triples.shape[0] * seq_len
     entries, width = table.shape
     slots = toks // peers
     share = width // peers
-
-    owner = ids // entries
-    key = owner * toks + jnp.arange(toks)[None]
-    spot = jnp.sum(key.reshape(-1, 1) < key, axis=0, keepdims=True)
-    first = jnp.sum(owner.reshape(-1, 1) < owner, axis=0, keepdims=True)
-    trip = (spot - first) // peers
-    trips = jnp.max(trip) + 1
-    trips = jnp.maximum(trips, swapped(trips, "core"))
-    trips = jnp.maximum(trips, swapped(trips, "yl"))
-    mine = owner == place
-    to_peer = (spot % peers == jnp.arange(peers)[:, None]) & mine
-    kept = spot == jnp.arange(slots)[:, None] * peers + place
-    sender = jnp.sum(jnp.where(kept, owner, 0), axis=1, keepdims=True)
-    sent_in = jnp.sum(jnp.where(kept, trip, 0), axis=1, keepdims=True)
-    from_peer = sender == jnp.arange(peers)[None]
-
-    def rows_of(now):
-        chosen = to_peer & (trip == now)
-        local = jnp.sum(jnp.where(chosen, ids - place * entries, 0), axis=1)
-        return jnp.take(table, local, axis=0, mode="clip").reshape(peers, 1, width)
-
-    def taken(now, rows):
-        picks = (from_peer & (sent_in == now)).astype(bf16)
-        return jnp.dot(picks, rows, preferred_element_type=f32)
 
     units = up_weight.shape[1]
     weights = from_column(jnp.concatenate([up_weight.T, down_weight], axis=0), "zh")
     up_rows = jnp.concatenate([w[:units] for w in weights], axis=0)
     down_rows = jnp.concatenate([w[units:] for w in weights], axis=0)
 
-    score_weight = jnp.concatenate(thirds(out_gain * class_weight)).astype(bf16)
-    score_weight = jnp.pad(score_weight, (0, width - score_weight.size))
-    extra = jnp.broadcast_to(score_weight, (peers, 1, width))
-    got = exchange(jnp.concatenate([rows_of(0), extra], axis=1), MP)
-    embed = taken(0, got[:, 0])
-    score_weight = got[:, 1, : 3 * share].astype(f32).reshape(peers, 3, share)
+    gains = out_gain.reshape(1, -1), class_weight.reshape(1, -1)
+
+    def rows_of(trip):
+        return exchange(to_send(place, trip, triples, words, *gains, table, peers), MP)
+
+    half = width // 2
+
+    def taken(got):
+        picks = got[:, 1, half : half + 1].astype(f32) == jnp.arange(slots, dtype=f32)[None]
+        rows = jnp.concatenate([got[:, 0, :half], got[:, 1, :half]], axis=1)
+        return lax.dot_general(
+            picks.astype(bf16), rows, (((0,), (0,)), ((), ())), preferred_element_type=f32
+        )
+
+    got = rows_of(jnp.int32(0))
+    trips = jnp.max(got[:, 1, half + 1].astype(f32)).astype(jnp.int32)
+    score_weight = got[:, 0, half : half + 3 * share].astype(f32).reshape(peers, 3, share)
     score_weight = jnp.sum(score_weight, axis=1).reshape(1, width)
 
     def another(state):
-        now, embed = state
-        return now + 1, embed + taken(now, exchange(rows_of(now), MP)[:, 0])
-
-    _, embed = lax.while_loop(lambda state: state[0] < trips, another, (jnp.int32(1), embed))
+        trip, embed = state
+        return trip + 1, embed + taken(rows_of(trip))
+
+    _, embed = lax.while_loop(lambda state: state[0] < trips, another, (jnp.int32(1), taken(got)))
 
     normed = (standardize(embed) * in_gain).astype(bf16)
     everyone = to_everyone(normed, ACT)
@@ -121,6 +242,7 @@
     level = got[:, 0, : slots * share].reshape(peers, slots, share)
     by_spot = (level * out_gain).astype(bf16).transpose(1, 0, 2).reshape(toks, share)
     score = got[:, 0, slots * share :][:, :slots].T.reshape(1, toks)
+    spot = positions(triples, words, entries).reshape(1, toks)
     where = spot == jnp.arange(toks)[:, None]
     encoded = lax.dot_general(
         by_spot, where.astype(bf16), (((0,), (0,)), ((), ())), preferred_element_type=f32

time: 104 us -> 99.9 us (0.961)
  Pallas kernels: 0 us -> 6.69 us
  waiting for transfers between devices: 40.4 us -> 35.8 us
  local copies, waits for them, and re-layouts: 8.49 us -> 4 us
  other arithmetic: 6.88 us -> 4.96 us
  starting transfers between devices: 42.5 us -> 44.2 us
  between operations: 2.77 us -> 1.58 us
    all_to_all x4, waiting for transfers between devices: 36.7 us -> 21.9 us  [exchange(): return lax.all_to_all(blocks, axes, split_axis=0, concat_axis=0, tiled=True)]
    ppermute x3, waiting for transfers between devices: 0.01 us -> 11.4 us  [from_column(): lax.ppermute(array, axis, [((i + step) % peers, i) for i in range(peers)])]
    all_to_all x4, starting transfers between devices: 22.6 us -> 32 us  [exchange(): return lax.all_to_all(blocks, axes, split_axis=0, concat_axis=0, tiled=True)]
    pallas_call x0 -> x2, Pallas kernels: none -> 6.69 us  [the longest x1 4.54 us: to_send(): pl.pallas_call(functools.partial(send_kernel, peers), out_shape=jax.Shape...]
    ppermute x4 -> x2, starting transfers between devices: 8.49 us -> 3.63 us  [swapped(): return lax.ppermute(array, axis, [(0, 1), (1, 0)])]
    gather x1 -> x0, local copies, waits for them, and re-layouts: 3.52 us -> none  [rows_of(): return jnp.take(table, local, axis=0, mode='clip').reshape(peers, 1, width)]
    ppermute x3, starting transfers between devices: 11.4 us -> 8.58 us  [from_column(): lax.ppermute(array, axis, [((i + step) % peers, i) for i in range(peers)])]
    ppermute x4 -> x2, waiting for transfers between devices: 3.68 us -> 2.49 us  [swapped(): return lax.ppermute(array, axis, [(0, 1), (1, 0)])]
  transfers between devices with their start and end apart: 11 -> 9, of which waited for: 7 -> 8; matrix products, arithmetic and copies ran while one was open for 10% -> 5% of each run, Pallas kernels for 0% -> 2%
where the time goes in v7:
time: 99.9 us; the launch traced here: 99.4 us
  starting transfers between devices  44.2 us (44%)
  waiting for transfers between devices  35.8 us (36%)
  Pallas kernels  6.69 us (7%)
  other arithmetic  4.96 us (5%)
  local copies, waits for them, and re-layouts  4 us (4%)
  matrix products  2.08 us (2%)
  between operations  1.58 us (2%)
    all_to_all x4, starting transfers between devices, exchange(): return lax.all_to_all(blocks, axes, split_axis=0, concat_axis=0, tiled=True)  32 us
    all_to_all x4, waiting for transfers between devices, exchange(): return lax.all_to_all(blocks, axes, split_axis=0, concat_axis=0, tiled=True)  21.9 us
    ppermute x3, waiting for transfers between devices, from_column(): lax.ppermute(array, axis, [((i + step) % peers, i) for i in range(peers)])  11.4 us
    ppermute x3, starting transfers between devices, from_column(): lax.ppermute(array, axis, [((i + step) % peers, i) for i in range(peers)])  8.58 us
    pallas_call x1, Pallas kernels, to_send(): pl.pallas_call(functools.partial(send_kernel, peers), out_shape=jax.Shape...  4.54 us
    ppermute x2, starting transfers between devices, swapped(): return lax.ppermute(array, axis, [(0, 1), (1, 0)])  3.63 us
    ppermute x2, waiting for transfers between devices, swapped(): return lax.ppermute(array, axis, [(0, 1), (1, 0)])  2.49 us
    pallas_call x1, Pallas kernels, positions(): pl.pallas_call(functools.partial(position_kernel, entries), out_shape=jax...  2.15 us
  transfers between devices with their start and end apart: 9, of which 8 were waited for; matrix products, arithmetic and copies ran while one was open for 5% of the time, Pallas kernels for 2%

profile of v7, /device:TPU:1, one launch (start us, length us, event | category | flops | bytes accessed | tf_op | source)
XLA Modules:
  0.0 99.4 jit_solution(17988949178359060475)
XLA Ops:
  1.3 4.5 %send_rows.2 = bf16[64,2,640]{2,1,0:T(2,128)(2,1)} custom-call(s32[2]{0:T(128)} %pad_add_fusion.1.where_ref, s32[3,8]{1,0:T(4,128)} %bitcast.53, s32[8,61]{1,0:T(8,128)} %words_v.1, f32[1,16]{1,0:T(1,128)} %bitcast.57, f32[1,16]{1,0:T(1,128)} %bitcast.60, bf16[2048,1024]{1,0:T(8,128)(2,1)} %table.1), custom_call_target="tpu_custom_call" | custom-call | tf_op jit(solution)/shard_map/send_rows/pallas_call | solution.py:125
  5.8 15.3 %all-to-all-start.1 = ((bf16[64,2,640]{2,1,0:T(2,128)(2,1)}), bf16[64,2,640]{2,1,0:T(2,128)(2,1)S(1)}, u32[]{:S(2)}, u32[]{:S(2)}) async-start(bf16[64,2,640]{2,1,0:T(2,128)(2,1)} %send_rows.2), calls=%async_computation.1 | async-start | bytes 327680 | tf_op jit(solution)/shard_map/all_to_all | solution.py:18
  21.2 2.0 %collective-permute-start.2 = (bf16[128,1024]{1,0:T(8,128)(2,1)S(1)}, bf16[128,1024]{1,0:T(8,128)(2,1)S(1)}, u32[]{:S(2)}, u32[]{:S(2)}) collective-permute-start(bf16[128,1024]{1,0:T(8,128)(2,1)S(1)} %pad_maximum_fusion), channel_id=1, source_target_pairs={{24,0},{0,8},{8,16},{16,24},{25,1},{1,9},{9,17},{17,25},{26,2},{2,... | collective-permute-start | bytes 786440 | tf_op jit(solution)/shard_map/ppermute | solution.py:28
  23.2 3.3 %collective-permute-start.1 = (bf16[128,1024]{1,0:T(8,128)(2,1)S(1)}, bf16[128,1024]{1,0:T(8,128)(2,1)S(1)}, u32[]{:S(2)}, u32[]{:S(2)}) collective-permute-start(bf16[128,1024]{1,0:T(8,128)(2,1)S(1)} %pad_maximum_fusion), channel_id=1, source_target_pairs={{16,0},{24,8},{0,16},{8,24},{17,1},{25,9},{1,17},{9,25},{18,2},{26... | collective-permute-start | bytes 786440 | tf_op jit(solution)/shard_map/ppermute | solution.py:28
  26.5 3.3 %collective-permute-start = (bf16[128,1024]{1,0:T(8,128)(2,1)S(1)}, bf16[128,1024]{1,0:T(8,128)(2,1)S(1)}, u32[]{:S(2)}, u32[]{:S(2)}) collective-permute-start(bf16[128,1024]{1,0:T(8,128)(2,1)S(1)} %pad_maximum_fusion), channel_id=1, source_target_pairs={{8,0},{16,8},{24,16},{0,24},{9,1},{17,9},{25,17},{1,25},{10,2},{18... | collective-permute-start | bytes 786440 | tf_op jit(solution)/shard_map/ppermute | solution.py:28
  29.8 3.0 %all-to-all-done.1 = bf16[64,2,640]{2,1,0:T(2,128)(2,1)S(1)} async-done(((bf16[64,2,640]{2,1,0:T(2,128)(2,1)}), bf16[64,2,640]{2,1,0:T(2,128)(2,1)S(1)}, u32[]{:S(2)}, u32[]{:S(2)}) %all-to-all-start.1) | async-done | bytes 163872 | tf_op jit(solution)/shard_map/all_to_all | solution.py:18
  32.8 0.7 slice_reduce_fusion
  36.0 0.7 broadcast_in_dim.31
  36.7 3.7 %all-to-all-start.2 = ((bf16[16,8,1024]{2,1,0:T(8,128)(2,1)}), bf16[16,8,1024]{2,1,0:T(8,128)(2,1)S(1)}, u32[]{:S(2)}, u32[]{:S(2)}) async-start(bf16[16,8,1024]{2,1,0:T(8,128)(2,1)} %broadcast_in_dim.31), calls=%async_computation.2 | async-start | bytes 524288 | tf_op jit(solution)/shard_map/all_to_all | solution.py:18
  40.5 9.9 %collective-permute-done.1 = bf16[128,1024]{1,0:T(8,128)(2,1)S(1)} collective-permute-done((bf16[128,1024]{1,0:T(8,128)(2,1)S(1)}, bf16[128,1024]{1,0:T(8,128)(2,1)S(1)}, u32[]{:S(2)}, u32[]{:S(2)}) %collective-permute-start.1) | collective-permute-done | bytes 262176 | tf_op jit(solution)/shard_map/ppermute | solution.py:28
  50.4 1.5 %collective-permute-done = bf16[128,1024]{1,0:T(8,128)(2,1)S(1)} collective-permute-done((bf16[128,1024]{1,0:T(8,128)(2,1)S(1)}, bf16[128,1024]{1,0:T(8,128)(2,1)S(1)}, u32[]{:S(2)}, u32[]{:S(2)}) %collective-permute-start) | collective-permute-done | bytes 262176 | tf_op jit(solution)/shard_map/ppermute | solution.py:28
  52.0 2.4 %all-to-all-done.2 = bf16[16,8,1024]{2,1,0:T(8,128)(2,1)S(1)} async-done(((bf16[16,8,1024]{2,1,0:T(8,128)(2,1)}), bf16[16,8,1024]{2,1,0:T(8,128)(2,1)S(1)}, u32[]{:S(2)}, u32[]{:S(2)}) %all-to-all-start.2) | async-done | bytes 262176 | tf_op jit(solution)/shard_map/all_to_all | solution.py:18
  54.4 1.5 %fusion.6 = bf16[16,8,1024]{2,1,0:T(8,128)(2,1)} fusion(bf16[64,1024]{1,0:T(8,128)(2,1)S(1)} %get-tuple-element.87, bf16[64,1024]{1,0:T(8,128)(2,1)S(1)} %get-tuple-element.85, bf16[64,1024]{1,0:T(8,128)(2,1)S(1)} %get-tuple-element.83, bf16[64,1024]{1,0:T(8,128)(2,1)S(1)} %copy-done.1, bf16[64,1024]{1,0:T(8,128)(2,1)S(1)} %get-tuple-element.86, ...), kind=kOutput, calls=%fused_computation.13 | convolution fusion | flops 140673024 | bytes 1572864 | tf_op jit(solution)/shard_map/dot_general | solution.py:233
  55.9 4.4 %all-to-all-start.3 = ((bf16[16,8,1024]{2,1,0:T(8,128)(2,1)}), bf16[16,8,1024]{2,1,0:T(8,128)(2,1)S(1)}, u32[]{:S(2)}, u32[]{:S(2)}) async-start(bf16[16,8,1024]{2,1,0:T(8,128)(2,1)} %fusion.6), calls=%async_computation.3 | async-start | bytes 524288 | tf_op jit(solution)/shard_map/all_to_all | solution.py:18
  60.3 2.1 %positions.1 = s32[8,64]{1,0:T(8,128)} custom-call(s32[3,8]{1,0:T(4,128)S(1)} %bitcast.55, s32[8,61]{1,0:T(8,128)S(1)} %get-tuple-element.207, s32[8,61]{1,0:T(8,128)S(1)} %get-tuple-element.207), custom_call_target="tpu_custom_call" | custom-call | tf_op jit(solution)/shard_map/positions/pallas_call | solution.py:168
  62.5 0.8 eq.57
  63.5 5.5 %all-to-all-done.3 = bf16[16,8,1024]{2,1,0:T(8,128)(2,1)S(1)} async-done(((bf16[16,8,1024]{2,1,0:T(8,128)(2,1)}), bf16[16,8,1024]{2,1,0:T(8,128)(2,1)S(1)}, u32[]{:S(2)}, u32[]{:S(2)}) %all-to-all-start.3) | async-done | bytes 262176 | tf_op jit(solution)/shard_map/all_to_all | solution.py:18
  69.9 0.7 copy.45
  70.6 8.6 %all-to-all-start.4 = ((f32[64,1,256]{2,1,0:T(1,128)}), f32[64,1,256]{2,1,0:T(1,128)S(1)}, u32[]{:S(2)}, u32[]{:S(2)}) async-start(f32[64,1,256]{2,1,0:T(1,128)} %copy.45), calls=%async_computation.4 | async-start | bytes 131072 | tf_op jit(solution)/shard_map/all_to_all | solution.py:18
  79.4 10.9 %all-to-all-done.4 = f32[64,1,256]{2,1,0:T(1,128)S(1)} async-done(((f32[64,1,256]{2,1,0:T(1,128)}), f32[64,1,256]{2,1,0:T(1,128)S(1)}, u32[]{:S(2)}, u32[]{:S(2)}) %all-to-all-start.4) | async-done | bytes 65568 | tf_op jit(solution)/shard_map/all_to_all | solution.py:18
  92.1 3.5 %collective-permute-start.3 = (f32[16]{0:T(128)S(1)}, f32[16]{0:T(128)S(1)}, u32[]{:S(2)}, u32[]{:S(2)}) collective-permute-start(f32[16]{0:T(128)S(1)} %multiply_reduce_fusion.3), channel_id=1, source_target_pairs={{0,64},{64,0},{1,65},{65,1},{2,66},{66,2},{3,67},{67,3},{4,68},{68... | collective-permute-start | bytes 200 | tf_op jit(solution)/shard_map/ppermute | solution.py:34
  95.6 0.8 collective-permute-done.3
  96.6 0.6 convert_bitcast_fusion
  97.2 1.7 %collective-permute-done.4 = f32[16]{0:T(128)S(1)} collective-permute-done((f32[16]{0:T(128)S(1)}, f32[16]{0:T(128)S(1)}, u32[]{:S(2)}, u32[]{:S(2)}) %collective-permute-start.4) | collective-permute-done | bytes 96 | tf_op jit(solution)/shard_map/ppermute | solution.py:34
  (63 shorter events, 6.1 us)
Async XLA Ops:
  0.6 34.6 %copy-start = (s32[8,61]{1,0:T(8,128)S(1)}, s32[8,61]{1,0:T(8,128)}, u32[]{:S(2)}) copy-start(s32[8,61]{1,0:T(8,128)} %words_v.1) | copy-start | bytes 5860
  0.6 34.6 %copy-start.5 = (f32[16]{0:T(128)S(1)}, f32[16]{0:T(128)}, u32[]{:S(2)}) copy-start(f32[16]{0:T(128)} %param.18) | copy-start | bytes 196
  0.7 34.6 %copy-start.3 = (s32[8,3]{0,1:T(4,128)S(1)}, s32[8,3]{0,1:T(4,128)}, u32[]{:S(2)}) copy-start(s32[8,3]{0,1:T(4,128)} %param.12) | copy-start | bytes 292
  0.7 34.6 %copy-start.6 = (f32[16]{0:T(128)S(1)}, f32[16]{0:T(128)}, u32[]{:S(2)}) copy-start(f32[16]{0:T(128)} %param.19) | copy-start | bytes 196
  0.7 20.5 %copy-start.1 = (bf16[64,1024]{1,0:T(8,128)(2,1)S(1)}, bf16[64,1024]{1,0:T(8,128)(2,1)}, u32[]{:S(2)}) copy-start(bf16[64,1024]{1,0:T(8,128)(2,1)} %param.17) | copy-start | bytes 393220
  0.7 20.5 %copy-start.2 = (bf16[1024,64]{0,1:T(8,128)(2,1)S(1)}, bf16[1024,64]{0,1:T(8,128)(2,1)}, u32[]{:S(2)}) copy-start(bf16[1024,64]{0,1:T(8,128)(2,1)} %param.16) | copy-start | bytes 393220
  5.8 27.0 %all-to-all-start.1 = ((bf16[64,2,640]{2,1,0:T(2,128)(2,1)}), bf16[64,2,640]{2,1,0:T(2,128)(2,1)S(1)}, u32[]{:S(2)}, u32[]{:S(2)}) async-start(bf16[64,2,640]{2,1,0:T(2,128)(2,1)} %send_rows.2), calls=%async_computation.1 | async-start | bytes 327680 | tf_op jit(solution)/shard_map/all_to_all | solution.py:18
  21.2 19.3 %collective-permute-start.2 = (bf16[128,1024]{1,0:T(8,128)(2,1)S(1)}, bf16[128,1024]{1,0:T(8,128)(2,1)S(1)}, u32[]{:S(2)}, u32[]{:S(2)}) collective-permute-start(bf16[128,1024]{1,0:T(8,128)(2,1)S(1)} %pad_maximum_fusion), channel_id=1, source_target_pairs={{24,0},{0,8},{8,16},{16,24},{25,1},{1,9},{9,17},{17,25},{26,2},{2,... | collective-permute-start | bytes 786440 | tf_op jit(solution)/shard_map/ppermute | solution.py:28
  23.2 27.2 %collective-permute-start.1 = (bf16[128,1024]{1,0:T(8,128)(2,1)S(1)}, bf16[128,1024]{1,0:T(8,128)(2,1)S(1)}, u32[]{:S(2)}, u32[]{:S(2)}) collective-permute-start(bf16[128,1024]{1,0:T(8,128)(2,1)S(1)} %pad_maximum_fusion), channel_id=1, source_target_pairs={{16,0},{24,8},{0,16},{8,24},{17,1},{25,9},{1,17},{9,25},{18,2},{26... | collective-permute-start | bytes 786440 | tf_op jit(solution)/shard_map/ppermute | solution.py:28
  26.5 25.5 %collective-permute-start = (bf16[128,1024]{1,0:T(8,128)(2,1)S(1)}, bf16[128,1024]{1,0:T(8,128)(2,1)S(1)}, u32[]{:S(2)}, u32[]{:S(2)}) collective-permute-start(bf16[128,1024]{1,0:T(8,128)(2,1)S(1)} %pad_maximum_fusion), channel_id=1, source_target_pairs={{8,0},{16,8},{24,16},{0,24},{9,1},{17,9},{25,17},{1,25},{10,2},{18... | collective-permute-start | bytes 786440 | tf_op jit(solution)/shard_map/ppermute | solution.py:28
  35.3 0.7 copy-start.4
  36.7 17.6 %all-to-all-start.2 = ((bf16[16,8,1024]{2,1,0:T(8,128)(2,1)}), bf16[16,8,1024]{2,1,0:T(8,128)(2,1)S(1)}, u32[]{:S(2)}, u32[]{:S(2)}) async-start(bf16[16,8,1024]{2,1,0:T(8,128)(2,1)} %broadcast_in_dim.31), calls=%async_computation.2 | async-start | bytes 524288 | tf_op jit(solution)/shard_map/all_to_all | solution.py:18
  54.4 37.1 %copy-start.7 = (s32[8]{0:T(128)S(1)}, s32[8]{0:T(128)}, u32[]{:S(2)}) copy-start(s32[8]{0:T(128)} %param.14) | copy-start | bytes 100
  55.9 13.1 %all-to-all-start.3 = ((bf16[16,8,1024]{2,1,0:T(8,128)(2,1)}), bf16[16,8,1024]{2,1,0:T(8,128)(2,1)S(1)}, u32[]{:S(2)}, u32[]{:S(2)}) async-start(bf16[16,8,1024]{2,1,0:T(8,128)(2,1)} %fusion.6), calls=%async_computation.3 | async-start | bytes 524288 | tf_op jit(solution)/shard_map/all_to_all | solution.py:18
  70.6 19.7 %all-to-all-start.4 = ((f32[64,1,256]{2,1,0:T(1,128)}), f32[64,1,256]{2,1,0:T(1,128)S(1)}, u32[]{:S(2)}, u32[]{:S(2)}) async-start(f32[64,1,256]{2,1,0:T(1,128)} %copy.45), calls=%async_computation.4 | async-start | bytes 131072 | tf_op jit(solution)/shard_map/all_to_all | solution.py:18
  92.1 4.3 %collective-permute-start.3 = (f32[16]{0:T(128)S(1)}, f32[16]{0:T(128)S(1)}, u32[]{:S(2)}, u32[]{:S(2)}) collective-permute-start(f32[16]{0:T(128)S(1)} %multiply_reduce_fusion.3), channel_id=1, source_target_pairs={{0,64},{64,0},{1,65},{65,1},{2,66},{66,2},{3,67},{67,3},{4,68},{68... | collective-permute-start | bytes 200 | tf_op jit(solution)/shard_map/ppermute | solution.py:34
  96.5 2.4 %collective-permute-start.4 = (f32[16]{0:T(128)S(1)}, f32[16]{0:T(128)S(1)}, u32[]{:S(2)}, u32[]{:S(2)}) collective-permute-start(f32[16]{0:T(128)S(1)} %add.58), channel_id=1, source_target_pairs={{0,128},{128,0},{1,129},{129,1},{2,130},{130,2},{3,131},{131,3},{4... | collective-permute-start | bytes 200 | tf_op jit(solution)/shard_map/ppermute | solution.py:34

commit v8 on v7

--- a/solution.py
+++ b/solution.py
@@ -24,7 +24,7 @@
 
 def from_column(array, axis):
     peers = lax.axis_size(axis)
-    return [array] + [
+    return [
         lax.ppermute(array, axis, [((i + step) % peers, i) for i in range(peers)])
         for step in range(1, peers)
     ]
@@ -35,14 +35,14 @@
 
 
 def send_kernel(
-    peers, where_ref, triples, words, gain, weight, table, sent, tiles, lanes, rows, held, sems
+    peers, place_ref, trip_ref, triples, words, gain, weight, table, sent, tiles, lanes, rows, held, sems
 ):
     lead, n_triples = triples.shape
     seq_len = lead + words.shape[1]
     entries, width = table.shape
     half = width // 2
-    low = where_ref[0] * entries
-    skipped = where_ref[1] * peers
+    low = place_ref[0] * entries
+    skipped = trip_ref[0] * peers
     group = 8
 
     def copy(number, local):
@@ -125,7 +125,7 @@
     return pl.pallas_call(
         functools.partial(send_kernel, peers),
         out_shape=jax.ShapeDtypeStruct((peers, 2, width // 2 + LANES), table.dtype),
-        in_specs=[smem] * 3 + [vmem] * 2 + [pl.BlockSpec(memory_space=pl.ANY)],
+        in_specs=[smem] * 4 + [vmem] * 2 + [pl.BlockSpec(memory_space=pl.ANY)],
         out_specs=vmem,
         scratch_shapes=[
             pltpu.VMEM((peers, 8, width), table.dtype),
@@ -135,7 +135,7 @@
             pltpu.SemaphoreType.DMA((peers,)),
         ],
         name="send_rows",
-    )(jnp.stack([place, trip]), triples.T, words, gain, weight, table)
+    )(place.reshape(1), trip.reshape(1), triples.T, words, gain, weight, table)
 
 
 def position_kernel(entries, triples, words, words_v, spot_ref, ids_ref):
@@ -194,10 +194,11 @@
     slots = toks // peers
     share = width // peers
 
-    units = up_weight.shape[1]
-    weights = from_column(jnp.concatenate([up_weight.T, down_weight], axis=0), "zh")
-    up_rows = jnp.concatenate([w[:units] for w in weights], axis=0)
-    down_rows = jnp.concatenate([w[units:] for w in weights], axis=0)
+    units = up_weight.shape[1] // lax.axis_size("core")
+    start = lax.axis_index("core") * units
+    up_part = lax.dynamic_slice_in_dim(up_weight.T, start, units, 0)
+    down_part = lax.dynamic_slice_in_dim(down_weight, start, units, 0)
+    came = from_column(jnp.concatenate([up_part, down_part], axis=0), "zh")
 
     gains = out_gain.reshape(1, -1), class_weight.reshape(1, -1)
 
@@ -215,6 +216,11 @@
 
     got = rows_of(jnp.int32(0))
     trips = jnp.max(got[:, 1, half + 1].astype(f32)).astype(jnp.int32)
+    came = jnp.where(trips <= toks, jnp.stack(came), 0)
+    came = jnp.concatenate([came, swapped(came, "core")], axis=0)
+    up_rows = jnp.concatenate([up_weight.T, came[:, :units].reshape(-1, width)], axis=0)
+    down_rows = jnp.concatenate([down_weight, came[:, units:].reshape(-1, width)], axis=0)
+
     score_weight = got[:, 0, half : half + 3 * share].astype(f32).reshape(peers, 3, share)
     score_weight = jnp.sum(score_weight, axis=1).reshape(1, width)
 

time: 99.9 us -> 102 us (1.021)
  waiting for transfers between devices: 35.8 us -> 37.8 us
    all_to_all x4, waiting for transfers between devices: 21.9 us -> 28.9 us  [exchange(): return lax.all_to_all(blocks, axes, split_axis=0, concat_axis=0, tiled=True)]
    ppermute x3, waiting for transfers between devices: 11.4 us -> 6.56 us  [from_column(): lax.ppermute(array, axis, [((i + step) % peers, i) for i in range(peers)])]
    ppermute x2 -> x3, starting transfers between devices: 3.63 us -> 4.65 us  [swapped(): return lax.ppermute(array, axis, [(0, 1), (1, 0)])]
    ppermute x2 -> x3, waiting for transfers between devices: 2.49 us -> 2.28 us  [swapped(): return lax.ppermute(array, axis, [(0, 1), (1, 0)])]
  transfers between devices with their start and end apart: 9 -> 10, of which waited for: 8 -> 8; matrix products, arithmetic and copies ran while one was open for 5% -> 5% of each run, Pallas kernels for 2% -> 2%
where the time goes in v8:
time: 102 us
  starting transfers between devices  44.9 us (44%)
  waiting for transfers between devices  37.8 us (37%)
  Pallas kernels  6.95 us (7%)
  other arithmetic  4.47 us (4%)
  local copies, waits for them, and re-layouts  3.97 us (4%)
  matrix products  2.08 us (2%)
  between operations  1.59 us (2%)
    all_to_all x4, starting transfers between devices, exchange(): return lax.all_to_all(blocks, axes, split_axis=0, concat_axis=0, tiled=True)  31.7 us
    all_to_all x4, waiting for transfers between devices, exchange(): return lax.all_to_all(blocks, axes, split_axis=0, concat_axis=0, tiled=True)  28.9 us
    ppermute x3, starting transfers between devices, from_column(): lax.ppermute(array, axis, [((i + step) % peers, i) for i in range(peers)])  8.58 us
    ppermute x3, waiting for transfers between devices, from_column(): lax.ppermute(array, axis, [((i + step) % peers, i) for i in range(peers)])  6.56 us
    pallas_call x1, Pallas kernels, to_send(): pl.pallas_call(functools.partial(send_kernel, peers), out_shape=jax.Shape...  4.8 us
    ppermute x3, starting transfers between devices, swapped(): return lax.ppermute(array, axis, [(0, 1), (1, 0)])  4.65 us
    ppermute x3, waiting for transfers between devices, swapped(): return lax.ppermute(array, axis, [(0, 1), (1, 0)])  2.28 us
    pallas_call x1, Pallas kernels, positions(): pl.pallas_call(functools.partial(position_kernel, entries), out_shape=jax...  2.15 us
  transfers between devices with their start and end apart: 10, of which 8 were waited for; matrix products, arithmetic and copies ran while one was open for 5% of the time, Pallas kernels for 2%

profile of v8, /device:TPU:1, one launch (start us, length us, event | category | flops | bytes accessed | tf_op | source)
XLA Modules:
  0.0 101.7 jit_solution(2680716546715823532)
XLA Ops:
  0.7 4.8 %send_rows.2 = bf16[64,2,640]{2,1,0:T(2,128)(2,1)} custom-call(s32[1]{0:T(128)} %bitcast.3.place_ref, s32[1]{0:T(128)} %constant.35.clone.1.trip_ref, s32[3,8]{1,0:T(4,128)} %bitcast.63, s32[8,61]{1,0:T(8,128)} %words_v.1, f32[1,16]{1,0:T(1,128)} %bitcast.68, f32[1,16]{1,0:T(1,128)} %bitcast.71, bf16[2048,1024]{1,0:T(8,128)(2,1)} %table.1), custom_call_target="tpu_custom_call" | custom-call | tf_op jit(solution)/shard_map/send_rows/pallas_call | solution.py:125
  5.5 15.1 %all-to-all-start.1 = ((bf16[64,2,640]{2,1,0:T(2,128)(2,1)}), bf16[64,2,640]{2,1,0:T(2,128)(2,1)S(1)}, u32[]{:S(2)}, u32[]{:S(2)}) async-start(bf16[64,2,640]{2,1,0:T(2,128)(2,1)} %send_rows.2), calls=%async_computation.1 | async-start | bytes 327680 | tf_op jit(solution)/shard_map/all_to_all | solution.py:18
  20.7 2.0 %collective-permute-start.2 = (bf16[64,1024]{1,0:T(8,128)(2,1)S(1)}, bf16[64,1024]{1,0:T(8,128)(2,1)S(1)}, u32[]{:S(2)}, u32[]{:S(2)}) collective-permute-start(bf16[64,1024]{1,0:T(8,128)(2,1)S(1)} %pad_maximum_fusion.1), channel_id=1, source_target_pairs={{24,0},{0,8},{8,16},{16,24},{25,1},{1,9},{9,17},{17,25},{26,2},{2,... | collective-permute-start | bytes 393224 | tf_op jit(solution)/shard_map/ppermute | solution.py:28
  22.7 3.3 %collective-permute-start.1 = (bf16[64,1024]{1,0:T(8,128)(2,1)S(1)}, bf16[64,1024]{1,0:T(8,128)(2,1)S(1)}, u32[]{:S(2)}, u32[]{:S(2)}) collective-permute-start(bf16[64,1024]{1,0:T(8,128)(2,1)S(1)} %pad_maximum_fusion.1), channel_id=1, source_target_pairs={{16,0},{24,8},{0,16},{8,24},{17,1},{25,9},{1,17},{9,25},{18,2},{26... | collective-permute-start | bytes 393224 | tf_op jit(solution)/shard_map/ppermute | solution.py:28
  26.0 3.3 %collective-permute-start = (bf16[64,1024]{1,0:T(8,128)(2,1)S(1)}, bf16[64,1024]{1,0:T(8,128)(2,1)S(1)}, u32[]{:S(2)}, u32[]{:S(2)}) collective-permute-start(bf16[64,1024]{1,0:T(8,128)(2,1)S(1)} %pad_maximum_fusion.1), channel_id=1, source_target_pairs={{8,0},{16,8},{24,16},{0,24},{9,1},{17,9},{25,17},{1,25},{10,2},{18... | collective-permute-start | bytes 393224 | tf_op jit(solution)/shard_map/ppermute | solution.py:28
  29.3 3.0 %all-to-all-done.1 = bf16[64,2,640]{2,1,0:T(2,128)(2,1)S(1)} async-done(((bf16[64,2,640]{2,1,0:T(2,128)(2,1)}), bf16[64,2,640]{2,1,0:T(2,128)(2,1)S(1)}, u32[]{:S(2)}, u32[]{:S(2)}) %all-to-all-start.1) | async-done | bytes 163872 | tf_op jit(solution)/shard_map/all_to_all | solution.py:18
  32.3 0.7 slice_reduce_fusion
  33.7 5.3 %collective-permute-done.1 = bf16[64,1024]{1,0:T(8,128)(2,1)S(1)} collective-permute-done((bf16[64,1024]{1,0:T(8,128)(2,1)S(1)}, bf16[64,1024]{1,0:T(8,128)(2,1)S(1)}, u32[]{:S(2)}, u32[]{:S(2)}) %collective-permute-start.1) | collective-permute-done | bytes 131104 | tf_op jit(solution)/shard_map/ppermute | solution.py:28
  39.0 1.3 %collective-permute-done = bf16[64,1024]{1,0:T(8,128)(2,1)S(1)} collective-permute-done((bf16[64,1024]{1,0:T(8,128)(2,1)S(1)}, bf16[64,1024]{1,0:T(8,128)(2,1)S(1)}, u32[]{:S(2)}, u32[]{:S(2)}) %collective-permute-start) | collective-permute-done | bytes 131104 | tf_op jit(solution)/shard_map/ppermute | solution.py:28
  40.3 0.7 collective-permute-start.3
  42.8 0.7 broadcast_in_dim.49
  43.5 6.6 %all-to-all-start.2 = ((bf16[16,8,1024]{2,1,0:T(8,128)(2,1)}), bf16[16,8,1024]{2,1,0:T(8,128)(2,1)S(1)}, u32[]{:S(2)}, u32[]{:S(2)}) async-start(bf16[16,8,1024]{2,1,0:T(8,128)(2,1)} %broadcast_in_dim.49), calls=%async_computation.2 | async-start | bytes 524288 | tf_op jit(solution)/shard_map/all_to_all | solution.py:18
  50.2 9.4 %all-to-all-done.2 = bf16[16,8,1024]{2,1,0:T(8,128)(2,1)S(1)} async-done(((bf16[16,8,1024]{2,1,0:T(8,128)(2,1)}), bf16[16,8,1024]{2,1,0:T(8,128)(2,1)S(1)}, u32[]{:S(2)}, u32[]{:S(2)}) %all-to-all-start.2) | async-done | bytes 262176 | tf_op jit(solution)/shard_map/all_to_all | solution.py:18
  59.6 1.5 %fusion.6 = bf16[16,8,1024]{2,1,0:T(8,128)(2,1)} fusion(bf16[192,1024]{1,0:T(8,128)(2,1)S(1)} %bitcast.56, bf16[64,1024]{1,0:T(8,128)(2,1)S(1)} %copy-done.3, bf16[192,1024]{1,0:T(8,128)(2,1)S(1)} %bitcast.55, bf16[64,1024]{1,0:T(8,128)(2,1)S(1)} %bitcast.67, bf16[16,8,1024]{2,1,0:T(8,128)(2,1)S(1)} %all-to-all-done.2), kind=kOutput, calls=%fused_computation.12 | convolution fusion | flops 138575872 | bytes 1572864 | tf_op jit(solution)/shard_map/dot_general | solution.py:239
  61.1 3.5 %all-to-all-start.3 = ((bf16[16,8,1024]{2,1,0:T(8,128)(2,1)}), bf16[16,8,1024]{2,1,0:T(8,128)(2,1)S(1)}, u32[]{:S(2)}, u32[]{:S(2)}) async-start(bf16[16,8,1024]{2,1,0:T(8,128)(2,1)} %fusion.6), calls=%async_computation.3 | async-start | bytes 524288 | tf_op jit(solution)/shard_map/all_to_all | solution.py:18
  64.7 2.1 %positions.1 = s32[8,64]{1,0:T(8,128)} custom-call(s32[3,8]{1,0:T(4,128)S(1)} %bitcast.65, s32[8,61]{1,0:T(8,128)S(1)} %get-tuple-element.199, s32[8,61]{1,0:T(8,128)S(1)} %get-tuple-element.199), custom_call_target="tpu_custom_call" | custom-call | tf_op jit(solution)/shard_map/positions/pallas_call | solution.py:168
  66.8 0.8 eq.57
  67.9 5.6 %all-to-all-done.3 = bf16[16,8,1024]{2,1,0:T(8,128)(2,1)S(1)} async-done(((bf16[16,8,1024]{2,1,0:T(8,128)(2,1)}), bf16[16,8,1024]{2,1,0:T(8,128)(2,1)S(1)}, u32[]{:S(2)}, u32[]{:S(2)}) %all-to-all-start.3) | async-done | bytes 262176 | tf_op jit(solution)/shard_map/all_to_all | solution.py:18
  74.3 0.7 copy.45
  75.0 6.4 %all-to-all-start.4 = ((f32[64,1,256]{2,1,0:T(1,128)}), f32[64,1,256]{2,1,0:T(1,128)S(1)}, u32[]{:S(2)}, u32[]{:S(2)}) async-start(f32[64,1,256]{2,1,0:T(1,128)} %copy.45), calls=%async_computation.4 | async-start | bytes 131072 | tf_op jit(solution)/shard_map/all_to_all | solution.py:18
  81.6 10.9 %all-to-all-done.4 = f32[64,1,256]{2,1,0:T(1,128)S(1)} async-done(((f32[64,1,256]{2,1,0:T(1,128)}), f32[64,1,256]{2,1,0:T(1,128)S(1)}, u32[]{:S(2)}, u32[]{:S(2)}) %all-to-all-start.4) | async-done | bytes 65568 | tf_op jit(solution)/shard_map/all_to_all | solution.py:18
  94.3 3.7 %collective-permute-start.4 = (f32[16]{0:T(128)S(1)}, f32[16]{0:T(128)S(1)}, u32[]{:S(2)}, u32[]{:S(2)}) collective-permute-start(f32[16]{0:T(128)S(1)} %multiply_reduce_fusion.3), channel_id=1, source_target_pairs={{0,64},{64,0},{1,65},{65,1},{2,66},{66,2},{3,67},{67,3},{4,68},{68... | collective-permute-start | bytes 200 | tf_op jit(solution)/shard_map/ppermute | solution.py:34
  98.0 0.8 collective-permute-done.4
  99.8 1.5 %collective-permute-done.5 = f32[16]{0:T(128)S(1)} collective-permute-done((f32[16]{0:T(128)S(1)}, f32[16]{0:T(128)S(1)}, u32[]{:S(2)}, u32[]{:S(2)}) %collective-permute-start.5) | collective-permute-done | bytes 96 | tf_op jit(solution)/shard_map/ppermute | solution.py:34
  (65 shorter events, 6.4 us)
Async XLA Ops:
  0.6 41.4 %copy-start.1 = (s32[8,3]{0,1:T(4,128)S(1)}, s32[8,3]{0,1:T(4,128)}, u32[]{:S(2)}) copy-start(s32[8,3]{0,1:T(4,128)} %param.12) | copy-start | bytes 292
  0.6 41.3 %copy-start = (s32[8,61]{1,0:T(8,128)S(1)}, s32[8,61]{1,0:T(8,128)}, u32[]{:S(2)}) copy-start(s32[8,61]{1,0:T(8,128)} %words_v.1) | copy-start | bytes 5860
  0.7 41.3 %copy-start.5 = (f32[16]{0:T(128)S(1)}, f32[16]{0:T(128)}, u32[]{:S(2)}) copy-start(f32[16]{0:T(128)} %param.18) | copy-start | bytes 196
  0.7 41.3 %copy-start.6 = (f32[16]{0:T(128)S(1)}, f32[16]{0:T(128)}, u32[]{:S(2)}) copy-start(f32[16]{0:T(128)} %param.19) | copy-start | bytes 196
  0.7 20.0 %copy-start.3 = (bf16[64,1024]{1,0:T(8,128)(2,1)S(1)}, bf16[64,1024]{1,0:T(8,128)(2,1)}, u32[]{:S(2)}) copy-start(bf16[64,1024]{1,0:T(8,128)(2,1)} %param.17) | copy-start | bytes 393220
  0.7 20.0 %copy-start.4 = (bf16[1024,64]{0,1:T(8,128)(2,1)S(1)}, bf16[1024,64]{0,1:T(8,128)(2,1)}, u32[]{:S(2)}) copy-start(bf16[1024,64]{0,1:T(8,128)(2,1)} %param.16) | copy-start | bytes 393220
  5.5 26.8 %all-to-all-start.1 = ((bf16[64,2,640]{2,1,0:T(2,128)(2,1)}), bf16[64,2,640]{2,1,0:T(2,128)(2,1)S(1)}, u32[]{:S(2)}, u32[]{:S(2)}) async-start(bf16[64,2,640]{2,1,0:T(2,128)(2,1)} %send_rows.2), calls=%async_computation.1 | async-start | bytes 327680 | tf_op jit(solution)/shard_map/all_to_all | solution.py:18
  20.7 13.0 %collective-permute-start.2 = (bf16[64,1024]{1,0:T(8,128)(2,1)S(1)}, bf16[64,1024]{1,0:T(8,128)(2,1)S(1)}, u32[]{:S(2)}, u32[]{:S(2)}) collective-permute-start(bf16[64,1024]{1,0:T(8,128)(2,1)S(1)} %pad_maximum_fusion.1), channel_id=1, source_target_pairs={{24,0},{0,8},{8,16},{16,24},{25,1},{1,9},{9,17},{17,25},{26,2},{2,... | collective-permute-start | bytes 393224 | tf_op jit(solution)/shard_map/ppermute | solution.py:28
  22.7 16.3 %collective-permute-start.1 = (bf16[64,1024]{1,0:T(8,128)(2,1)S(1)}, bf16[64,1024]{1,0:T(8,128)(2,1)S(1)}, u32[]{:S(2)}, u32[]{:S(2)}) collective-permute-start(bf16[64,1024]{1,0:T(8,128)(2,1)S(1)} %pad_maximum_fusion.1), channel_id=1, source_target_pairs={{16,0},{24,8},{0,16},{8,24},{17,1},{25,9},{1,17},{9,25},{18,2},{26... | collective-permute-start | bytes 393224 | tf_op jit(solution)/shard_map/ppermute | solution.py:28
  26.0 14.2 %collective-permute-start = (bf16[64,1024]{1,0:T(8,128)(2,1)S(1)}, bf16[64,1024]{1,0:T(8,128)(2,1)S(1)}, u32[]{:S(2)}, u32[]{:S(2)}) collective-permute-start(bf16[64,1024]{1,0:T(8,128)(2,1)S(1)} %pad_maximum_fusion.1), channel_id=1, source_target_pairs={{8,0},{16,8},{24,16},{0,24},{9,1},{17,9},{25,17},{1,25},{10,2},{18... | collective-permute-start | bytes 393224 | tf_op jit(solution)/shard_map/ppermute | solution.py:28
  40.3 9.8 %collective-permute-start.3 = (bf16[3,64,1024]{2,1,0:T(8,128)(2,1)S(1)}, bf16[3,64,1024]{2,1,0:T(8,128)(2,1)S(1)}, u32[]{:S(2)}, u32[]{:S(2)}) collective-permute-start(bf16[3,64,1024]{2,1,0:T(8,128)(2,1)S(1)} %maximum_select_fusion), channel_id=1, source_target_pairs={{0,64},{64,0},{1,65},{65,1},{2,66},{66,2},{3,67},{67,3},{4,68},{68... | collective-permute-start | bytes 1179656 | tf_op jit(solution)/shard_map/ppermute | solution.py:34
  42.0 0.7 copy-start.2
  43.5 16.1 %all-to-all-start.2 = ((bf16[16,8,1024]{2,1,0:T(8,128)(2,1)}), bf16[16,8,1024]{2,1,0:T(8,128)(2,1)S(1)}, u32[]{:S(2)}, u32[]{:S(2)}) async-start(bf16[16,8,1024]{2,1,0:T(8,128)(2,1)} %broadcast_in_dim.49), calls=%async_computation.2 | async-start | bytes 524288 | tf_op jit(solution)/shard_map/all_to_all | solution.py:18
  59.6 34.1 %copy-start.7 = (s32[8]{0:T(128)S(1)}, s32[8]{0:T(128)}, u32[]{:S(2)}) copy-start(s32[8]{0:T(128)} %param.14) | copy-start | bytes 100
  61.1 12.4 %all-to-all-start.3 = ((bf16[16,8,1024]{2,1,0:T(8,128)(2,1)}), bf16[16,8,1024]{2,1,0:T(8,128)(2,1)S(1)}, u32[]{:S(2)}, u32[]{:S(2)}) async-start(bf16[16,8,1024]{2,1,0:T(8,128)(2,1)} %fusion.6), calls=%async_computation.3 | async-start | bytes 524288 | tf_op jit(solution)/shard_map/all_to_all | solution.py:18
  75.0 17.5 %all-to-all-start.4 = ((f32[64,1,256]{2,1,0:T(1,128)}), f32[64,1,256]{2,1,0:T(1,128)S(1)}, u32[]{:S(2)}, u32[]{:S(2)}) async-start(f32[64,1,256]{2,1,0:T(1,128)} %copy.45), calls=%async_computation.4 | async-start | bytes 131072 | tf_op jit(solution)/shard_map/all_to_all | solution.py:18
  94.3 4.5 %collective-permute-start.4 = (f32[16]{0:T(128)S(1)}, f32[16]{0:T(128)S(1)}, u32[]{:S(2)}, u32[]{:S(2)}) collective-permute-start(f32[16]{0:T(128)S(1)} %multiply_reduce_fusion.3), channel_id=1, source_target_pairs={{0,64},{64,0},{1,65},{65,1},{2,66},{66,2},{3,67},{67,3},{4,68},{68... | collective-permute-start | bytes 200 | tf_op jit(solution)/shard_map/ppermute | solution.py:34
  98.8 2.4 %collective-permute-start.5 = (f32[16]{0:T(128)S(1)}, f32[16]{0:T(128)S(1)}, u32[]{:S(2)}, u32[]{:S(2)}) collective-permute-start(f32[16]{0:T(128)S(1)} %add.63), channel_id=1, source_target_pairs={{0,128},{128,0},{1,129},{129,1},{2,130},{130,2},{3,131},{131,3},{4... | collective-permute-start | bytes 200 | tf_op jit(solution)/shard_map/ppermute | solution.py:34

commit v9 on v8

--- a/solution.py
+++ b/solution.py
@@ -22,12 +22,9 @@
     return exchange(jnp.broadcast_to(array, (lax.axis_size(axes), *array.shape)), axes)
 
 
-def from_column(array, axis):
+def moved(array, axis, step):
     peers = lax.axis_size(axis)
-    return [
-        lax.ppermute(array, axis, [((i + step) % peers, i) for i in range(peers)])
-        for step in range(1, peers)
-    ]
+    return lax.ppermute(array, axis, [((i + step) % peers, i) for i in range(peers)])
 
 
 def swapped(array, axis):
@@ -194,11 +191,21 @@
     slots = toks // peers
     share = width // peers
 
-    units = up_weight.shape[1] // lax.axis_size("core")
-    start = lax.axis_index("core") * units
-    up_part = lax.dynamic_slice_in_dim(up_weight.T, start, units, 0)
-    down_part = lax.dynamic_slice_in_dim(down_weight, start, units, 0)
-    came = from_column(jnp.concatenate([up_part, down_part], axis=0), "zh")
+    units = up_weight.shape[1]
+    half_units = units // lax.axis_size("core")
+    start = lax.axis_index("core") * half_units
+    up_half = lax.dynamic_slice_in_dim(up_weight.T, start, half_units, 0)
+    down_half = lax.dynamic_slice_in_dim(down_weight, start, half_units, 0)
+    own = jnp.concatenate([up_weight.T, down_weight], axis=0)
+    far = moved(jnp.concatenate([up_half, down_half], axis=0), "zh", 2)
+    weights = [own, moved(own, "zh", 1), moved(own, "zh", 3)]
+    halves = [far, swapped(far, "core")]
+    up_rows = jnp.concatenate(
+        [w[:units] for w in weights] + [h[:half_units] for h in halves], axis=0
+    )
+    down_rows = jnp.concatenate(
+        [w[units:] for w in weights] + [h[half_units:] for h in halves], axis=0
+    )
 
     gains = out_gain.reshape(1, -1), class_weight.reshape(1, -1)
 
@@ -216,11 +223,6 @@
 
     got = rows_of(jnp.int32(0))
     trips = jnp.max(got[:, 1, half + 1].astype(f32)).astype(jnp.int32)
-    came = jnp.where(trips <= toks, jnp.stack(came), 0)
-    came = jnp.concatenate([came, swapped(came, "core")], axis=0)
-    up_rows = jnp.concatenate([up_weight.T, came[:, :units].reshape(-1, width)], axis=0)
-    down_rows = jnp.concatenate([down_weight, came[:, units:].reshape(-1, width)], axis=0)
-
     score_weight = got[:, 0, half : half + 3 * share].astype(f32).reshape(peers, 3, share)
     score_weight = jnp.sum(score_weight, axis=1).reshape(1, width)
 

time: 102 us -> 100 us (0.980)
  starting transfers between devices: 44.9 us -> 40.6 us
  local copies, waits for them, and re-layouts: 3.97 us -> 5.72 us
    all_to_all x4, starting transfers between devices: 31.7 us -> 22.5 us  [exchange(): return lax.all_to_all(blocks, axes, split_axis=0, concat_axis=0, tiled=True)]
    ppermute x3, waiting for transfers between devices: 6.56 us -> 0.01 us  [moved(): lax.ppermute(array, axis, [((i + step) % peers, i) for i in range(peers)])]
    all_to_all x4, waiting for transfers between devices: 28.9 us -> 35.1 us  [exchange(): return lax.all_to_all(blocks, axes, split_axis=0, concat_axis=0, tiled=True)]
    ppermute x3, starting transfers between devices: 4.65 us -> 7.8 us  [swapped(): return lax.ppermute(array, axis, [(0, 1), (1, 0)])]
    ppermute x3, starting transfers between devices: 8.58 us -> 10.3 us  [moved(): lax.ppermute(array, axis, [((i + step) % peers, i) for i in range(peers)])]
    dynamic_slice x2, local copies, waits for them, and re-layouts: 0.03 us -> 1.69 us  [the longest x1 0.84 us: on_device(): down_half = lax.dynamic_slice_in_dim(down_weight, start, half_units, 0)]
    concatenate x2, other arithmetic: 0.06 us -> 1.11 us  [the longest x1 1.1 us: on_device(): own = jnp.concatenate([up_weight.T, down_weight], axis=0)]
  transfers between devices with their start and end apart: 10 -> 10, of which waited for: 8 -> 6; matrix products, arithmetic and copies ran while one was open for 5% -> 6% of each run, Pallas kernels for 2% -> 6%
where the time goes in v9:
time: 100 us; the launch traced here: 99.4 us
  starting transfers between devices  40.6 us (41%)
  waiting for transfers between devices  37.5 us (38%)
  Pallas kernels  6.44 us (6%)
  local copies, waits for them, and re-layouts  5.72 us (6%)
  other arithmetic  5.47 us (5%)
  matrix products  2.09 us (2%)
  between operations  1.6 us (2%)
    all_to_all x4, waiting for transfers between devices, exchange(): return lax.all_to_all(blocks, axes, split_axis=0, concat_axis=0, tiled=True)  35.1 us
    all_to_all x4, starting transfers between devices, exchange(): return lax.all_to_all(blocks, axes, split_axis=0, concat_axis=0, tiled=True)  22.5 us
    ppermute x3, starting transfers between devices, moved(): lax.ppermute(array, axis, [((i + step) % peers, i) for i in range(peers)])  10.3 us
    ppermute x3, starting transfers between devices, swapped(): return lax.ppermute(array, axis, [(0, 1), (1, 0)])  7.8 us
    pallas_call x1, Pallas kernels, to_send(): pl.pallas_call(functools.partial(send_kernel, peers), out_shape=jax.Shape...  4.29 us
    ppermute x3, waiting for transfers between devices, swapped(): return lax.ppermute(array, axis, [(0, 1), (1, 0)])  2.35 us
    pallas_call x1, Pallas kernels, positions(): pl.pallas_call(functools.partial(position_kernel, entries), out_shape=jax...  2.15 us
  transfers between devices with their start and end apart: 10, of which 6 were waited for; matrix products, arithmetic and copies ran while one was open for 6% of the time, Pallas kernels for 6%

profile of v9, /device:TPU:1, one launch (start us, length us, event | category | flops | bytes accessed | tf_op | source)
XLA Modules:
  0.0 99.4 jit_solution(7204747067007316170)
XLA Ops:
  0.7 1.1 %pad_maximum_fusion = bf16[128,1024]{1,0:T(8,128)(2,1)S(1)} fusion(bf16[64,1024]{1,0:T(8,128)(2,1)} %param.17, bf16[64,1024]{1,0:T(8,128)(2,1)} %bitcast.53), kind=kLoop, calls=%fused_computation.18 | loop fusion | flops 524288 | bytes 524288 | tf_op jit(solution)/shard_map/concatenate | solution.py:199
  1.8 6.9 %collective-permute-start = (bf16[128,1024]{1,0:T(8,128)(2,1)S(1)}, bf16[128,1024]{1,0:T(8,128)(2,1)S(1)}, u32[]{:S(2)}, u32[]{:S(2)}) collective-permute-start(bf16[128,1024]{1,0:T(8,128)(2,1)S(1)} %pad_maximum_fusion), channel_id=1, source_target_pairs={{8,0},{16,8},{24,16},{0,24},{9,1},{17,9},{25,17},{1,25},{10,2},{18... | collective-permute-start | bytes 786440 | tf_op jit(solution)/shard_map/ppermute | solution.py:27
  8.7 0.8 constant_dynamic-slice_fusion
  9.6 0.8 dynamic-slice_bitcast_fusion
  10.4 3.3 %collective-permute-start.2 = (bf16[64,1024]{1,0:T(8,128)(2,1)S(1)}, bf16[64,1024]{1,0:T(8,128)(2,1)S(1)}, u32[]{:S(2)}, u32[]{:S(2)}) collective-permute-start(bf16[64,1024]{1,0:T(8,128)(2,1)S(1)} %pad_maximum_fusion.1), channel_id=1, source_target_pairs={{16,0},{24,8},{0,16},{8,24},{17,1},{25,9},{1,17},{9,25},{18,2},{26... | collective-permute-start | bytes 393224 | tf_op jit(solution)/shard_map/ppermute | solution.py:27
  13.8 4.3 %send_rows.2 = bf16[64,2,640]{2,1,0:T(2,128)(2,1)} custom-call(s32[1]{0:T(128)} %bitcast.3.place_ref, s32[1]{0:T(128)} %constant.34.clone.1.trip_ref, s32[3,8]{1,0:T(4,128)} %bitcast.57, s32[8,61]{1,0:T(8,128)} %words_v.1, f32[1,16]{1,0:T(1,128)} %bitcast.61, f32[1,16]{1,0:T(1,128)} %bitcast.64, bf16[2048,1024]{1,0:T(8,128)(2,1)} %table.1), custom_call_target="tpu_custom_call" | custom-call | tf_op jit(solution)/shard_map/send_rows/pallas_call | solution.py:122
  18.1 10.8 %all-to-all-start.1 = ((bf16[64,2,640]{2,1,0:T(2,128)(2,1)}), bf16[64,2,640]{2,1,0:T(2,128)(2,1)S(1)}, u32[]{:S(2)}, u32[]{:S(2)}) async-start(bf16[64,2,640]{2,1,0:T(2,128)(2,1)} %send_rows.2), calls=%async_computation.1 | async-start | bytes 327680 | tf_op jit(solution)/shard_map/all_to_all | solution.py:18
  29.0 1.5 %collective-permute-start.3 = (bf16[64,1024]{1,0:T(8,128)(2,1)S(1)}, bf16[64,1024]{1,0:T(8,128)(2,1)S(1)}, u32[]{:S(2)}, u32[]{:S(2)}) collective-permute-start(bf16[64,1024]{1,0:T(8,128)(2,1)S(1)} %collective-permute-done.2), channel_id=1, source_target_pairs={{0,64},{64,0},{1,65},{65,1},{2,66},{66,2},{3,67},{67,3},{4,68},{68... | collective-permute-start | bytes 393224 | tf_op jit(solution)/shard_map/ppermute | solution.py:31
  30.5 10.1 %all-to-all-done.1 = bf16[64,2,640]{2,1,0:T(2,128)(2,1)S(1)} async-done(((bf16[64,2,640]{2,1,0:T(2,128)(2,1)}), bf16[64,2,640]{2,1,0:T(2,128)(2,1)S(1)}, u32[]{:S(2)}, u32[]{:S(2)}) %all-to-all-start.1) | async-done | bytes 163872 | tf_op jit(solution)/shard_map/all_to_all | solution.py:18
  40.6 0.7 slice_reduce_fusion
  43.8 0.7 broadcast_in_dim.31
  44.5 3.5 %all-to-all-start.2 = ((bf16[16,8,1024]{2,1,0:T(8,128)(2,1)}), bf16[16,8,1024]{2,1,0:T(8,128)(2,1)S(1)}, u32[]{:S(2)}, u32[]{:S(2)}) async-start(bf16[16,8,1024]{2,1,0:T(8,128)(2,1)} %broadcast_in_dim.31), calls=%async_computation.2 | async-start | bytes 524288 | tf_op jit(solution)/shard_map/all_to_all | solution.py:18
  48.2 8.6 %all-to-all-done.2 = bf16[16,8,1024]{2,1,0:T(8,128)(2,1)S(1)} async-done(((bf16[16,8,1024]{2,1,0:T(8,128)(2,1)}), bf16[16,8,1024]{2,1,0:T(8,128)(2,1)S(1)}, u32[]{:S(2)}, u32[]{:S(2)}) %all-to-all-start.2) | async-done | bytes 262176 | tf_op jit(solution)/shard_map/all_to_all | solution.py:18
  56.8 1.6 %fusion.6 = bf16[16,8,1024]{2,1,0:T(8,128)(2,1)} fusion(bf16[256,1024]{1,0:T(8,128)(2,1)S(1)} %get-tuple-element.89, bf16[256,1024]{1,0:T(8,128)(2,1)S(1)} %get-tuple-element.88, bf16[16,8,1024]{2,1,0:T(8,128)(2,1)S(1)} %all-to-all-done.2), kind=kOutput, calls=%fused_computation.12 | convolution fusion | flops 136478720 | bytes 1572864 | tf_op jit(solution)/shard_map/dot_general | solution.py:241
  58.3 3.5 %all-to-all-start.3 = ((bf16[16,8,1024]{2,1,0:T(8,128)(2,1)}), bf16[16,8,1024]{2,1,0:T(8,128)(2,1)S(1)}, u32[]{:S(2)}, u32[]{:S(2)}) async-start(bf16[16,8,1024]{2,1,0:T(8,128)(2,1)} %fusion.6), calls=%async_computation.3 | async-start | bytes 524288 | tf_op jit(solution)/shard_map/all_to_all | solution.py:18
  61.9 2.1 %positions.1 = s32[8,64]{1,0:T(8,128)} custom-call(s32[3,8]{1,0:T(4,128)S(1)} %bitcast.59, s32[8,61]{1,0:T(8,128)S(1)} %get-tuple-element.209, s32[8,61]{1,0:T(8,128)S(1)} %get-tuple-element.209), custom_call_target="tpu_custom_call" | custom-call | tf_op jit(solution)/shard_map/positions/pallas_call | solution.py:165
  64.0 0.8 eq.57
  65.1 5.5 %all-to-all-done.3 = bf16[16,8,1024]{2,1,0:T(8,128)(2,1)S(1)} async-done(((bf16[16,8,1024]{2,1,0:T(8,128)(2,1)}), bf16[16,8,1024]{2,1,0:T(8,128)(2,1)S(1)}, u32[]{:S(2)}, u32[]{:S(2)}) %all-to-all-start.3) | async-done | bytes 262176 | tf_op jit(solution)/shard_map/all_to_all | solution.py:18
  71.4 0.7 copy.45
  72.1 4.6 %all-to-all-start.4 = ((f32[64,1,256]{2,1,0:T(1,128)}), f32[64,1,256]{2,1,0:T(1,128)S(1)}, u32[]{:S(2)}, u32[]{:S(2)}) async-start(f32[64,1,256]{2,1,0:T(1,128)} %copy.45), calls=%async_computation.4 | async-start | bytes 131072 | tf_op jit(solution)/shard_map/all_to_all | solution.py:18
  76.9 10.9 %all-to-all-done.4 = f32[64,1,256]{2,1,0:T(1,128)S(1)} async-done(((f32[64,1,256]{2,1,0:T(1,128)}), f32[64,1,256]{2,1,0:T(1,128)S(1)}, u32[]{:S(2)}, u32[]{:S(2)}) %all-to-all-start.4) | async-done | bytes 65568 | tf_op jit(solution)/shard_map/all_to_all | solution.py:18
  89.6 6.1 %collective-permute-start.4 = (f32[16]{0:T(128)S(1)}, f32[16]{0:T(128)S(1)}, u32[]{:S(2)}, u32[]{:S(2)}) collective-permute-start(f32[16]{0:T(128)S(1)} %multiply_reduce_fusion.3), channel_id=1, source_target_pairs={{0,64},{64,0},{1,65},{65,1},{2,66},{66,2},{3,67},{67,3},{4,68},{68... | collective-permute-start | bytes 200 | tf_op jit(solution)/shard_map/ppermute | solution.py:31
  95.7 0.8 collective-permute-done.4
  97.4 1.5 %collective-permute-done.5 = f32[16]{0:T(128)S(1)} collective-permute-done((f32[16]{0:T(128)S(1)}, f32[16]{0:T(128)S(1)}, u32[]{:S(2)}, u32[]{:S(2)}) %collective-permute-start.5) | collective-permute-done | bytes 96 | tf_op jit(solution)/shard_map/ppermute | solution.py:31
  (69 shorter events, 6.3 us)
Async XLA Ops:
  0.6 28.3 %copy-start.1 = (bf16[64,1024]{1,0:T(8,128)(2,1)S(1)}, bf16[64,1024]{1,0:T(8,128)(2,1)}, u32[]{:S(2)}) copy-start(bf16[64,1024]{1,0:T(8,128)(2,1)} %param.17) | copy-start | bytes 393220
  0.6 28.3 %copy-start = (bf16[1024,64]{0,1:T(8,128)(2,1)S(1)}, bf16[1024,64]{0,1:T(8,128)(2,1)}, u32[]{:S(2)}) copy-start(bf16[1024,64]{0,1:T(8,128)(2,1)} %param.16) | copy-start | bytes 393220
  0.7 42.4 %copy-start.3 = (s32[8,3]{0,1:T(4,128)S(1)}, s32[8,3]{0,1:T(4,128)}, u32[]{:S(2)}) copy-start(s32[8,3]{0,1:T(4,128)} %param.12) | copy-start | bytes 292
  0.7 42.4 %copy-start.2 = (s32[8,61]{1,0:T(8,128)S(1)}, s32[8,61]{1,0:T(8,128)}, u32[]{:S(2)}) copy-start(s32[8,61]{1,0:T(8,128)} %words_v.1) | copy-start | bytes 5860
  0.7 42.4 %copy-start.5 = (f32[16]{0:T(128)S(1)}, f32[16]{0:T(128)}, u32[]{:S(2)}) copy-start(f32[16]{0:T(128)} %param.18) | copy-start | bytes 196
  0.7 42.4 %copy-start.6 = (f32[16]{0:T(128)S(1)}, f32[16]{0:T(128)}, u32[]{:S(2)}) copy-start(f32[16]{0:T(128)} %param.19) | copy-start | bytes 196
  1.8 28.7 %collective-permute-start = (bf16[128,1024]{1,0:T(8,128)(2,1)S(1)}, bf16[128,1024]{1,0:T(8,128)(2,1)S(1)}, u32[]{:S(2)}, u32[]{:S(2)}) collective-permute-start(bf16[128,1024]{1,0:T(8,128)(2,1)S(1)} %pad_maximum_fusion), channel_id=1, source_target_pairs={{8,0},{16,8},{24,16},{0,24},{9,1},{17,9},{25,17},{1,25},{10,2},{18... | collective-permute-start | bytes 786440 | tf_op jit(solution)/shard_map/ppermute | solution.py:27
  8.7 39.3 %collective-permute-start.1 = (bf16[128,1024]{1,0:T(8,128)(2,1)S(1)}, bf16[128,1024]{1,0:T(8,128)(2,1)S(1)}, u32[]{:S(2)}, u32[]{:S(2)}) collective-permute-start(bf16[128,1024]{1,0:T(8,128)(2,1)S(1)} %pad_maximum_fusion), channel_id=1, source_target_pairs={{24,0},{0,8},{8,16},{16,24},{25,1},{1,9},{9,17},{17,25},{26,2},{2,... | collective-permute-start | bytes 786440 | tf_op jit(solution)/shard_map/ppermute | solution.py:27
  10.4 18.5 %collective-permute-start.2 = (bf16[64,1024]{1,0:T(8,128)(2,1)S(1)}, bf16[64,1024]{1,0:T(8,128)(2,1)S(1)}, u32[]{:S(2)}, u32[]{:S(2)}) collective-permute-start(bf16[64,1024]{1,0:T(8,128)(2,1)S(1)} %pad_maximum_fusion.1), channel_id=1, source_target_pairs={{16,0},{24,8},{0,16},{8,24},{17,1},{25,9},{1,17},{9,25},{18,2},{26... | collective-permute-start | bytes 393224 | tf_op jit(solution)/shard_map/ppermute | solution.py:27
  18.1 22.5 %all-to-all-start.1 = ((bf16[64,2,640]{2,1,0:T(2,128)(2,1)}), bf16[64,2,640]{2,1,0:T(2,128)(2,1)S(1)}, u32[]{:S(2)}, u32[]{:S(2)}) async-start(bf16[64,2,640]{2,1,0:T(2,128)(2,1)} %send_rows.2), calls=%async_computation.1 | async-start | bytes 327680 | tf_op jit(solution)/shard_map/all_to_all | solution.py:18
  29.0 19.2 %collective-permute-start.3 = (bf16[64,1024]{1,0:T(8,128)(2,1)S(1)}, bf16[64,1024]{1,0:T(8,128)(2,1)S(1)}, u32[]{:S(2)}, u32[]{:S(2)}) collective-permute-start(bf16[64,1024]{1,0:T(8,128)(2,1)S(1)} %collective-permute-done.2), channel_id=1, source_target_pairs={{0,64},{64,0},{1,65},{65,1},{2,66},{66,2},{3,67},{67,3},{4,68},{68... | collective-permute-start | bytes 393224 | tf_op jit(solution)/shard_map/ppermute | solution.py:31
  43.0 0.7 copy-start.4
  44.5 12.2 %all-to-all-start.2 = ((bf16[16,8,1024]{2,1,0:T(8,128)(2,1)}), bf16[16,8,1024]{2,1,0:T(8,128)(2,1)S(1)}, u32[]{:S(2)}, u32[]{:S(2)}) async-start(bf16[16,8,1024]{2,1,0:T(8,128)(2,1)} %broadcast_in_dim.31), calls=%async_computation.2 | async-start | bytes 524288 | tf_op jit(solution)/shard_map/all_to_all | solution.py:18
  48.1 40.9 %copy-start.7 = (s32[8]{0:T(128)S(1)}, s32[8]{0:T(128)}, u32[]{:S(2)}) copy-start(s32[8]{0:T(128)} %param.14) | copy-start | bytes 100
  58.3 12.2 %all-to-all-start.3 = ((bf16[16,8,1024]{2,1,0:T(8,128)(2,1)}), bf16[16,8,1024]{2,1,0:T(8,128)(2,1)S(1)}, u32[]{:S(2)}, u32[]{:S(2)}) async-start(bf16[16,8,1024]{2,1,0:T(8,128)(2,1)} %fusion.6), calls=%async_computation.3 | async-start | bytes 524288 | tf_op jit(solution)/shard_map/all_to_all | solution.py:18
  72.1 15.7 %all-to-all-start.4 = ((f32[64,1,256]{2,1,0:T(1,128)}), f32[64,1,256]{2,1,0:T(1,128)S(1)}, u32[]{:S(2)}, u32[]{:S(2)}) async-start(f32[64,1,256]{2,1,0:T(1,128)} %copy.45), calls=%async_computation.4 | async-start | bytes 131072 | tf_op jit(solution)/shard_map/all_to_all | solution.py:18
  89.6 6.9 %collective-permute-start.4 = (f32[16]{0:T(128)S(1)}, f32[16]{0:T(128)S(1)}, u32[]{:S(2)}, u32[]{:S(2)}) collective-permute-start(f32[16]{0:T(128)S(1)} %multiply_reduce_fusion.3), channel_id=1, source_target_pairs={{0,64},{64,0},{1,65},{65,1},{2,66},{66,2},{3,67},{67,3},{4,68},{68... | collective-permute-start | bytes 200 | tf_op jit(solution)/shard_map/ppermute | solution.py:31
  96.5 2.4 %collective-permute-start.5 = (f32[16]{0:T(128)S(1)}, f32[16]{0:T(128)S(1)}, u32[]{:S(2)}, u32[]{:S(2)}) collective-permute-start(f32[16]{0:T(128)S(1)} %add.63), channel_id=1, source_target_pairs={{0,128},{128,0},{1,129},{129,1},{2,130},{130,2},{3,131},{131,3},{4... | collective-permute-start | bytes 200 | tf_op jit(solution)/shard_map/ppermute | solution.py:31

commit v10 on v8

--- a/solution.py
+++ b/solution.py
@@ -12,6 +12,7 @@
 DP = ("yl", "core")
 ACT = ("yh", "zl", "x")
 LANES = 128
+COVER = 40_000_000
 
 
 def exchange(blocks, axes):
@@ -22,12 +23,12 @@
     return exchange(jnp.broadcast_to(array, (lax.axis_size(axes), *array.shape)), axes)
 
 
-def from_column(array, axis):
-    peers = lax.axis_size(axis)
-    return [
-        lax.ppermute(array, axis, [((i + step) % peers, i) for i in range(peers)])
-        for step in range(1, peers)
+def from_column(array):
+    steps, places = lax.axis_size("zh"), lax.axis_size(DP)
+    moves = [
+        (d * steps + (i + d) % steps, d * steps + i) for d in range(places) for i in range(steps)
     ]
+    return lax.ppermute(array, (*DP, "zh"), moves)
 
 
 def swapped(array, axis):
@@ -91,10 +92,8 @@
     middle = (exact - high).astype(jnp.bfloat16).astype(jnp.float32)
     least = (exact - high - middle).astype(jnp.bfloat16).astype(jnp.float32)
     parts = high + pltpu.roll(middle, share, 1) + pltpu.roll(least, 2 * share, 1)
-    trips = ((held[0] + peers - 1) // peers).astype(jnp.float32)
     row_of = lax.broadcasted_iota(jnp.int32, parts.shape, 0)
     lane = lax.broadcasted_iota(jnp.int32, parts.shape, 1)
-    parts = jnp.where((row_of == 1) & (lane == 1), trips, parts)
     slot_at = (row_of == 1) & (lane == 0)
     blank = jnp.where(slot_at, -1.0, parts)[0:2]
     sent[:, :, 0:half] = jnp.zeros((peers, 2, half), sent.dtype)
@@ -138,7 +137,7 @@
     )(place.reshape(1), trip.reshape(1), triples.T, words, gain, weight, table)
 
 
-def position_kernel(entries, triples, words, words_v, spot_ref, ids_ref):
+def position_kernel(entries, peers, triples, words, words_v, after, spot_ref, trips_ref, ids_ref):
     n_triples, seq_len = spot_ref.shape
     lead = triples.shape[0]
     toks = n_triples * seq_len
@@ -147,32 +146,41 @@
         for i in range(n_triples):
             ids_ref[i : i + 1, j : j + 1] = jnp.full((1, 1), triples[j, i], jnp.int32)
     ids_ref[:, lead:] = words_v[...]
-    keys = (ids_ref[...] >> shift) * toks
-    keys = keys + lax.broadcasted_iota(jnp.int32, keys.shape, 0) * seq_len
+    least = (ids_ref[...] >> shift) * toks
+    keys = least + lax.broadcasted_iota(jnp.int32, least.shape, 0) * seq_len
     keys = keys + lax.broadcasted_iota(jnp.int32, keys.shape, 1)
 
-    def scan(i, spot):
+    def scan(i, carry):
+        spot, first = carry
         for j in range(seq_len):
             token = triples[j, i] if j < lead else words[i, j - lead]
             key = (token >> shift) * toks + (i * seq_len + j)
             spot = spot + (key < keys).astype(jnp.int32)
-        return spot
-
-    spot_ref[...] = lax.fori_loop(0, n_triples, scan, jnp.zeros(keys.shape, jnp.int32))
-
-
-def positions(triples, words, entries):
+            first = first + (key < least).astype(jnp.int32)
+        return spot, first
+
+    none = jnp.zeros(keys.shape, jnp.int32)
+    spot, first = lax.fori_loop(0, n_triples, scan, (none, none))
+    spot_ref[...] = spot
+    trips_ref[0] = jnp.max((spot - first).astype(jnp.float32)).astype(jnp.int32) // peers + 1
+
+
+def positions(triples, words, entries, peers, after):
     shape = (triples.shape[0], triples.shape[1] + words.shape[1])
     smem = pl.BlockSpec(memory_space=pltpu.SMEM)
     vmem = pl.BlockSpec(memory_space=pltpu.VMEM)
     return pl.pallas_call(
-        functools.partial(position_kernel, entries),
-        out_shape=jax.ShapeDtypeStruct(shape, jnp.int32),
-        in_specs=[smem, smem, vmem],
-        out_specs=vmem,
+        functools.partial(position_kernel, entries, peers),
+        out_shape=(
+            jax.ShapeDtypeStruct(shape, jnp.int32),
+            jax.ShapeDtypeStruct((1,), jnp.int32),
+        ),
+        in_specs=[smem, smem, vmem, pl.BlockSpec(memory_space=pl.ANY)],
+        out_specs=(vmem, smem),
+        cost_estimate=pl.CostEstimate(flops=0, transcendentals=0, bytes_accessed=COVER),
         scratch_shapes=[pltpu.VMEM(shape, jnp.int32)],
         name="positions",
-    )(triples.T, words, words)
+    )(triples.T, words, words, after)
 
 
 def standardize(values):
@@ -194,16 +202,17 @@
     slots = toks // peers
     share = width // peers
 
-    units = up_weight.shape[1] // lax.axis_size("core")
-    start = lax.axis_index("core") * units
-    up_part = lax.dynamic_slice_in_dim(up_weight.T, start, units, 0)
-    down_part = lax.dynamic_slice_in_dim(down_weight, start, units, 0)
-    came = from_column(jnp.concatenate([up_part, down_part], axis=0), "zh")
+    units = up_weight.shape[1]
+    weights = from_column(jnp.concatenate([up_weight.T, down_weight], axis=0))[None]
+    weights = jnp.concatenate([weights, swapped(weights, "core")], axis=0)
+    weights = jnp.concatenate([weights, swapped(weights, "yl")], axis=0)
+    up_rows = weights[:, :units].reshape(-1, width)
+    down_rows = weights[:, units:].reshape(-1, width)
 
     gains = out_gain.reshape(1, -1), class_weight.reshape(1, -1)
 
-    def rows_of(trip):
-        return exchange(to_send(place, trip, triples, words, *gains, table, peers), MP)
+    def to_peers(trip):
+        return to_send(place, trip, triples, words, *gains, table, peers)
 
     half = width // 2
 
@@ -214,21 +223,17 @@
             picks.astype(bf16), rows, (((0,), (0,)), ((), ())), preferred_element_type=f32
         )
 
-    got = rows_of(jnp.int32(0))
-    trips = jnp.max(got[:, 1, half + 1].astype(f32)).astype(jnp.int32)
-    came = jnp.where(trips <= toks, jnp.stack(came), 0)
-    came = jnp.concatenate([came, swapped(came, "core")], axis=0)
-    up_rows = jnp.concatenate([up_weight.T, came[:, :units].reshape(-1, width)], axis=0)
-    down_rows = jnp.concatenate([down_weight, came[:, units:].reshape(-1, width)], axis=0)
-
+    sent = to_peers(jnp.int32(0))
+    got = exchange(sent, MP)
+    spot, trips = positions(triples, words, entries, peers, sent)
     score_weight = got[:, 0, half : half + 3 * share].astype(f32).reshape(peers, 3, share)
     score_weight = jnp.sum(score_weight, axis=1).reshape(1, width)
 
     def another(state):
         trip, embed = state
-        return trip + 1, embed + taken(rows_of(trip))
-
-    _, embed = lax.while_loop(lambda state: state[0] < trips, another, (jnp.int32(1), taken(got)))
+        return trip + 1, embed + taken(exchange(to_peers(trip), MP))
+
+    _, embed = lax.while_loop(lambda state: state[0] < trips[0], another, (jnp.int32(1), taken(got)))
 
     normed = (standardize(embed) * in_gain).astype(bf16)
     everyone = to_everyone(normed, ACT)
@@ -248,7 +253,7 @@
     level = got[:, 0, : slots * share].reshape(peers, slots, share)
     by_spot = (level * out_gain).astype(bf16).transpose(1, 0, 2).reshape(toks, share)
     score = got[:, 0, slots * share :][:, :slots].T.reshape(1, toks)
-    spot = positions(triples, words, entries).reshape(1, toks)
+    spot = spot.reshape(1, toks)
     where = spot == jnp.arange(toks)[:, None]
     encoded = lax.dot_general(
         by_spot, where.astype(bf16), (((0,), (0,)), ((), ())), preferred_element_type=f32

time: 102 us -> 104 us (1.020)
  starting transfers between devices: 44.9 us -> 49.8 us
  waiting for transfers between devices: 37.8 us -> 36.4 us
  local copies, waits for them, and re-layouts: 3.97 us -> 2.87 us
    ppermute x3 -> x4, starting transfers between devices: 4.65 us -> 12 us  [swapped(): return lax.ppermute(array, axis, [(0, 1), (1, 0)])]
    all_to_all x4, waiting for transfers between devices: 28.9 us -> 22.7 us  [exchange(): return lax.all_to_all(blocks, axes, split_axis=0, concat_axis=0, tiled=True)]
    ppermute x3 -> x4, waiting for transfers between devices: 2.28 us -> 8.38 us  [swapped(): return lax.ppermute(array, axis, [(0, 1), (1, 0)])]
    ppermute x3 -> x1, starting transfers between devices: 8.58 us -> 5.07 us  [from_column(): return lax.ppermute(array, (*DP, 'zh'), moves)]
    ppermute x3 -> x1, waiting for transfers between devices: 6.56 us -> 5.35 us  [from_column(): return lax.ppermute(array, (*DP, 'zh'), moves)]
    all_to_all x4, starting transfers between devices: 31.7 us -> 32.7 us  [exchange(): return lax.all_to_all(blocks, axes, split_axis=0, concat_axis=0, tiled=True)]
  transfers between devices with their start and end apart: 10 -> 9, of which waited for: 8 -> 7; matrix products, arithmetic and copies ran while one was open for 5% -> 3% of each run, Pallas kernels for 2% -> 2%
where the time goes in v10:
time: 104 us; the launch traced here: 103 us
  starting transfers between devices  49.8 us (48%)
  waiting for transfers between devices  36.4 us (35%)
  Pallas kernels  6.81 us (7%)
  other arithmetic  3.79 us (4%)
  local copies, waits for them, and re-layouts  2.87 us (3%)
  matrix products  2.08 us (2%)
    all_to_all x4, starting transfers between devices, exchange(): return lax.all_to_all(blocks, axes, split_axis=0, concat_axis=0, tiled=True)  32.7 us
    all_to_all x4, waiting for transfers between devices, exchange(): return lax.all_to_all(blocks, axes, split_axis=0, concat_axis=0, tiled=True)  22.7 us
    ppermute x4, starting transfers between devices, swapped(): return lax.ppermute(array, axis, [(0, 1), (1, 0)])  12 us
    ppermute x4, waiting for transfers between devices, swapped(): return lax.ppermute(array, axis, [(0, 1), (1, 0)])  8.38 us
    ppermute x1, waiting for transfers between devices, from_column(): return lax.ppermute(array, (*DP, 'zh'), moves)  5.35 us
    ppermute x1, starting transfers between devices, from_column(): return lax.ppermute(array, (*DP, 'zh'), moves)  5.07 us
    pallas_call x1, Pallas kernels, to_send(): pl.pallas_call(functools.partial(send_kernel, peers), out_shape=jax.Shape...  4.61 us
    pallas_call x1, Pallas kernels, positions(): pl.pallas_call(functools.partial(position_kernel, entries, peers), out_sh...  2.2 us
  transfers between devices with their start and end apart: 9, of which 7 were waited for; matrix products, arithmetic and copies ran while one was open for 3% of the time, Pallas kernels for 2%

profile of v10, /device:TPU:1, one launch (start us, length us, event | category | flops | bytes accessed | tf_op | source)
XLA Modules:
  0.0 103.4 jit_solution(10369998481235632007)
XLA Ops:
  0.7 4.6 %send_rows.2.after = bf16[64,2,640]{2,1,0:T(2,128)(2,1)} custom-call(s32[1]{0:T(128)} %bitcast.4.place_ref, s32[1]{0:T(128)} %constant.30.clone.1.trip_ref, s32[3,8]{1,0:T(4,128)} %bitcast.64, s32[8,61]{1,0:T(8,128)} %words_v.1, f32[1,16]{1,0:T(1,128)} %bitcast.68, f32[1,16]{1,0:T(1,128)} %bitcast.71, bf16[2048,1024]{1,0:T(8,128)(2,1)} %table.1), custom_call_target="tpu_custom_call" | custom-call | tf_op jit(solution)/shard_map/send_rows/pallas_call | solution.py:124
  5.3 14.8 %all-to-all-start.1 = ((bf16[64,2,640]{2,1,0:T(2,128)(2,1)}), bf16[64,2,640]{2,1,0:T(2,128)(2,1)S(1)}, u32[]{:S(2)}, u32[]{:S(2)}) async-start(bf16[64,2,640]{2,1,0:T(2,128)(2,1)} %send_rows.2.after), calls=%async_computation.1 | async-start | bytes 327680 | tf_op jit(solution)/shard_map/all_to_all | solution.py:19
  20.2 5.1 %collective-permute-start = (bf16[128,1024]{1,0:T(8,128)(2,1)S(1)}, bf16[128,1024]{1,0:T(8,128)(2,1)S(1)}, u32[]{:S(2)}, u32[]{:S(2)}) collective-permute-start(bf16[128,1024]{1,0:T(8,128)(2,1)S(1)} %pad_maximum_fusion.2), channel_id=1, source_target_pairs={{0,0},{8,8},{16,16},{24,24},{72,64},{80,72},{88,80},{64,88},{144,1... | collective-permute-start | bytes 786440 | tf_op jit(solution)/shard_map/ppermute | solution.py:31
  25.3 2.2 %positions.1 = (s32[8,64]{1,0:T(8,128)}, s32[1]{0:T(128)}) custom-call(s32[3,8]{1,0:T(4,128)S(1)} %bitcast.65, s32[8,61]{1,0:T(8,128)S(1)} %copy-done, s32[8,61]{1,0:T(8,128)S(1)} %copy-done, bf16[64,2,640]{2,1,0:T(2,128)(2,1)} %send_rows.2.after), custom_call_target="tpu_custom_call" | custom-call | bytes 40000000 | tf_op jit(solution)/shard_map/positions/pallas_call | solution.py:172
  27.5 5.3 %collective-permute-done = bf16[128,1024]{1,0:T(8,128)(2,1)S(1)} collective-permute-done((bf16[128,1024]{1,0:T(8,128)(2,1)S(1)}, bf16[128,1024]{1,0:T(8,128)(2,1)S(1)}, u32[]{:S(2)}, u32[]{:S(2)}) %collective-permute-start) | collective-permute-done | bytes 262176 | tf_op jit(solution)/shard_map/ppermute | solution.py:31
  33.1 0.6 fusion.60
  33.9 0.7 while.10
  34.8 7.8 %collective-permute-start.2 = (bf16[2,128,1024]{2,1,0:T(8,128)(2,1)S(1)}, bf16[2,128,1024]{2,1,0:T(8,128)(2,1)S(1)}, u32[]{:S(2)}, u32[]{:S(2)}) collective-permute-start(bf16[2,128,1024]{2,1,0:T(8,128)(2,1)S(1)} %pad_maximum_fusion.1), channel_id=1, source_target_pairs={{0,128},{128,0},{1,129},{129,1},{2,130},{130,2},{3,131},{131,3},{4... | collective-permute-start | bytes 1572872 | tf_op jit(solution)/shard_map/ppermute | solution.py:35
  42.6 0.7 broadcast_in_dim.48
  43.4 7.3 %all-to-all-start.2 = ((bf16[16,8,1024]{2,1,0:T(8,128)(2,1)}), bf16[16,8,1024]{2,1,0:T(8,128)(2,1)S(1)}, u32[]{:S(2)}, u32[]{:S(2)}) async-start(bf16[16,8,1024]{2,1,0:T(8,128)(2,1)} %broadcast_in_dim.48), calls=%async_computation.2 | async-start | bytes 524288 | tf_op jit(solution)/shard_map/all_to_all | solution.py:19
  50.7 6.4 %collective-permute-done.2 = bf16[2,128,1024]{2,1,0:T(8,128)(2,1)S(1)} collective-permute-done((bf16[2,128,1024]{2,1,0:T(8,128)(2,1)S(1)}, bf16[2,128,1024]{2,1,0:T(8,128)(2,1)S(1)}, u32[]{:S(2)}, u32[]{:S(2)}) %collective-permute-start.2) | collective-permute-done | bytes 524320 | tf_op jit(solution)/shard_map/ppermute | solution.py:35
  57.3 3.4 %all-to-all-done.2 = bf16[16,8,1024]{2,1,0:T(8,128)(2,1)S(1)} async-done(((bf16[16,8,1024]{2,1,0:T(8,128)(2,1)}), bf16[16,8,1024]{2,1,0:T(8,128)(2,1)S(1)}, u32[]{:S(2)}, u32[]{:S(2)}) %all-to-all-start.2) | async-done | bytes 262176 | tf_op jit(solution)/shard_map/all_to_all | solution.py:19
  60.8 1.5 %fusion.6 = bf16[16,8,1024]{2,1,0:T(8,128)(2,1)} fusion(bf16[256,1024]{1,0:T(8,128)(2,1)S(1)} %bitcast.59, bf16[256,1024]{1,0:T(8,128)(2,1)S(1)} %bitcast.58, bf16[16,8,1024]{2,1,0:T(8,128)(2,1)S(1)} %all-to-all-done.2), kind=kOutput, calls=%fused_computation.12 | convolution fusion | flops 136478720 | bytes 1572864 | tf_op jit(solution)/shard_map/dot_general | solution.py:244
  62.3 4.1 %all-to-all-start.3 = ((bf16[16,8,1024]{2,1,0:T(8,128)(2,1)}), bf16[16,8,1024]{2,1,0:T(8,128)(2,1)S(1)}, u32[]{:S(2)}, u32[]{:S(2)}) async-start(bf16[16,8,1024]{2,1,0:T(8,128)(2,1)} %fusion.6), calls=%async_computation.3 | async-start | bytes 524288 | tf_op jit(solution)/shard_map/all_to_all | solution.py:19
  66.8 8.4 %all-to-all-done.3 = bf16[16,8,1024]{2,1,0:T(8,128)(2,1)S(1)} async-done(((bf16[16,8,1024]{2,1,0:T(8,128)(2,1)}), bf16[16,8,1024]{2,1,0:T(8,128)(2,1)S(1)}, u32[]{:S(2)}, u32[]{:S(2)}) %all-to-all-start.3) | async-done | bytes 262176 | tf_op jit(solution)/shard_map/all_to_all | solution.py:19
  76.0 0.7 copy.45
  76.7 6.5 %all-to-all-start.4 = ((f32[64,1,256]{2,1,0:T(1,128)}), f32[64,1,256]{2,1,0:T(1,128)S(1)}, u32[]{:S(2)}, u32[]{:S(2)}) async-start(f32[64,1,256]{2,1,0:T(1,128)} %copy.45), calls=%async_computation.4 | async-start | bytes 131072 | tf_op jit(solution)/shard_map/all_to_all | solution.py:19
  83.4 10.9 %all-to-all-done.4 = f32[64,1,256]{2,1,0:T(1,128)S(1)} async-done(((f32[64,1,256]{2,1,0:T(1,128)}), f32[64,1,256]{2,1,0:T(1,128)S(1)}, u32[]{:S(2)}, u32[]{:S(2)}) %all-to-all-start.4) | async-done | bytes 65568 | tf_op jit(solution)/shard_map/all_to_all | solution.py:19
  95.5 0.5 fusion.66
  96.1 3.6 %collective-permute-start.3 = (f32[16]{0:T(128)S(1)}, f32[16]{0:T(128)S(1)}, u32[]{:S(2)}, u32[]{:S(2)}) collective-permute-start(f32[16]{0:T(128)S(1)} %multiply_reduce_fusion.3), channel_id=1, source_target_pairs={{0,64},{64,0},{1,65},{65,1},{2,66},{66,2},{3,67},{67,3},{4,68},{68... | collective-permute-start | bytes 200 | tf_op jit(solution)/shard_map/ppermute | solution.py:35
  99.7 0.8 collective-permute-done.3
  100.5 0.6 collective-permute-start.4
  101.1 0.6 convert_bitcast_fusion
  101.7 1.1 %collective-permute-done.4 = f32[16]{0:T(128)S(1)} collective-permute-done((f32[16]{0:T(128)S(1)}, f32[16]{0:T(128)S(1)}, u32[]{:S(2)}, u32[]{:S(2)}) %collective-permute-start.4) | collective-permute-done | bytes 96 | tf_op jit(solution)/shard_map/ppermute | solution.py:35
  (63 shorter events, 4.1 us)
Async XLA Ops:
  0.6 24.6 %copy-start = (s32[8,61]{1,0:T(8,128)S(1)}, s32[8,61]{1,0:T(8,128)}, u32[]{:S(2)}) copy-start(s32[8,61]{1,0:T(8,128)} %words_v.1) | copy-start | bytes 5860
  0.6 33.2 %copy-start.5 = (f32[16]{0:T(128)S(1)}, f32[16]{0:T(128)}, u32[]{:S(2)}) copy-start(f32[16]{0:T(128)} %param.18) | copy-start | bytes 196
  0.7 24.6 %copy-start.3 = (s32[8,3]{0,1:T(4,128)S(1)}, s32[8,3]{0,1:T(4,128)}, u32[]{:S(2)}) copy-start(s32[8,3]{0,1:T(4,128)} %param.12) | copy-start | bytes 292
  0.7 33.2 %copy-start.6 = (f32[16]{0:T(128)S(1)}, f32[16]{0:T(128)}, u32[]{:S(2)}) copy-start(f32[16]{0:T(128)} %param.19) | copy-start | bytes 196
  0.7 19.5 %copy-start.1 = (bf16[64,1024]{1,0:T(8,128)(2,1)S(1)}, bf16[64,1024]{1,0:T(8,128)(2,1)}, u32[]{:S(2)}) copy-start(bf16[64,1024]{1,0:T(8,128)(2,1)} %param.17) | copy-start | bytes 393220
  0.7 19.5 %copy-start.2 = (bf16[1024,64]{0,1:T(8,128)(2,1)S(1)}, bf16[1024,64]{0,1:T(8,128)(2,1)}, u32[]{:S(2)}) copy-start(bf16[1024,64]{0,1:T(8,128)(2,1)} %param.16) | copy-start | bytes 393220
  5.3 27.5 %all-to-all-start.1 = ((bf16[64,2,640]{2,1,0:T(2,128)(2,1)}), bf16[64,2,640]{2,1,0:T(2,128)(2,1)S(1)}, u32[]{:S(2)}, u32[]{:S(2)}) async-start(bf16[64,2,640]{2,1,0:T(2,128)(2,1)} %send_rows.2.after), calls=%async_computation.1 | async-start | bytes 327680 | tf_op jit(solution)/shard_map/all_to_all | solution.py:19
  20.2 12.7 %collective-permute-start = (bf16[128,1024]{1,0:T(8,128)(2,1)S(1)}, bf16[128,1024]{1,0:T(8,128)(2,1)S(1)}, u32[]{:S(2)}, u32[]{:S(2)}) collective-permute-start(bf16[128,1024]{1,0:T(8,128)(2,1)S(1)} %pad_maximum_fusion.2), channel_id=1, source_target_pairs={{0,0},{8,8},{16,16},{24,24},{72,64},{80,72},{88,80},{64,88},{144,1... | collective-permute-start | bytes 786440 | tf_op jit(solution)/shard_map/ppermute | solution.py:31
  32.8 1.9 %collective-permute-start.1 = (bf16[1,128,1024]{2,1,0:T(8,128)(2,1)S(1)}, bf16[1,128,1024]{2,1,0:T(8,128)(2,1)S(1)}, u32[]{:S(2)}, u32[]{:S(2)}) collective-permute-start(bf16[1,128,1024]{2,1,0:T(8,128)(2,1)S(1)} %bitcast.55), channel_id=1, source_target_pairs={{0,64},{64,0},{1,65},{65,1},{2,66},{66,2},{3,67},{67,3},{4,68},{68... | collective-permute-start | bytes 786440 | tf_op jit(solution)/shard_map/ppermute | solution.py:35
  33.9 8.7 %copy-start.4 = (f32[1024]{0:T(1024)S(1)}, f32[1024]{0:T(1024)}, u32[]{:S(2)}) copy-start(f32[1024]{0:T(1024)} %param.15) | copy-start | bytes 12292
  34.8 22.3 %collective-permute-start.2 = (bf16[2,128,1024]{2,1,0:T(8,128)(2,1)S(1)}, bf16[2,128,1024]{2,1,0:T(8,128)(2,1)S(1)}, u32[]{:S(2)}, u32[]{:S(2)}) collective-permute-start(bf16[2,128,1024]{2,1,0:T(8,128)(2,1)S(1)} %pad_maximum_fusion.1), channel_id=1, source_target_pairs={{0,128},{128,0},{1,129},{129,1},{2,130},{130,2},{3,131},{131,3},{4... | collective-permute-start | bytes 1572872 | tf_op jit(solution)/shard_map/ppermute | solution.py:35
  43.4 17.4 %all-to-all-start.2 = ((bf16[16,8,1024]{2,1,0:T(8,128)(2,1)}), bf16[16,8,1024]{2,1,0:T(8,128)(2,1)S(1)}, u32[]{:S(2)}, u32[]{:S(2)}) async-start(bf16[16,8,1024]{2,1,0:T(8,128)(2,1)} %broadcast_in_dim.48), calls=%async_computation.2 | async-start | bytes 524288 | tf_op jit(solution)/shard_map/all_to_all | solution.py:19
  50.7 15.7 %copy-start.7 = (s32[8,64]{1,0:T(8,128)S(1)}, s32[8,64]{1,0:T(8,128)}, u32[]{:S(2)}) copy-start(s32[8,64]{1,0:T(8,128)} %get-tuple-element.55) | copy-start | bytes 6148
  57.3 38.2 %copy-start.8 = (s32[8]{0:T(128)S(1)}, s32[8]{0:T(128)}, u32[]{:S(2)}) copy-start(s32[8]{0:T(128)} %param.14) | copy-start | bytes 100
  62.3 12.8 %all-to-all-start.3 = ((bf16[16,8,1024]{2,1,0:T(8,128)(2,1)}), bf16[16,8,1024]{2,1,0:T(8,128)(2,1)S(1)}, u32[]{:S(2)}, u32[]{:S(2)}) async-start(bf16[16,8,1024]{2,1,0:T(8,128)(2,1)} %fusion.6), calls=%async_computation.3 | async-start | bytes 524288 | tf_op jit(solution)/shard_map/all_to_all | solution.py:19
  76.7 17.7 %all-to-all-start.4 = ((f32[64,1,256]{2,1,0:T(1,128)}), f32[64,1,256]{2,1,0:T(1,128)S(1)}, u32[]{:S(2)}, u32[]{:S(2)}) async-start(f32[64,1,256]{2,1,0:T(1,128)} %copy.45), calls=%async_computation.4 | async-start | bytes 131072 | tf_op jit(solution)/shard_map/all_to_all | solution.py:19
  96.1 4.4 %collective-permute-start.3 = (f32[16]{0:T(128)S(1)}, f32[16]{0:T(128)S(1)}, u32[]{:S(2)}, u32[]{:S(2)}) collective-permute-start(f32[16]{0:T(128)S(1)} %multiply_reduce_fusion.3), channel_id=1, source_target_pairs={{0,64},{64,0},{1,65},{65,1},{2,66},{66,2},{3,67},{67,3},{4,68},{68... | collective-permute-start | bytes 200 | tf_op jit(solution)/shard_map/ppermute | solution.py:35
  100.5 2.4 %collective-permute-start.4 = (f32[16]{0:T(128)S(1)}, f32[16]{0:T(128)S(1)}, u32[]{:S(2)}, u32[]{:S(2)}) collective-permute-start(f32[16]{0:T(128)S(1)} %add.58), channel_id=1, source_target_pairs={{0,128},{128,0},{1,129},{129,1},{2,130},{130,2},{3,131},{131,3},{4... | collective-permute-start | bytes 200 | tf_op jit(solution)/shard_map/ppermute | solution.py:35

commit v11 on v10

--- a/solution.py
+++ b/solution.py
@@ -23,12 +23,9 @@
     return exchange(jnp.broadcast_to(array, (lax.axis_size(axes), *array.shape)), axes)
 
 
-def from_column(array):
-    steps, places = lax.axis_size("zh"), lax.axis_size(DP)
-    moves = [
-        (d * steps + (i + d) % steps, d * steps + i) for d in range(places) for i in range(steps)
-    ]
-    return lax.ppermute(array, (*DP, "zh"), moves)
+def moved(array, axis, step):
+    peers = lax.axis_size(axis)
+    return lax.ppermute(array, axis, [((i + step) % peers, i) for i in range(peers)])
 
 
 def swapped(array, axis):
@@ -203,11 +200,19 @@
     share = width // peers
 
     units = up_weight.shape[1]
-    weights = from_column(jnp.concatenate([up_weight.T, down_weight], axis=0))[None]
-    weights = jnp.concatenate([weights, swapped(weights, "core")], axis=0)
-    weights = jnp.concatenate([weights, swapped(weights, "yl")], axis=0)
-    up_rows = weights[:, :units].reshape(-1, width)
-    down_rows = weights[:, units:].reshape(-1, width)
+    half_units = units // lax.axis_size("core")
+    start = lax.axis_index("core") * half_units
+    own = lax.optimization_barrier(jnp.concatenate([up_weight.T, down_weight], axis=0))
+    far = lax.dynamic_slice_in_dim(own.reshape(2, units, width), start, half_units, 1)
+    far = moved(far.reshape(units, width), "zh", 2)
+    weights = [own, moved(own, "zh", 1), moved(own, "zh", 3)]
+    halves = [far, swapped(far, "core")]
+    up_rows = jnp.concatenate(
+        [w[:units] for w in weights] + [h[:half_units] for h in halves], axis=0
+    )
+    down_rows = jnp.concatenate(
+        [w[units:] for w in weights] + [h[half_units:] for h in halves], axis=0
+    )
 
     gains = out_gain.reshape(1, -1), class_weight.reshape(1, -1)
 

time: 104 us -> 97.2 us (0.935)
  starting transfers between devices: 49.8 us -> 40.7 us
  waiting for transfers between devices: 36.4 us -> 37.9 us
    all_to_all x4, waiting for transfers between devices: 22.7 us -> 35.7 us  [exchange(): return lax.all_to_all(blocks, axes, split_axis=0, concat_axis=0, tiled=True)]
    all_to_all x4, starting transfers between devices: 32.7 us -> 23 us  [exchange(): return lax.all_to_all(blocks, axes, split_axis=0, concat_axis=0, tiled=True)]
    ppermute x4 -> x3, waiting for transfers between devices: 8.38 us -> 2.21 us  [swapped(): return lax.ppermute(array, axis, [(0, 1), (1, 0)])]
    ppermute x1 -> x3, waiting for transfers between devices: 5.35 us -> 0.01 us  [moved(): lax.ppermute(array, axis, [((i + step) % peers, i) for i in range(peers)])]
    ppermute x1 -> x3, starting transfers between devices: 5.07 us -> 10.3 us  [moved(): lax.ppermute(array, axis, [((i + step) % peers, i) for i in range(peers)])]
    ppermute x4 -> x3, starting transfers between devices: 12 us -> 7.47 us  [swapped(): return lax.ppermute(array, axis, [(0, 1), (1, 0)])]
  transfers between devices with their start and end apart: 9 -> 10, of which waited for: 7 -> 6; matrix products, arithmetic and copies ran while one was open for 3% -> 3% of each run, Pallas kernels for 2% -> 7%
where the time goes in v11:
time: 97.2 us; the launch traced here: 96.7 us
  starting transfers between devices  40.7 us (42%)
  waiting for transfers between devices  37.9 us (39%)
  Pallas kernels  6.9 us (7%)
  other arithmetic  4.62 us (5%)
  local copies, waits for them, and re-layouts  2.85 us (3%)
  matrix products  2.08 us (2%)
    all_to_all x4, waiting for transfers between devices, exchange(): return lax.all_to_all(blocks, axes, split_axis=0, concat_axis=0, tiled=True)  35.7 us
    all_to_all x4, starting transfers between devices, exchange(): return lax.all_to_all(blocks, axes, split_axis=0, concat_axis=0, tiled=True)  23 us
    ppermute x3, starting transfers between devices, moved(): lax.ppermute(array, axis, [((i + step) % peers, i) for i in range(peers)])  10.3 us
    ppermute x3, starting transfers between devices, swapped(): return lax.ppermute(array, axis, [(0, 1), (1, 0)])  7.47 us
    pallas_call x1, Pallas kernels, to_send(): pl.pallas_call(functools.partial(send_kernel, peers), out_shape=jax.Shape...  4.7 us
    ppermute x3, waiting for transfers between devices, swapped(): return lax.ppermute(array, axis, [(0, 1), (1, 0)])  2.21 us
    pallas_call x1, Pallas kernels, positions(): pl.pallas_call(functools.partial(position_kernel, entries, peers), out_sh...  2.2 us
  transfers between devices with their start and end apart: 10, of which 6 were waited for; matrix products, arithmetic and copies ran while one was open for 3% of the time, Pallas kernels for 7%

profile of v11, /device:TPU:1, one launch (start us, length us, event | category | flops | bytes accessed | tf_op | source)
XLA Modules:
  0.0 96.7 jit_solution(11609239964868409141)
XLA Ops:
  0.7 1.0 %pad_maximum_fusion = bf16[128,1024]{1,0:T(8,128)(2,1)S(1)} fusion(bf16[64,1024]{1,0:T(8,128)(2,1)} %param.17, bf16[64,1024]{1,0:T(8,128)(2,1)} %bitcast.59), kind=kLoop, calls=%fused_computation.18 | loop fusion | flops 524288 | bytes 524288 | tf_op jit(solution)/shard_map/concatenate | solution.py:205
  1.7 6.9 %collective-permute-start = (bf16[128,1024]{1,0:T(8,128)(2,1)S(1)}, bf16[128,1024]{1,0:T(8,128)(2,1)S(1)}, u32[]{:S(2)}, u32[]{:S(2)}) collective-permute-start(bf16[128,1024]{1,0:T(8,128)(2,1)S(1)} %pad_maximum_fusion), channel_id=1, source_target_pairs={{8,0},{16,8},{24,16},{0,24},{9,1},{17,9},{25,17},{1,25},{10,2},{18... | collective-permute-start | bytes 786440 | tf_op jit(solution)/shard_map/ppermute | solution.py:28
  8.6 3.3 %collective-permute-start.2 = (bf16[64,1024]{1,0:T(8,128)(2,1)S(1)}, bf16[64,1024]{1,0:T(8,128)(2,1)S(1)}, u32[]{:S(2)}, u32[]{:S(2)}) collective-permute-start(bf16[64,1024]{1,0:T(8,128)(2,1)S(1)} %bitcast.57), channel_id=1, source_target_pairs={{16,0},{24,8},{0,16},{8,24},{17,1},{25,9},{1,17},{9,25},{18,2},{26... | collective-permute-start | bytes 393224 | tf_op jit(solution)/shard_map/ppermute | solution.py:28
  12.0 4.7 %send_rows.2.after = bf16[64,2,640]{2,1,0:T(2,128)(2,1)} custom-call(s32[1]{0:T(128)} %bitcast.4.place_ref, s32[1]{0:T(128)} %constant.33.clone.1.trip_ref, s32[3,8]{1,0:T(4,128)} %bitcast.60, s32[8,61]{1,0:T(8,128)} %words_v.1, f32[1,16]{1,0:T(1,128)} %bitcast.64, f32[1,16]{1,0:T(1,128)} %bitcast.67, bf16[2048,1024]{1,0:T(8,128)(2,1)} %table.1), custom_call_target="tpu_custom_call" | custom-call | tf_op jit(solution)/shard_map/send_rows/pallas_call | solution.py:121
  16.7 10.1 %all-to-all-start.1 = ((bf16[64,2,640]{2,1,0:T(2,128)(2,1)}), bf16[64,2,640]{2,1,0:T(2,128)(2,1)S(1)}, u32[]{:S(2)}, u32[]{:S(2)}) async-start(bf16[64,2,640]{2,1,0:T(2,128)(2,1)} %send_rows.2.after), calls=%async_computation.1 | async-start | bytes 327680 | tf_op jit(solution)/shard_map/all_to_all | solution.py:19
  26.9 2.2 %positions.1 = (s32[8,64]{1,0:T(8,128)}, s32[1]{0:T(128)}) custom-call(s32[3,8]{1,0:T(4,128)S(1)} %bitcast.61, s32[8,61]{1,0:T(8,128)S(1)} %copy-done, s32[8,61]{1,0:T(8,128)S(1)} %copy-done, bf16[64,2,640]{2,1,0:T(2,128)(2,1)} %send_rows.2.after), custom_call_target="tpu_custom_call" | custom-call | bytes 40000000 | tf_op jit(solution)/shard_map/positions/pallas_call | solution.py:169
  29.1 2.0 %collective-permute-start.3 = (bf16[64,1024]{1,0:T(8,128)(2,1)S(1)}, bf16[64,1024]{1,0:T(8,128)(2,1)S(1)}, u32[]{:S(2)}, u32[]{:S(2)}) collective-permute-start(bf16[64,1024]{1,0:T(8,128)(2,1)S(1)} %collective-permute-done.2), channel_id=1, source_target_pairs={{0,64},{64,0},{1,65},{65,1},{2,66},{66,2},{3,67},{67,3},{4,68},{68... | collective-permute-start | bytes 393224 | tf_op jit(solution)/shard_map/ppermute | solution.py:32
  31.1 7.8 %all-to-all-done.1 = bf16[64,2,640]{2,1,0:T(2,128)(2,1)S(1)} async-done(((bf16[64,2,640]{2,1,0:T(2,128)(2,1)}), bf16[64,2,640]{2,1,0:T(2,128)(2,1)S(1)}, u32[]{:S(2)}, u32[]{:S(2)}) %all-to-all-start.1) | async-done | bytes 163872 | tf_op jit(solution)/shard_map/all_to_all | solution.py:19
  39.2 0.6 fusion.60
  40.0 0.7 while.10
  40.9 0.7 broadcast_in_dim.31
  41.6 3.5 %all-to-all-start.2 = ((bf16[16,8,1024]{2,1,0:T(8,128)(2,1)}), bf16[16,8,1024]{2,1,0:T(8,128)(2,1)S(1)}, u32[]{:S(2)}, u32[]{:S(2)}) async-start(bf16[16,8,1024]{2,1,0:T(8,128)(2,1)} %broadcast_in_dim.31), calls=%async_computation.2 | async-start | bytes 524288 | tf_op jit(solution)/shard_map/all_to_all | solution.py:19
  45.3 8.6 %all-to-all-done.2 = bf16[16,8,1024]{2,1,0:T(8,128)(2,1)S(1)} async-done(((bf16[16,8,1024]{2,1,0:T(8,128)(2,1)}), bf16[16,8,1024]{2,1,0:T(8,128)(2,1)S(1)}, u32[]{:S(2)}, u32[]{:S(2)}) %all-to-all-start.2) | async-done | bytes 262176 | tf_op jit(solution)/shard_map/all_to_all | solution.py:19
  53.9 1.5 %fusion.6 = bf16[16,8,1024]{2,1,0:T(8,128)(2,1)} fusion(bf16[256,1024]{1,0:T(8,128)(2,1)S(1)} %get-tuple-element.95, bf16[256,1024]{1,0:T(8,128)(2,1)S(1)} %get-tuple-element.94, bf16[16,8,1024]{2,1,0:T(8,128)(2,1)S(1)} %all-to-all-done.2), kind=kOutput, calls=%fused_computation.12 | convolution fusion | flops 136478720 | bytes 1572864 | tf_op jit(solution)/shard_map/dot_general | solution.py:249
  55.4 3.5 %all-to-all-start.3 = ((bf16[16,8,1024]{2,1,0:T(8,128)(2,1)}), bf16[16,8,1024]{2,1,0:T(8,128)(2,1)S(1)}, u32[]{:S(2)}, u32[]{:S(2)}) async-start(bf16[16,8,1024]{2,1,0:T(8,128)(2,1)} %fusion.6), calls=%async_computation.3 | async-start | bytes 524288 | tf_op jit(solution)/shard_map/all_to_all | solution.py:19
  59.3 8.3 %all-to-all-done.3 = bf16[16,8,1024]{2,1,0:T(8,128)(2,1)S(1)} async-done(((bf16[16,8,1024]{2,1,0:T(8,128)(2,1)}), bf16[16,8,1024]{2,1,0:T(8,128)(2,1)S(1)}, u32[]{:S(2)}, u32[]{:S(2)}) %all-to-all-start.3) | async-done | bytes 262176 | tf_op jit(solution)/shard_map/all_to_all | solution.py:19
  68.5 0.7 copy.45
  69.2 5.8 %all-to-all-start.4 = ((f32[64,1,256]{2,1,0:T(1,128)}), f32[64,1,256]{2,1,0:T(1,128)S(1)}, u32[]{:S(2)}, u32[]{:S(2)}) async-start(f32[64,1,256]{2,1,0:T(1,128)} %copy.45), calls=%async_computation.4 | async-start | bytes 131072 | tf_op jit(solution)/shard_map/all_to_all | solution.py:19
  75.2 10.9 %all-to-all-done.4 = f32[64,1,256]{2,1,0:T(1,128)S(1)} async-done(((f32[64,1,256]{2,1,0:T(1,128)}), f32[64,1,256]{2,1,0:T(1,128)S(1)}, u32[]{:S(2)}, u32[]{:S(2)}) %all-to-all-start.4) | async-done | bytes 65568 | tf_op jit(solution)/shard_map/all_to_all | solution.py:19
  87.3 0.5 fusion.66
  87.9 5.0 %collective-permute-start.4 = (f32[16]{0:T(128)S(1)}, f32[16]{0:T(128)S(1)}, u32[]{:S(2)}, u32[]{:S(2)}) collective-permute-start(f32[16]{0:T(128)S(1)} %multiply_reduce_fusion.3), channel_id=1, source_target_pairs={{0,64},{64,0},{1,65},{65,1},{2,66},{66,2},{3,67},{67,3},{4,68},{68... | collective-permute-start | bytes 200 | tf_op jit(solution)/shard_map/ppermute | solution.py:32
  92.9 0.8 collective-permute-done.4
  94.2 0.6 convert_bitcast_fusion
  94.8 1.4 %collective-permute-done.5 = f32[16]{0:T(128)S(1)} collective-permute-done((f32[16]{0:T(128)S(1)}, f32[16]{0:T(128)S(1)}, u32[]{:S(2)}, u32[]{:S(2)}) %collective-permute-start.5) | collective-permute-done | bytes 96 | tf_op jit(solution)/shard_map/ppermute | solution.py:32
  (64 shorter events, 4.3 us)
Async XLA Ops:
  0.6 26.2 %copy-start.1 = (s32[8,3]{0,1:T(4,128)S(1)}, s32[8,3]{0,1:T(4,128)}, u32[]{:S(2)}) copy-start(s32[8,3]{0,1:T(4,128)} %param.12) | copy-start | bytes 292
  0.6 26.2 %copy-start = (s32[8,61]{1,0:T(8,128)S(1)}, s32[8,61]{1,0:T(8,128)}, u32[]{:S(2)}) copy-start(s32[8,61]{1,0:T(8,128)} %words_v.1) | copy-start | bytes 5860
  0.7 39.3 %copy-start.3 = (f32[16]{0:T(128)S(1)}, f32[16]{0:T(128)}, u32[]{:S(2)}) copy-start(f32[16]{0:T(128)} %param.18) | copy-start | bytes 196
  0.7 39.3 %copy-start.4 = (f32[16]{0:T(128)S(1)}, f32[16]{0:T(128)}, u32[]{:S(2)}) copy-start(f32[16]{0:T(128)} %param.19) | copy-start | bytes 196
  1.7 29.4 %collective-permute-start = (bf16[128,1024]{1,0:T(8,128)(2,1)S(1)}, bf16[128,1024]{1,0:T(8,128)(2,1)S(1)}, u32[]{:S(2)}, u32[]{:S(2)}) collective-permute-start(bf16[128,1024]{1,0:T(8,128)(2,1)S(1)} %pad_maximum_fusion), channel_id=1, source_target_pairs={{8,0},{16,8},{24,16},{0,24},{9,1},{17,9},{25,17},{1,25},{10,2},{18... | collective-permute-start | bytes 786440 | tf_op jit(solution)/shard_map/ppermute | solution.py:28
  8.6 36.6 %collective-permute-start.1 = (bf16[128,1024]{1,0:T(8,128)(2,1)S(1)}, bf16[128,1024]{1,0:T(8,128)(2,1)S(1)}, u32[]{:S(2)}, u32[]{:S(2)}) collective-permute-start(bf16[128,1024]{1,0:T(8,128)(2,1)S(1)} %pad_maximum_fusion), channel_id=1, source_target_pairs={{24,0},{0,8},{8,16},{16,24},{25,1},{1,9},{9,17},{17,25},{26,2},{2,... | collective-permute-start | bytes 786440 | tf_op jit(solution)/shard_map/ppermute | solution.py:28
  8.6 20.4 %collective-permute-start.2 = (bf16[64,1024]{1,0:T(8,128)(2,1)S(1)}, bf16[64,1024]{1,0:T(8,128)(2,1)S(1)}, u32[]{:S(2)}, u32[]{:S(2)}) collective-permute-start(bf16[64,1024]{1,0:T(8,128)(2,1)S(1)} %bitcast.57), channel_id=1, source_target_pairs={{16,0},{24,8},{0,16},{8,24},{17,1},{25,9},{1,17},{9,25},{18,2},{26... | collective-permute-start | bytes 393224 | tf_op jit(solution)/shard_map/ppermute | solution.py:28
  16.7 22.3 %all-to-all-start.1 = ((bf16[64,2,640]{2,1,0:T(2,128)(2,1)}), bf16[64,2,640]{2,1,0:T(2,128)(2,1)S(1)}, u32[]{:S(2)}, u32[]{:S(2)}) async-start(bf16[64,2,640]{2,1,0:T(2,128)(2,1)} %send_rows.2.after), calls=%async_computation.1 | async-start | bytes 327680 | tf_op jit(solution)/shard_map/all_to_all | solution.py:19
  29.1 16.2 %collective-permute-start.3 = (bf16[64,1024]{1,0:T(8,128)(2,1)S(1)}, bf16[64,1024]{1,0:T(8,128)(2,1)S(1)}, u32[]{:S(2)}, u32[]{:S(2)}) collective-permute-start(bf16[64,1024]{1,0:T(8,128)(2,1)S(1)} %collective-permute-done.2), channel_id=1, source_target_pairs={{0,64},{64,0},{1,65},{65,1},{2,66},{66,2},{3,67},{67,3},{4,68},{68... | collective-permute-start | bytes 393224 | tf_op jit(solution)/shard_map/ppermute | solution.py:32
  40.0 0.9 copy-start.2
  40.7 18.3 %copy-start.5 = (s32[8,64]{1,0:T(8,128)S(1)}, s32[8,64]{1,0:T(8,128)}, u32[]{:S(2)}) copy-start(s32[8,64]{1,0:T(8,128)} %get-tuple-element.55) | copy-start | bytes 6148
  41.6 12.2 %all-to-all-start.2 = ((bf16[16,8,1024]{2,1,0:T(8,128)(2,1)}), bf16[16,8,1024]{2,1,0:T(8,128)(2,1)S(1)}, u32[]{:S(2)}, u32[]{:S(2)}) async-start(bf16[16,8,1024]{2,1,0:T(8,128)(2,1)} %broadcast_in_dim.31), calls=%async_computation.2 | async-start | bytes 524288 | tf_op jit(solution)/shard_map/all_to_all | solution.py:19
  45.2 42.1 %copy-start.6 = (s32[8]{0:T(128)S(1)}, s32[8]{0:T(128)}, u32[]{:S(2)}) copy-start(s32[8]{0:T(128)} %param.14) | copy-start | bytes 100
  55.4 12.2 %all-to-all-start.3 = ((bf16[16,8,1024]{2,1,0:T(8,128)(2,1)}), bf16[16,8,1024]{2,1,0:T(8,128)(2,1)S(1)}, u32[]{:S(2)}, u32[]{:S(2)}) async-start(bf16[16,8,1024]{2,1,0:T(8,128)(2,1)} %fusion.6), calls=%async_computation.3 | async-start | bytes 524288 | tf_op jit(solution)/shard_map/all_to_all | solution.py:19
  69.2 16.9 %all-to-all-start.4 = ((f32[64,1,256]{2,1,0:T(1,128)}), f32[64,1,256]{2,1,0:T(1,128)S(1)}, u32[]{:S(2)}, u32[]{:S(2)}) async-start(f32[64,1,256]{2,1,0:T(1,128)} %copy.45), calls=%async_computation.4 | async-start | bytes 131072 | tf_op jit(solution)/shard_map/all_to_all | solution.py:19
  87.9 5.9 %collective-permute-start.4 = (f32[16]{0:T(128)S(1)}, f32[16]{0:T(128)S(1)}, u32[]{:S(2)}, u32[]{:S(2)}) collective-permute-start(f32[16]{0:T(128)S(1)} %multiply_reduce_fusion.3), channel_id=1, source_target_pairs={{0,64},{64,0},{1,65},{65,1},{2,66},{66,2},{3,67},{67,3},{4,68},{68... | collective-permute-start | bytes 200 | tf_op jit(solution)/shard_map/ppermute | solution.py:32
  93.8 2.4 %collective-permute-start.5 = (f32[16]{0:T(128)S(1)}, f32[16]{0:T(128)S(1)}, u32[]{:S(2)}, u32[]{:S(2)}) collective-permute-start(f32[16]{0:T(128)S(1)} %add.62), channel_id=1, source_target_pairs={{0,128},{128,0},{1,129},{129,1},{2,130},{130,2},{3,131},{131,3},{4... | collective-permute-start | bytes 200 | tf_op jit(solution)/shard_map/ppermute | solution.py:32

commit v12 on v11

--- a/solution.py
+++ b/solution.py
@@ -90,8 +90,7 @@
     least = (exact - high - middle).astype(jnp.bfloat16).astype(jnp.float32)
     parts = high + pltpu.roll(middle, share, 1) + pltpu.roll(least, 2 * share, 1)
     row_of = lax.broadcasted_iota(jnp.int32, parts.shape, 0)
-    lane = lax.broadcasted_iota(jnp.int32, parts.shape, 1)
-    slot_at = (row_of == 1) & (lane == 0)
+    slot_at = row_of == 1
     blank = jnp.where(slot_at, -1.0, parts)[0:2]
     sent[:, :, 0:half] = jnp.zeros((peers, 2, half), sent.dtype)
     sent[:, :, half:] = jnp.broadcast_to(blank[None], (peers, 2, LANES)).astype(sent.dtype)
@@ -222,7 +221,7 @@
     half = width // 2
 
     def taken(got):
-        picks = got[:, 1, half : half + 1].astype(f32) == jnp.arange(slots, dtype=f32)[None]
+        picks = got[:, 1, half : half + slots].astype(f32) == jnp.arange(slots, dtype=f32)[None]
         rows = jnp.concatenate([got[:, 0, :half], got[:, 1, :half]], axis=1)
         return lax.dot_general(
             picks.astype(bf16), rows, (((0,), (0,)), ((), ())), preferred_element_type=f32
@@ -269,8 +268,8 @@
     diff = jax.nn.sigmoid(scores) - labels.astype(f32)
     pooled = jnp.mean(encoded.reshape(share, toks // seq_len, seq_len), axis=2)
     grad = jnp.sum(diff[None] * pooled, axis=1)
-    grad = grad + swapped(grad, "core")
-    grad = grad + swapped(grad, "yl")
+    across = lax.ppermute(grad, DP, [(0, 3), (1, 2), (2, 1), (3, 0)])
+    grad = (grad + swapped(grad, "core")) + (swapped(grad, "yl") + across)
     return encoded.T.astype(bf16), scores, grad
 
 

time: 97.2 us -> 97 us (level)
  starting transfers between devices: 40.7 us -> 41.8 us
  waiting for transfers between devices: 37.9 us -> 36.9 us
    ppermute x0 -> x1, starting transfers between devices: none -> 5.85 us  [on_device(): across = lax.ppermute(grad, DP, [(0, 3), (1, 2), (2, 1), (3, 0)])]
    ppermute x3, starting transfers between devices: 7.47 us -> 2.81 us  [swapped(): return lax.ppermute(array, axis, [(0, 1), (1, 0)])]
    ppermute x3, waiting for transfers between devices: 2.21 us -> 0.01 us  [swapped(): return lax.ppermute(array, axis, [(0, 1), (1, 0)])]
    ppermute x0 -> x1, waiting for transfers between devices: none -> 1.22 us  [on_device(): across = lax.ppermute(grad, DP, [(0, 3), (1, 2), (2, 1), (3, 0)])]
  transfers between devices with their start and end apart: 10 -> 11, of which waited for: 6 -> 5; matrix products, arithmetic and copies ran while one was open for 3% -> 2% of each run, Pallas kernels for 7% -> 7%
where the time goes in v12:
time: 97 us; the launch traced here: 96.3 us
  starting transfers between devices  41.8 us (43%)
  waiting for transfers between devices  36.9 us (38%)
  Pallas kernels  7.02 us (7%)
  other arithmetic  4.11 us (4%)
  local copies, waits for them, and re-layouts  2.86 us (3%)
  matrix products  2.03 us (2%)
    all_to_all x4, waiting for transfers between devices, exchange(): return lax.all_to_all(blocks, axes, split_axis=0, concat_axis=0, tiled=True)  35.7 us
    all_to_all x4, starting transfers between devices, exchange(): return lax.all_to_all(blocks, axes, split_axis=0, concat_axis=0, tiled=True)  22.9 us
    ppermute x3, starting transfers between devices, moved(): lax.ppermute(array, axis, [((i + step) % peers, i) for i in range(peers)])  10.3 us
    ppermute x1, starting transfers between devices, on_device(): across = lax.ppermute(grad, DP, [(0, 3), (1, 2), (2, 1), (3, 0)])  5.85 us
    pallas_call x1, Pallas kernels, to_send(): pl.pallas_call(functools.partial(send_kernel, peers), out_shape=jax.Shape...  4.82 us
    ppermute x3, starting transfers between devices, swapped(): return lax.ppermute(array, axis, [(0, 1), (1, 0)])  2.81 us
    pallas_call x1, Pallas kernels, positions(): pl.pallas_call(functools.partial(position_kernel, entries, peers), out_sh...  2.2 us
  transfers between devices with their start and end apart: 11, of which 5 were waited for; matrix products, arithmetic and copies ran while one was open for 2% of the time, Pallas kernels for 7%

profile of v12, /device:TPU:1, one launch (start us, length us, event | category | flops | bytes accessed | tf_op | source)
XLA Modules:
  0.0 96.3 jit_solution(3591381613743188959)
XLA Ops:
  0.7 1.0 %pad_maximum_fusion = bf16[128,1024]{1,0:T(8,128)(2,1)S(1)} fusion(bf16[64,1024]{1,0:T(8,128)(2,1)} %param.17, bf16[64,1024]{1,0:T(8,128)(2,1)} %bitcast.65), kind=kLoop, calls=%fused_computation.16 | loop fusion | flops 524288 | bytes 524288 | tf_op jit(solution)/shard_map/concatenate | solution.py:204
  1.7 6.9 %collective-permute-start = (bf16[128,1024]{1,0:T(8,128)(2,1)S(1)}, bf16[128,1024]{1,0:T(8,128)(2,1)S(1)}, u32[]{:S(2)}, u32[]{:S(2)}) collective-permute-start(bf16[128,1024]{1,0:T(8,128)(2,1)S(1)} %pad_maximum_fusion), channel_id=1, source_target_pairs={{8,0},{16,8},{24,16},{0,24},{9,1},{17,9},{25,17},{1,25},{10,2},{18... | collective-permute-start | bytes 786440 | tf_op jit(solution)/shard_map/ppermute | solution.py:28
  8.6 3.3 %collective-permute-start.2 = (bf16[64,1024]{1,0:T(8,128)(2,1)S(1)}, bf16[64,1024]{1,0:T(8,128)(2,1)S(1)}, u32[]{:S(2)}, u32[]{:S(2)}) collective-permute-start(bf16[64,1024]{1,0:T(8,128)(2,1)S(1)} %bitcast.62), channel_id=1, source_target_pairs={{16,0},{24,8},{0,16},{8,24},{17,1},{25,9},{1,17},{9,25},{18,2},{26... | collective-permute-start | bytes 393224 | tf_op jit(solution)/shard_map/ppermute | solution.py:28
  12.0 4.8 %send_rows.2.after = bf16[64,2,640]{2,1,0:T(2,128)(2,1)} custom-call(s32[1]{0:T(128)} %bitcast.5.place_ref, s32[1]{0:T(128)} %constant.33.clone.1.trip_ref, s32[3,8]{1,0:T(4,128)} %bitcast.66, s32[8,61]{1,0:T(8,128)} %words_v.1, f32[1,16]{1,0:T(1,128)} %bitcast.70, f32[1,16]{1,0:T(1,128)} %bitcast.73, bf16[2048,1024]{1,0:T(8,128)(2,1)} %table.1), custom_call_target="tpu_custom_call" | custom-call | tf_op jit(solution)/shard_map/send_rows/pallas_call | solution.py:120
  16.8 9.9 %all-to-all-start.1 = ((bf16[64,2,640]{2,1,0:T(2,128)(2,1)}), bf16[64,2,640]{2,1,0:T(2,128)(2,1)S(1)}, u32[]{:S(2)}, u32[]{:S(2)}) async-start(bf16[64,2,640]{2,1,0:T(2,128)(2,1)} %send_rows.2.after), calls=%async_computation.1 | async-start | bytes 327680 | tf_op jit(solution)/shard_map/all_to_all | solution.py:19
  26.8 2.2 %positions.1 = (s32[8,64]{1,0:T(8,128)}, s32[1]{0:T(128)}) custom-call(s32[3,8]{1,0:T(4,128)S(1)} %bitcast.67, s32[8,61]{1,0:T(8,128)S(1)} %copy-done, s32[8,61]{1,0:T(8,128)S(1)} %copy-done, bf16[64,2,640]{2,1,0:T(2,128)(2,1)} %send_rows.2.after), custom_call_target="tpu_custom_call" | custom-call | bytes 40000000 | tf_op jit(solution)/shard_map/positions/pallas_call | solution.py:168
  29.0 2.0 %collective-permute-start.3 = (bf16[64,1024]{1,0:T(8,128)(2,1)S(1)}, bf16[64,1024]{1,0:T(8,128)(2,1)S(1)}, u32[]{:S(2)}, u32[]{:S(2)}) collective-permute-start(bf16[64,1024]{1,0:T(8,128)(2,1)S(1)} %collective-permute-done.2), channel_id=1, source_target_pairs={{0,64},{64,0},{1,65},{65,1},{2,66},{66,2},{3,67},{67,3},{4,68},{68... | collective-permute-start | bytes 393224 | tf_op jit(solution)/shard_map/ppermute | solution.py:32
  31.1 7.8 %all-to-all-done.1 = bf16[64,2,640]{2,1,0:T(2,128)(2,1)S(1)} async-done(((bf16[64,2,640]{2,1,0:T(2,128)(2,1)}), bf16[64,2,640]{2,1,0:T(2,128)(2,1)S(1)}, u32[]{:S(2)}, u32[]{:S(2)}) %all-to-all-start.1) | async-done | bytes 163872 | tf_op jit(solution)/shard_map/all_to_all | solution.py:19
  39.3 0.7 while.10
  40.3 0.7 broadcast_in_dim.31
  41.1 3.5 %all-to-all-start.2 = ((bf16[16,8,1024]{2,1,0:T(8,128)(2,1)}), bf16[16,8,1024]{2,1,0:T(8,128)(2,1)S(1)}, u32[]{:S(2)}, u32[]{:S(2)}) async-start(bf16[16,8,1024]{2,1,0:T(8,128)(2,1)} %broadcast_in_dim.31), calls=%async_computation.2 | async-start | bytes 524288 | tf_op jit(solution)/shard_map/all_to_all | solution.py:19
  44.7 8.6 %all-to-all-done.2 = bf16[16,8,1024]{2,1,0:T(8,128)(2,1)S(1)} async-done(((bf16[16,8,1024]{2,1,0:T(8,128)(2,1)}), bf16[16,8,1024]{2,1,0:T(8,128)(2,1)S(1)}, u32[]{:S(2)}, u32[]{:S(2)}) %all-to-all-start.2) | async-done | bytes 262176 | tf_op jit(solution)/shard_map/all_to_all | solution.py:19
  53.3 1.6 %fusion.4 = bf16[16,8,1024]{2,1,0:T(8,128)(2,1)} fusion(bf16[256,1024]{1,0:T(8,128)(2,1)S(1)} %get-tuple-element.95, bf16[256,1024]{1,0:T(8,128)(2,1)S(1)} %get-tuple-element.94, bf16[16,8,1024]{2,1,0:T(8,128)(2,1)S(1)} %all-to-all-done.2), kind=kOutput, calls=%fused_computation.10 | convolution fusion | flops 136478720 | bytes 1572864 | tf_op jit(solution)/shard_map/dot_general | solution.py:248
  54.9 3.5 %all-to-all-start.3 = ((bf16[16,8,1024]{2,1,0:T(8,128)(2,1)}), bf16[16,8,1024]{2,1,0:T(8,128)(2,1)S(1)}, u32[]{:S(2)}, u32[]{:S(2)}) async-start(bf16[16,8,1024]{2,1,0:T(8,128)(2,1)} %fusion.4), calls=%async_computation.3 | async-start | bytes 524288 | tf_op jit(solution)/shard_map/all_to_all | solution.py:19
  58.8 8.3 %all-to-all-done.3 = bf16[16,8,1024]{2,1,0:T(8,128)(2,1)S(1)} async-done(((bf16[16,8,1024]{2,1,0:T(8,128)(2,1)}), bf16[16,8,1024]{2,1,0:T(8,128)(2,1)S(1)}, u32[]{:S(2)}, u32[]{:S(2)}) %all-to-all-start.3) | async-done | bytes 262176 | tf_op jit(solution)/shard_map/all_to_all | solution.py:19
  67.9 0.7 copy.45
  68.6 5.9 %all-to-all-start.4 = ((f32[64,1,256]{2,1,0:T(1,128)}), f32[64,1,256]{2,1,0:T(1,128)S(1)}, u32[]{:S(2)}, u32[]{:S(2)}) async-start(f32[64,1,256]{2,1,0:T(1,128)} %copy.45), calls=%async_computation.4 | async-start | bytes 131072 | tf_op jit(solution)/shard_map/all_to_all | solution.py:19
  74.7 10.9 %all-to-all-done.4 = f32[64,1,256]{2,1,0:T(1,128)S(1)} async-done(((f32[64,1,256]{2,1,0:T(1,128)}), f32[64,1,256]{2,1,0:T(1,128)S(1)}, u32[]{:S(2)}, u32[]{:S(2)}) %all-to-all-start.4) | async-done | bytes 65568 | tf_op jit(solution)/shard_map/all_to_all | solution.py:19
  86.3 0.6 convert_bitcast_fusion
  87.4 0.5 fusion.62
  88.0 0.8 collective-permute-start.5
  88.7 5.8 %collective-permute-start.6 = (f32[16]{0:T(128)S(1)}, f32[16]{0:T(128)S(1)}, u32[]{:S(2)}, u32[]{:S(2)}) collective-permute-start(f32[16]{0:T(128)S(1)} %multiply_reduce_fusion.3), channel_id=1, source_target_pairs={{0,192},{64,128},{128,64},{192,0},{1,193},{65,129},{129,65},{193,1... | collective-permute-start | bytes 200 | tf_op jit(solution)/shard_map/ppermute | solution.py:271
  94.6 1.2 %collective-permute-done.6 = f32[16]{0:T(128)S(1)} collective-permute-done((f32[16]{0:T(128)S(1)}, f32[16]{0:T(128)S(1)}, u32[]{:S(2)}, u32[]{:S(2)}) %collective-permute-start.6) | collective-permute-done | bytes 96 | tf_op jit(solution)/shard_map/ppermute | solution.py:271
  95.8 0.5 add_add_fusion
  (65 shorter events, 3.4 us)
Async XLA Ops:
  0.6 26.1 %copy-start.1 = (s32[8,3]{0,1:T(4,128)S(1)}, s32[8,3]{0,1:T(4,128)}, u32[]{:S(2)}) copy-start(s32[8,3]{0,1:T(4,128)} %param.12) | copy-start | bytes 292
  0.6 26.1 %copy-start = (s32[8,61]{1,0:T(8,128)S(1)}, s32[8,61]{1,0:T(8,128)}, u32[]{:S(2)}) copy-start(s32[8,61]{1,0:T(8,128)} %words_v.1) | copy-start | bytes 5860
  0.7 38.7 %copy-start.3 = (f32[16]{0:T(128)S(1)}, f32[16]{0:T(128)}, u32[]{:S(2)}) copy-start(f32[16]{0:T(128)} %param.18) | copy-start | bytes 196
  0.7 38.7 %copy-start.4 = (f32[16]{0:T(128)S(1)}, f32[16]{0:T(128)}, u32[]{:S(2)}) copy-start(f32[16]{0:T(128)} %param.19) | copy-start | bytes 196
  1.7 29.4 %collective-permute-start = (bf16[128,1024]{1,0:T(8,128)(2,1)S(1)}, bf16[128,1024]{1,0:T(8,128)(2,1)S(1)}, u32[]{:S(2)}, u32[]{:S(2)}) collective-permute-start(bf16[128,1024]{1,0:T(8,128)(2,1)S(1)} %pad_maximum_fusion), channel_id=1, source_target_pairs={{8,0},{16,8},{24,16},{0,24},{9,1},{17,9},{25,17},{1,25},{10,2},{18... | collective-permute-start | bytes 786440 | tf_op jit(solution)/shard_map/ppermute | solution.py:28
  8.6 36.0 %collective-permute-start.1 = (bf16[128,1024]{1,0:T(8,128)(2,1)S(1)}, bf16[128,1024]{1,0:T(8,128)(2,1)S(1)}, u32[]{:S(2)}, u32[]{:S(2)}) collective-permute-start(bf16[128,1024]{1,0:T(8,128)(2,1)S(1)} %pad_maximum_fusion), channel_id=1, source_target_pairs={{24,0},{0,8},{8,16},{16,24},{25,1},{1,9},{9,17},{17,25},{26,2},{2,... | collective-permute-start | bytes 786440 | tf_op jit(solution)/shard_map/ppermute | solution.py:28
  8.6 20.4 %collective-permute-start.2 = (bf16[64,1024]{1,0:T(8,128)(2,1)S(1)}, bf16[64,1024]{1,0:T(8,128)(2,1)S(1)}, u32[]{:S(2)}, u32[]{:S(2)}) collective-permute-start(bf16[64,1024]{1,0:T(8,128)(2,1)S(1)} %bitcast.62), channel_id=1, source_target_pairs={{16,0},{24,8},{0,16},{8,24},{17,1},{25,9},{1,17},{9,25},{18,2},{26... | collective-permute-start | bytes 393224 | tf_op jit(solution)/shard_map/ppermute | solution.py:28
  16.8 22.1 %all-to-all-start.1 = ((bf16[64,2,640]{2,1,0:T(2,128)(2,1)}), bf16[64,2,640]{2,1,0:T(2,128)(2,1)S(1)}, u32[]{:S(2)}, u32[]{:S(2)}) async-start(bf16[64,2,640]{2,1,0:T(2,128)(2,1)} %send_rows.2.after), calls=%async_computation.1 | async-start | bytes 327680 | tf_op jit(solution)/shard_map/all_to_all | solution.py:19
  29.0 15.7 %collective-permute-start.3 = (bf16[64,1024]{1,0:T(8,128)(2,1)S(1)}, bf16[64,1024]{1,0:T(8,128)(2,1)S(1)}, u32[]{:S(2)}, u32[]{:S(2)}) collective-permute-start(bf16[64,1024]{1,0:T(8,128)(2,1)S(1)} %collective-permute-done.2), channel_id=1, source_target_pairs={{0,64},{64,0},{1,65},{65,1},{2,66},{66,2},{3,67},{67,3},{4,68},{68... | collective-permute-start | bytes 393224 | tf_op jit(solution)/shard_map/ppermute | solution.py:32
  39.3 0.9 copy-start.2
  40.1 18.3 %copy-start.5 = (s32[8,64]{1,0:T(8,128)S(1)}, s32[8,64]{1,0:T(8,128)}, u32[]{:S(2)}) copy-start(s32[8,64]{1,0:T(8,128)} %get-tuple-element.55) | copy-start | bytes 6148
  41.1 12.2 %all-to-all-start.2 = ((bf16[16,8,1024]{2,1,0:T(8,128)(2,1)}), bf16[16,8,1024]{2,1,0:T(8,128)(2,1)S(1)}, u32[]{:S(2)}, u32[]{:S(2)}) async-start(bf16[16,8,1024]{2,1,0:T(8,128)(2,1)} %broadcast_in_dim.31), calls=%async_computation.2 | async-start | bytes 524288 | tf_op jit(solution)/shard_map/all_to_all | solution.py:19
  44.6 42.8 %copy-start.6 = (s32[8]{0:T(128)S(1)}, s32[8]{0:T(128)}, u32[]{:S(2)}) copy-start(s32[8]{0:T(128)} %param.14) | copy-start | bytes 100
  54.9 12.2 %all-to-all-start.3 = ((bf16[16,8,1024]{2,1,0:T(8,128)(2,1)}), bf16[16,8,1024]{2,1,0:T(8,128)(2,1)S(1)}, u32[]{:S(2)}, u32[]{:S(2)}) async-start(bf16[16,8,1024]{2,1,0:T(8,128)(2,1)} %fusion.4), calls=%async_computation.3 | async-start | bytes 524288 | tf_op jit(solution)/shard_map/all_to_all | solution.py:19
  68.6 17.0 %all-to-all-start.4 = ((f32[64,1,256]{2,1,0:T(1,128)}), f32[64,1,256]{2,1,0:T(1,128)S(1)}, u32[]{:S(2)}, u32[]{:S(2)}) async-start(f32[64,1,256]{2,1,0:T(1,128)} %copy.45), calls=%async_computation.4 | async-start | bytes 131072 | tf_op jit(solution)/shard_map/all_to_all | solution.py:19
  88.0 6.6 %collective-permute-start.5 = (f32[16]{0:T(128)S(1)}, f32[16]{0:T(128)S(1)}, u32[]{:S(2)}, u32[]{:S(2)}) collective-permute-start(f32[16]{0:T(128)S(1)} %multiply_reduce_fusion.3), channel_id=1, source_target_pairs={{0,128},{128,0},{1,129},{129,1},{2,130},{130,2},{3,131},{131,3},{4... | collective-permute-start | bytes 200 | tf_op jit(solution)/shard_map/ppermute | solution.py:32
  88.7 7.1 %collective-permute-start.6 = (f32[16]{0:T(128)S(1)}, f32[16]{0:T(128)S(1)}, u32[]{:S(2)}, u32[]{:S(2)}) collective-permute-start(f32[16]{0:T(128)S(1)} %multiply_reduce_fusion.3), channel_id=1, source_target_pairs={{0,192},{64,128},{128,64},{192,0},{1,193},{65,129},{129,65},{193,1... | collective-permute-start | bytes 200 | tf_op jit(solution)/shard_map/ppermute | solution.py:271
  94.6 1.2 %collective-permute-start.4 = (f32[16]{0:T(128)S(1)}, f32[16]{0:T(128)S(1)}, u32[]{:S(2)}, u32[]{:S(2)}) collective-permute-start(f32[16]{0:T(128)S(1)} %multiply_reduce_fusion.3), channel_id=1, source_target_pairs={{0,64},{64,0},{1,65},{65,1},{2,66},{66,2},{3,67},{67,3},{4,68},{68... | collective-permute-start | bytes 200 | tf_op jit(solution)/shard_map/ppermute | solution.py:32

commit v13 on v12

--- a/solution.py
+++ b/solution.py
@@ -253,10 +253,10 @@
 
     blocks = level.reshape(slots, peers, share).transpose(1, 0, 2).reshape(peers, 1, -1)
     score = jnp.broadcast_to(jnp.pad(score, (0, LANES - slots)), (peers, 1, LANES))
-    got = exchange(jnp.concatenate([blocks, score], axis=2), MP)
-    level = got[:, 0, : slots * share].reshape(peers, slots, share)
+    got = exchange(jnp.concatenate([blocks, score], axis=1), MP)
+    level = got[:, 0].reshape(peers, slots, share)
     by_spot = (level * out_gain).astype(bf16).transpose(1, 0, 2).reshape(toks, share)
-    score = got[:, 0, slots * share :][:, :slots].T.reshape(1, toks)
+    score = got[:, 1, :slots].T.reshape(1, toks)
     spot = spot.reshape(1, toks)
     where = spot == jnp.arange(toks)[:, None]
     encoded = lax.dot_general(

time: 97 us -> 97 us (level)
  no operation moved by 1% of the time
where the time goes in v13:
time: 97 us; the launch traced here: 96.3 us
  starting transfers between devices  41.9 us (43%)
  waiting for transfers between devices  37.1 us (38%)
  Pallas kernels  6.7 us (7%)
  other arithmetic  4.03 us (4%)
  local copies, waits for them, and re-layouts  2.95 us (3%)
  matrix products  2.02 us (2%)
    all_to_all x4, waiting for transfers between devices, exchange(): return lax.all_to_all(blocks, axes, split_axis=0, concat_axis=0, tiled=True)  35.8 us
    all_to_all x4, starting transfers between devices, exchange(): return lax.all_to_all(blocks, axes, split_axis=0, concat_axis=0, tiled=True)  23.2 us
    ppermute x3, starting transfers between devices, moved(): lax.ppermute(array, axis, [((i + step) % peers, i) for i in range(peers)])  10.3 us
    ppermute x1, starting transfers between devices, on_device(): across = lax.ppermute(grad, DP, [(0, 3), (1, 2), (2, 1), (3, 0)])  6.25 us
    pallas_call x1, Pallas kernels, to_send(): pl.pallas_call(functools.partial(send_kernel, peers), out_shape=jax.Shape...  4.5 us
    pallas_call x1, Pallas kernels, positions(): pl.pallas_call(functools.partial(position_kernel, entries, peers), out_sh...  2.2 us
    ppermute x3, starting transfers between devices, swapped(): return lax.ppermute(array, axis, [(0, 1), (1, 0)])  2.17 us
  transfers between devices with their start and end apart: 11, of which 5 were waited for; matrix products, arithmetic and copies ran while one was open for 2% of the time, Pallas kernels for 7%

profile of v13, /device:TPU:1, one launch (start us, length us, event | category | flops | bytes accessed | tf_op | source)
XLA Modules:
  0.0 96.3 jit_solution(5684250919392941582)
XLA Ops:
  0.7 1.0 %pad_maximum_fusion = bf16[128,1024]{1,0:T(8,128)(2,1)S(1)} fusion(bf16[64,1024]{1,0:T(8,128)(2,1)} %param.17, bf16[64,1024]{1,0:T(8,128)(2,1)} %bitcast.65), kind=kLoop, calls=%fused_computation.16 | loop fusion | flops 524288 | bytes 524288 | tf_op jit(solution)/shard_map/concatenate | solution.py:204
  1.7 6.9 %collective-permute-start = (bf16[128,1024]{1,0:T(8,128)(2,1)S(1)}, bf16[128,1024]{1,0:T(8,128)(2,1)S(1)}, u32[]{:S(2)}, u32[]{:S(2)}) collective-permute-start(bf16[128,1024]{1,0:T(8,128)(2,1)S(1)} %pad_maximum_fusion), channel_id=1, source_target_pairs={{8,0},{16,8},{24,16},{0,24},{9,1},{17,9},{25,17},{1,25},{10,2},{18... | collective-permute-start | bytes 786440 | tf_op jit(solution)/shard_map/ppermute | solution.py:28
  8.6 3.3 %collective-permute-start.2 = (bf16[64,1024]{1,0:T(8,128)(2,1)S(1)}, bf16[64,1024]{1,0:T(8,128)(2,1)S(1)}, u32[]{:S(2)}, u32[]{:S(2)}) collective-permute-start(bf16[64,1024]{1,0:T(8,128)(2,1)S(1)} %bitcast.62), channel_id=1, source_target_pairs={{16,0},{24,8},{0,16},{8,24},{17,1},{25,9},{1,17},{9,25},{18,2},{26... | collective-permute-start | bytes 393224 | tf_op jit(solution)/shard_map/ppermute | solution.py:28
  12.0 4.5 %send_rows.2.after = bf16[64,2,640]{2,1,0:T(2,128)(2,1)} custom-call(s32[1]{0:T(128)} %bitcast.5.place_ref, s32[1]{0:T(128)} %constant.33.clone.1.trip_ref, s32[3,8]{1,0:T(4,128)} %bitcast.66, s32[8,61]{1,0:T(8,128)} %words_v.1, f32[1,16]{1,0:T(1,128)} %bitcast.70, f32[1,16]{1,0:T(1,128)} %bitcast.73, bf16[2048,1024]{1,0:T(8,128)(2,1)} %table.1), custom_call_target="tpu_custom_call" | custom-call | tf_op jit(solution)/shard_map/send_rows/pallas_call | solution.py:120
  16.5 10.2 %all-to-all-start.1 = ((bf16[64,2,640]{2,1,0:T(2,128)(2,1)}), bf16[64,2,640]{2,1,0:T(2,128)(2,1)S(1)}, u32[]{:S(2)}, u32[]{:S(2)}) async-start(bf16[64,2,640]{2,1,0:T(2,128)(2,1)} %send_rows.2.after), calls=%async_computation.1 | async-start | bytes 327680 | tf_op jit(solution)/shard_map/all_to_all | solution.py:19
  26.7 2.2 %positions.1 = (s32[8,64]{1,0:T(8,128)}, s32[1]{0:T(128)}) custom-call(s32[3,8]{1,0:T(4,128)S(1)} %bitcast.67, s32[8,61]{1,0:T(8,128)S(1)} %copy-done, s32[8,61]{1,0:T(8,128)S(1)} %copy-done, bf16[64,2,640]{2,1,0:T(2,128)(2,1)} %send_rows.2.after), custom_call_target="tpu_custom_call" | custom-call | bytes 40000000 | tf_op jit(solution)/shard_map/positions/pallas_call | solution.py:168
  28.9 1.9 %collective-permute-start.3 = (bf16[64,1024]{1,0:T(8,128)(2,1)S(1)}, bf16[64,1024]{1,0:T(8,128)(2,1)S(1)}, u32[]{:S(2)}, u32[]{:S(2)}) collective-permute-start(bf16[64,1024]{1,0:T(8,128)(2,1)S(1)} %collective-permute-done.2), channel_id=1, source_target_pairs={{0,64},{64,0},{1,65},{65,1},{2,66},{66,2},{3,67},{67,3},{4,68},{68... | collective-permute-start | bytes 393224 | tf_op jit(solution)/shard_map/ppermute | solution.py:32
  30.8 8.0 %all-to-all-done.1 = bf16[64,2,640]{2,1,0:T(2,128)(2,1)S(1)} async-done(((bf16[64,2,640]{2,1,0:T(2,128)(2,1)}), bf16[64,2,640]{2,1,0:T(2,128)(2,1)S(1)}, u32[]{:S(2)}, u32[]{:S(2)}) %all-to-all-start.1) | async-done | bytes 163872 | tf_op jit(solution)/shard_map/all_to_all | solution.py:19
  39.2 0.7 while.10
  40.2 0.7 broadcast_in_dim.31
  40.9 3.5 %all-to-all-start.2 = ((bf16[16,8,1024]{2,1,0:T(8,128)(2,1)}), bf16[16,8,1024]{2,1,0:T(8,128)(2,1)S(1)}, u32[]{:S(2)}, u32[]{:S(2)}) async-start(bf16[16,8,1024]{2,1,0:T(8,128)(2,1)} %broadcast_in_dim.31), calls=%async_computation.2 | async-start | bytes 524288 | tf_op jit(solution)/shard_map/all_to_all | solution.py:19
  44.6 8.6 %all-to-all-done.2 = bf16[16,8,1024]{2,1,0:T(8,128)(2,1)S(1)} async-done(((bf16[16,8,1024]{2,1,0:T(8,128)(2,1)}), bf16[16,8,1024]{2,1,0:T(8,128)(2,1)S(1)}, u32[]{:S(2)}, u32[]{:S(2)}) %all-to-all-start.2) | async-done | bytes 262176 | tf_op jit(solution)/shard_map/all_to_all | solution.py:19
  53.2 1.6 %fusion.4 = bf16[16,8,1024]{2,1,0:T(8,128)(2,1)} fusion(bf16[256,1024]{1,0:T(8,128)(2,1)S(1)} %get-tuple-element.95, bf16[256,1024]{1,0:T(8,128)(2,1)S(1)} %get-tuple-element.94, bf16[16,8,1024]{2,1,0:T(8,128)(2,1)S(1)} %all-to-all-done.2), kind=kOutput, calls=%fused_computation.10 | convolution fusion | flops 136478720 | bytes 1572864 | tf_op jit(solution)/shard_map/dot_general | solution.py:248
  54.7 3.5 %all-to-all-start.3 = ((bf16[16,8,1024]{2,1,0:T(8,128)(2,1)}), bf16[16,8,1024]{2,1,0:T(8,128)(2,1)S(1)}, u32[]{:S(2)}, u32[]{:S(2)}) async-start(bf16[16,8,1024]{2,1,0:T(8,128)(2,1)} %fusion.4), calls=%async_computation.3 | async-start | bytes 524288 | tf_op jit(solution)/shard_map/all_to_all | solution.py:19
  58.6 8.3 %all-to-all-done.3 = bf16[16,8,1024]{2,1,0:T(8,128)(2,1)S(1)} async-done(((bf16[16,8,1024]{2,1,0:T(8,128)(2,1)}), bf16[16,8,1024]{2,1,0:T(8,128)(2,1)S(1)}, u32[]{:S(2)}, u32[]{:S(2)}) %all-to-all-start.3) | async-done | bytes 262176 | tf_op jit(solution)/shard_map/all_to_all | solution.py:19
  67.8 0.7 copy.45
  68.5 6.0 %all-to-all-start.4 = ((f32[64,2,128]{2,1,0:T(2,128)}), f32[64,2,128]{2,1,0:T(2,128)S(1)}, u32[]{:S(2)}, u32[]{:S(2)}) async-start(f32[64,2,128]{2,1,0:T(2,128)} %copy.45), calls=%async_computation.4 | async-start | bytes 131072 | tf_op jit(solution)/shard_map/all_to_all | solution.py:19
  74.7 10.9 %all-to-all-done.4 = f32[64,2,128]{2,1,0:T(2,128)S(1)} async-done(((f32[64,2,128]{2,1,0:T(2,128)}), f32[64,2,128]{2,1,0:T(2,128)S(1)}, u32[]{:S(2)}, u32[]{:S(2)}) %all-to-all-start.4) | async-done | bytes 65568 | tf_op jit(solution)/shard_map/all_to_all | solution.py:19
  86.2 0.6 convert_bitcast_fusion
  87.4 0.5 fusion.62
  88.0 0.3 collective-permute-start.5
  88.3 6.3 %collective-permute-start.6 = (f32[16]{0:T(128)S(1)}, f32[16]{0:T(128)S(1)}, u32[]{:S(2)}, u32[]{:S(2)}) collective-permute-start(f32[16]{0:T(128)S(1)} %multiply_reduce_fusion.3), channel_id=1, source_target_pairs={{0,192},{64,128},{128,64},{192,0},{1,193},{65,129},{129,65},{193,1... | collective-permute-start | bytes 200 | tf_op jit(solution)/shard_map/ppermute | solution.py:271
  94.5 1.2 %collective-permute-done.6 = f32[16]{0:T(128)S(1)} collective-permute-done((f32[16]{0:T(128)S(1)}, f32[16]{0:T(128)S(1)}, u32[]{:S(2)}, u32[]{:S(2)}) %collective-permute-start.6) | collective-permute-done | bytes 96 | tf_op jit(solution)/shard_map/ppermute | solution.py:271
  95.8 0.5 add_add_fusion
  (66 shorter events, 3.4 us)
Async XLA Ops:
  0.6 26.0 %copy-start.1 = (s32[8,3]{0,1:T(4,128)S(1)}, s32[8,3]{0,1:T(4,128)}, u32[]{:S(2)}) copy-start(s32[8,3]{0,1:T(4,128)} %param.12) | copy-start | bytes 292
  0.6 26.0 %copy-start = (s32[8,61]{1,0:T(8,128)S(1)}, s32[8,61]{1,0:T(8,128)}, u32[]{:S(2)}) copy-start(s32[8,61]{1,0:T(8,128)} %words_v.1) | copy-start | bytes 5860
  0.7 38.6 %copy-start.3 = (f32[16]{0:T(128)S(1)}, f32[16]{0:T(128)}, u32[]{:S(2)}) copy-start(f32[16]{0:T(128)} %param.18) | copy-start | bytes 196
  0.7 38.5 %copy-start.4 = (f32[16]{0:T(128)S(1)}, f32[16]{0:T(128)}, u32[]{:S(2)}) copy-start(f32[16]{0:T(128)} %param.19) | copy-start | bytes 196
  1.7 29.1 %collective-permute-start = (bf16[128,1024]{1,0:T(8,128)(2,1)S(1)}, bf16[128,1024]{1,0:T(8,128)(2,1)S(1)}, u32[]{:S(2)}, u32[]{:S(2)}) collective-permute-start(bf16[128,1024]{1,0:T(8,128)(2,1)S(1)} %pad_maximum_fusion), channel_id=1, source_target_pairs={{8,0},{16,8},{24,16},{0,24},{9,1},{17,9},{25,17},{1,25},{10,2},{18... | collective-permute-start | bytes 786440 | tf_op jit(solution)/shard_map/ppermute | solution.py:28
  8.6 35.9 %collective-permute-start.1 = (bf16[128,1024]{1,0:T(8,128)(2,1)S(1)}, bf16[128,1024]{1,0:T(8,128)(2,1)S(1)}, u32[]{:S(2)}, u32[]{:S(2)}) collective-permute-start(bf16[128,1024]{1,0:T(8,128)(2,1)S(1)} %pad_maximum_fusion), channel_id=1, source_target_pairs={{24,0},{0,8},{8,16},{16,24},{25,1},{1,9},{9,17},{17,25},{26,2},{2,... | collective-permute-start | bytes 786440 | tf_op jit(solution)/shard_map/ppermute | solution.py:28
  8.6 20.3 %collective-permute-start.2 = (bf16[64,1024]{1,0:T(8,128)(2,1)S(1)}, bf16[64,1024]{1,0:T(8,128)(2,1)S(1)}, u32[]{:S(2)}, u32[]{:S(2)}) collective-permute-start(bf16[64,1024]{1,0:T(8,128)(2,1)S(1)} %bitcast.62), channel_id=1, source_target_pairs={{16,0},{24,8},{0,16},{8,24},{17,1},{25,9},{1,17},{9,25},{18,2},{26... | collective-permute-start | bytes 393224 | tf_op jit(solution)/shard_map/ppermute | solution.py:28
  16.5 22.3 %all-to-all-start.1 = ((bf16[64,2,640]{2,1,0:T(2,128)(2,1)}), bf16[64,2,640]{2,1,0:T(2,128)(2,1)S(1)}, u32[]{:S(2)}, u32[]{:S(2)}) async-start(bf16[64,2,640]{2,1,0:T(2,128)(2,1)} %send_rows.2.after), calls=%async_computation.1 | async-start | bytes 327680 | tf_op jit(solution)/shard_map/all_to_all | solution.py:19
  28.9 15.6 %collective-permute-start.3 = (bf16[64,1024]{1,0:T(8,128)(2,1)S(1)}, bf16[64,1024]{1,0:T(8,128)(2,1)S(1)}, u32[]{:S(2)}, u32[]{:S(2)}) collective-permute-start(bf16[64,1024]{1,0:T(8,128)(2,1)S(1)} %collective-permute-done.2), channel_id=1, source_target_pairs={{0,64},{64,0},{1,65},{65,1},{2,66},{66,2},{3,67},{67,3},{4,68},{68... | collective-permute-start | bytes 393224 | tf_op jit(solution)/shard_map/ppermute | solution.py:32
  39.2 0.9 copy-start.2
  39.9 18.3 %copy-start.5 = (s32[8,64]{1,0:T(8,128)S(1)}, s32[8,64]{1,0:T(8,128)}, u32[]{:S(2)}) copy-start(s32[8,64]{1,0:T(8,128)} %get-tuple-element.55) | copy-start | bytes 6148
  40.9 12.2 %all-to-all-start.2 = ((bf16[16,8,1024]{2,1,0:T(8,128)(2,1)}), bf16[16,8,1024]{2,1,0:T(8,128)(2,1)S(1)}, u32[]{:S(2)}, u32[]{:S(2)}) async-start(bf16[16,8,1024]{2,1,0:T(8,128)(2,1)} %broadcast_in_dim.31), calls=%async_computation.2 | async-start | bytes 524288 | tf_op jit(solution)/shard_map/all_to_all | solution.py:19
  44.5 42.9 %copy-start.6 = (s32[8]{0:T(128)S(1)}, s32[8]{0:T(128)}, u32[]{:S(2)}) copy-start(s32[8]{0:T(128)} %param.14) | copy-start | bytes 100
  54.7 12.2 %all-to-all-start.3 = ((bf16[16,8,1024]{2,1,0:T(8,128)(2,1)}), bf16[16,8,1024]{2,1,0:T(8,128)(2,1)S(1)}, u32[]{:S(2)}, u32[]{:S(2)}) async-start(bf16[16,8,1024]{2,1,0:T(8,128)(2,1)} %fusion.4), calls=%async_computation.3 | async-start | bytes 524288 | tf_op jit(solution)/shard_map/all_to_all | solution.py:19
  68.5 17.1 %all-to-all-start.4 = ((f32[64,2,128]{2,1,0:T(2,128)}), f32[64,2,128]{2,1,0:T(2,128)S(1)}, u32[]{:S(2)}, u32[]{:S(2)}) async-start(f32[64,2,128]{2,1,0:T(2,128)} %copy.45), calls=%async_computation.4 | async-start | bytes 131072 | tf_op jit(solution)/shard_map/all_to_all | solution.py:19
  88.0 6.6 %collective-permute-start.5 = (f32[16]{0:T(128)S(1)}, f32[16]{0:T(128)S(1)}, u32[]{:S(2)}, u32[]{:S(2)}) collective-permute-start(f32[16]{0:T(128)S(1)} %multiply_reduce_fusion.3), channel_id=1, source_target_pairs={{0,128},{128,0},{1,129},{129,1},{2,130},{130,2},{3,131},{131,3},{4... | collective-permute-start | bytes 200 | tf_op jit(solution)/shard_map/ppermute | solution.py:32
  88.3 7.5 %collective-permute-start.6 = (f32[16]{0:T(128)S(1)}, f32[16]{0:T(128)S(1)}, u32[]{:S(2)}, u32[]{:S(2)}) collective-permute-start(f32[16]{0:T(128)S(1)} %multiply_reduce_fusion.3), channel_id=1, source_target_pairs={{0,192},{64,128},{128,64},{192,0},{1,193},{65,129},{129,65},{193,1... | collective-permute-start | bytes 200 | tf_op jit(solution)/shard_map/ppermute | solution.py:271
  94.5 1.2 %collective-permute-start.4 = (f32[16]{0:T(128)S(1)}, f32[16]{0:T(128)S(1)}, u32[]{:S(2)}, u32[]{:S(2)}) collective-permute-start(f32[16]{0:T(128)S(1)} %multiply_reduce_fusion.3), channel_id=1, source_target_pairs={{0,64},{64,0},{1,65},{65,1},{2,66},{66,2},{3,67},{67,3},{4,68},{68... | collective-permute-start | bytes 200 | tf_op jit(solution)/shard_map/ppermute | solution.py:32

commit v14 on v13

--- a/solution.py
+++ b/solution.py
@@ -260,17 +260,17 @@
     spot = spot.reshape(1, toks)
     where = spot == jnp.arange(toks)[:, None]
     encoded = lax.dot_general(
-        by_spot, where.astype(bf16), (((0,), (0,)), ((), ())), preferred_element_type=f32
+        by_spot, where.astype(bf16), (((0,), (0,)), ((), ())), preferred_element_type=bf16
     )
     triple = jnp.arange(toks // seq_len)[:, None]
     of_triple = jnp.sum(jnp.where(where, jnp.arange(toks)[None] // seq_len, 0), axis=1)
     scores = jnp.sum(jnp.where(of_triple[None] == triple, score, 0.0), axis=1) / seq_len
     diff = jax.nn.sigmoid(scores) - labels.astype(f32)
-    pooled = jnp.mean(encoded.reshape(share, toks // seq_len, seq_len), axis=2)
+    pooled = jnp.mean(encoded.astype(f32).reshape(share, toks // seq_len, seq_len), axis=2)
     grad = jnp.sum(diff[None] * pooled, axis=1)
     across = lax.ppermute(grad, DP, [(0, 3), (1, 2), (2, 1), (3, 0)])
     grad = (grad + swapped(grad, "core")) + (swapped(grad, "yl") + across)
-    return encoded.T.astype(bf16), scores, grad
+    return encoded.T, scores, grad
 
 
 def solution(mesh):

time: 97 us -> 96.5 us (level)
  no operation moved by 1% of the time
where the time goes in v14:
time: 96.5 us; the launch traced here: 95.8 us
  starting transfers between devices  41.7 us (43%)
  waiting for transfers between devices  37.4 us (39%)
  Pallas kernels  6.6 us (7%)
  other arithmetic  3.41 us (4%)
  local copies, waits for them, and re-layouts  2.96 us (3%)
  matrix products  2.03 us (2%)
    all_to_all x4, waiting for transfers between devices, exchange(): return lax.all_to_all(blocks, axes, split_axis=0, concat_axis=0, tiled=True)  36.2 us
    all_to_all x4, starting transfers between devices, exchange(): return lax.all_to_all(blocks, axes, split_axis=0, concat_axis=0, tiled=True)  23.7 us
    ppermute x3, starting transfers between devices, moved(): lax.ppermute(array, axis, [((i + step) % peers, i) for i in range(peers)])  10.3 us
    ppermute x1, starting transfers between devices, on_device(): across = lax.ppermute(grad, DP, [(0, 3), (1, 2), (2, 1), (3, 0)])  5.81 us
    pallas_call x1, Pallas kernels, to_send(): pl.pallas_call(functools.partial(send_kernel, peers), out_shape=jax.Shape...  4.4 us
    pallas_call x1, Pallas kernels, positions(): pl.pallas_call(functools.partial(position_kernel, entries, peers), out_sh...  2.2 us
    ppermute x3, starting transfers between devices, swapped(): return lax.ppermute(array, axis, [(0, 1), (1, 0)])  1.94 us
  transfers between devices with their start and end apart: 11, of which 5 were waited for; matrix products, arithmetic and copies ran while one was open for 2% of the time, Pallas kernels for 7%

profile of v14, /device:TPU:1, one launch (start us, length us, event | category | flops | bytes accessed | tf_op | source)
XLA Modules:
  0.0 95.8 jit_solution(16163061468197411384)
XLA Ops:
  0.7 1.0 %pad_maximum_fusion = bf16[128,1024]{1,0:T(8,128)(2,1)S(1)} fusion(bf16[64,1024]{1,0:T(8,128)(2,1)} %param.17, bf16[64,1024]{1,0:T(8,128)(2,1)} %bitcast.64), kind=kLoop, calls=%fused_computation.16 | loop fusion | flops 524288 | bytes 524288 | tf_op jit(solution)/shard_map/concatenate | solution.py:204
  1.7 6.9 %collective-permute-start = (bf16[128,1024]{1,0:T(8,128)(2,1)S(1)}, bf16[128,1024]{1,0:T(8,128)(2,1)S(1)}, u32[]{:S(2)}, u32[]{:S(2)}) collective-permute-start(bf16[128,1024]{1,0:T(8,128)(2,1)S(1)} %pad_maximum_fusion), channel_id=1, source_target_pairs={{8,0},{16,8},{24,16},{0,24},{9,1},{17,9},{25,17},{1,25},{10,2},{18... | collective-permute-start | bytes 786440 | tf_op jit(solution)/shard_map/ppermute | solution.py:28
  8.6 3.3 %collective-permute-start.2 = (bf16[64,1024]{1,0:T(8,128)(2,1)S(1)}, bf16[64,1024]{1,0:T(8,128)(2,1)S(1)}, u32[]{:S(2)}, u32[]{:S(2)}) collective-permute-start(bf16[64,1024]{1,0:T(8,128)(2,1)S(1)} %bitcast.61), channel_id=1, source_target_pairs={{16,0},{24,8},{0,16},{8,24},{17,1},{25,9},{1,17},{9,25},{18,2},{26... | collective-permute-start | bytes 393224 | tf_op jit(solution)/shard_map/ppermute | solution.py:28
  12.0 4.4 %send_rows.2.after = bf16[64,2,640]{2,1,0:T(2,128)(2,1)} custom-call(s32[1]{0:T(128)} %bitcast.5.place_ref, s32[1]{0:T(128)} %constant.33.clone.1.trip_ref, s32[3,8]{1,0:T(4,128)} %bitcast.65, s32[8,61]{1,0:T(8,128)} %words_v.1, f32[1,16]{1,0:T(1,128)} %bitcast.69, f32[1,16]{1,0:T(1,128)} %bitcast.72, bf16[2048,1024]{1,0:T(8,128)(2,1)} %table.1), custom_call_target="tpu_custom_call" | custom-call | tf_op jit(solution)/shard_map/send_rows/pallas_call | solution.py:120
  16.4 10.5 %all-to-all-start.1 = ((bf16[64,2,640]{2,1,0:T(2,128)(2,1)}), bf16[64,2,640]{2,1,0:T(2,128)(2,1)S(1)}, u32[]{:S(2)}, u32[]{:S(2)}) async-start(bf16[64,2,640]{2,1,0:T(2,128)(2,1)} %send_rows.2.after), calls=%async_computation.1 | async-start | bytes 327680 | tf_op jit(solution)/shard_map/all_to_all | solution.py:19
  26.9 2.2 %positions.1 = (s32[8,64]{1,0:T(8,128)}, s32[1]{0:T(128)}) custom-call(s32[3,8]{1,0:T(4,128)S(1)} %bitcast.66, s32[8,61]{1,0:T(8,128)S(1)} %copy-done, s32[8,61]{1,0:T(8,128)S(1)} %copy-done, bf16[64,2,640]{2,1,0:T(2,128)(2,1)} %send_rows.2.after), custom_call_target="tpu_custom_call" | custom-call | bytes 40000000 | tf_op jit(solution)/shard_map/positions/pallas_call | solution.py:168
  29.1 1.5 %collective-permute-start.3 = (bf16[64,1024]{1,0:T(8,128)(2,1)S(1)}, bf16[64,1024]{1,0:T(8,128)(2,1)S(1)}, u32[]{:S(2)}, u32[]{:S(2)}) collective-permute-start(bf16[64,1024]{1,0:T(8,128)(2,1)S(1)} %collective-permute-done.2), channel_id=1, source_target_pairs={{0,64},{64,0},{1,65},{65,1},{2,66},{66,2},{3,67},{67,3},{4,68},{68... | collective-permute-start | bytes 393224 | tf_op jit(solution)/shard_map/ppermute | solution.py:32
  30.7 8.3 %all-to-all-done.1 = bf16[64,2,640]{2,1,0:T(2,128)(2,1)S(1)} async-done(((bf16[64,2,640]{2,1,0:T(2,128)(2,1)}), bf16[64,2,640]{2,1,0:T(2,128)(2,1)S(1)}, u32[]{:S(2)}, u32[]{:S(2)}) %all-to-all-start.1) | async-done | bytes 163872 | tf_op jit(solution)/shard_map/all_to_all | solution.py:19
  39.5 0.7 while.10
  40.5 0.7 broadcast_in_dim.31
  41.2 3.5 %all-to-all-start.2 = ((bf16[16,8,1024]{2,1,0:T(8,128)(2,1)}), bf16[16,8,1024]{2,1,0:T(8,128)(2,1)S(1)}, u32[]{:S(2)}, u32[]{:S(2)}) async-start(bf16[16,8,1024]{2,1,0:T(8,128)(2,1)} %broadcast_in_dim.31), calls=%async_computation.2 | async-start | bytes 524288 | tf_op jit(solution)/shard_map/all_to_all | solution.py:19
  44.8 8.6 %all-to-all-done.2 = bf16[16,8,1024]{2,1,0:T(8,128)(2,1)S(1)} async-done(((bf16[16,8,1024]{2,1,0:T(8,128)(2,1)}), bf16[16,8,1024]{2,1,0:T(8,128)(2,1)S(1)}, u32[]{:S(2)}, u32[]{:S(2)}) %all-to-all-start.2) | async-done | bytes 262176 | tf_op jit(solution)/shard_map/all_to_all | solution.py:19
  53.4 1.6 %fusion.4 = bf16[16,8,1024]{2,1,0:T(8,128)(2,1)} fusion(bf16[256,1024]{1,0:T(8,128)(2,1)S(1)} %get-tuple-element.95, bf16[256,1024]{1,0:T(8,128)(2,1)S(1)} %get-tuple-element.94, bf16[16,8,1024]{2,1,0:T(8,128)(2,1)S(1)} %all-to-all-done.2), kind=kOutput, calls=%fused_computation.10 | convolution fusion | flops 136478720 | bytes 1572864 | tf_op jit(solution)/shard_map/dot_general | solution.py:248
  55.0 3.5 %all-to-all-start.3 = ((bf16[16,8,1024]{2,1,0:T(8,128)(2,1)}), bf16[16,8,1024]{2,1,0:T(8,128)(2,1)S(1)}, u32[]{:S(2)}, u32[]{:S(2)}) async-start(bf16[16,8,1024]{2,1,0:T(8,128)(2,1)} %fusion.4), calls=%async_computation.3 | async-start | bytes 524288 | tf_op jit(solution)/shard_map/all_to_all | solution.py:19
  58.9 8.3 %all-to-all-done.3 = bf16[16,8,1024]{2,1,0:T(8,128)(2,1)S(1)} async-done(((bf16[16,8,1024]{2,1,0:T(8,128)(2,1)}), bf16[16,8,1024]{2,1,0:T(8,128)(2,1)S(1)}, u32[]{:S(2)}, u32[]{:S(2)}) %all-to-all-start.3) | async-done | bytes 262176 | tf_op jit(solution)/shard_map/all_to_all | solution.py:19
  68.1 0.7 copy.45
  68.8 6.2 %all-to-all-start.4 = ((f32[64,2,128]{2,1,0:T(2,128)}), f32[64,2,128]{2,1,0:T(2,128)S(1)}, u32[]{:S(2)}, u32[]{:S(2)}) async-start(f32[64,2,128]{2,1,0:T(2,128)} %copy.45), calls=%async_computation.4 | async-start | bytes 131072 | tf_op jit(solution)/shard_map/all_to_all | solution.py:19
  75.2 10.9 %all-to-all-done.4 = f32[64,2,128]{2,1,0:T(2,128)S(1)} async-done(((f32[64,2,128]{2,1,0:T(2,128)}), f32[64,2,128]{2,1,0:T(2,128)S(1)}, u32[]{:S(2)}, u32[]{:S(2)}) %all-to-all-start.4) | async-done | bytes 65568 | tf_op jit(solution)/shard_map/all_to_all | solution.py:19
  86.4 0.3 fusion.5
  87.3 0.5 fusion.62
  87.9 0.4 collective-permute-start.5
  88.3 5.8 %collective-permute-start.6 = (f32[16]{0:T(128)S(1)}, f32[16]{0:T(128)S(1)}, u32[]{:S(2)}, u32[]{:S(2)}) collective-permute-start(f32[16]{0:T(128)S(1)} %multiply_reduce_fusion.3), channel_id=1, source_target_pairs={{0,192},{64,128},{128,64},{192,0},{1,193},{65,129},{129,65},{193,1... | collective-permute-start | bytes 200 | tf_op jit(solution)/shard_map/ppermute | solution.py:271
  94.1 1.2 %collective-permute-done.6 = f32[16]{0:T(128)S(1)} collective-permute-done((f32[16]{0:T(128)S(1)}, f32[16]{0:T(128)S(1)}, u32[]{:S(2)}, u32[]{:S(2)}) %collective-permute-start.6) | collective-permute-done | bytes 96 | tf_op jit(solution)/shard_map/ppermute | solution.py:271
  95.3 0.5 add_add_fusion
  (67 shorter events, 3.1 us)
Async XLA Ops:
  0.6 26.2 %copy-start.1 = (s32[8,3]{0,1:T(4,128)S(1)}, s32[8,3]{0,1:T(4,128)}, u32[]{:S(2)}) copy-start(s32[8,3]{0,1:T(4,128)} %param.12) | copy-start | bytes 292
  0.6 26.2 %copy-start = (s32[8,61]{1,0:T(8,128)S(1)}, s32[8,61]{1,0:T(8,128)}, u32[]{:S(2)}) copy-start(s32[8,61]{1,0:T(8,128)} %words_v.1) | copy-start | bytes 5860
  0.7 38.8 %copy-start.3 = (f32[16]{0:T(128)S(1)}, f32[16]{0:T(128)}, u32[]{:S(2)}) copy-start(f32[16]{0:T(128)} %param.18) | copy-start | bytes 196
  0.7 38.8 %copy-start.4 = (f32[16]{0:T(128)S(1)}, f32[16]{0:T(128)}, u32[]{:S(2)}) copy-start(f32[16]{0:T(128)} %param.19) | copy-start | bytes 196
  1.7 29.0 %collective-permute-start = (bf16[128,1024]{1,0:T(8,128)(2,1)S(1)}, bf16[128,1024]{1,0:T(8,128)(2,1)S(1)}, u32[]{:S(2)}, u32[]{:S(2)}) collective-permute-start(bf16[128,1024]{1,0:T(8,128)(2,1)S(1)} %pad_maximum_fusion), channel_id=1, source_target_pairs={{8,0},{16,8},{24,16},{0,24},{9,1},{17,9},{25,17},{1,25},{10,2},{18... | collective-permute-start | bytes 786440 | tf_op jit(solution)/shard_map/ppermute | solution.py:28
  8.6 36.1 %collective-permute-start.1 = (bf16[128,1024]{1,0:T(8,128)(2,1)S(1)}, bf16[128,1024]{1,0:T(8,128)(2,1)S(1)}, u32[]{:S(2)}, u32[]{:S(2)}) collective-permute-start(bf16[128,1024]{1,0:T(8,128)(2,1)S(1)} %pad_maximum_fusion), channel_id=1, source_target_pairs={{24,0},{0,8},{8,16},{16,24},{25,1},{1,9},{9,17},{17,25},{26,2},{2,... | collective-permute-start | bytes 786440 | tf_op jit(solution)/shard_map/ppermute | solution.py:28
  8.6 20.5 %collective-permute-start.2 = (bf16[64,1024]{1,0:T(8,128)(2,1)S(1)}, bf16[64,1024]{1,0:T(8,128)(2,1)S(1)}, u32[]{:S(2)}, u32[]{:S(2)}) collective-permute-start(bf16[64,1024]{1,0:T(8,128)(2,1)S(1)} %bitcast.61), channel_id=1, source_target_pairs={{16,0},{24,8},{0,16},{8,24},{17,1},{25,9},{1,17},{9,25},{18,2},{26... | collective-permute-start | bytes 393224 | tf_op jit(solution)/shard_map/ppermute | solution.py:28
  16.4 22.6 %all-to-all-start.1 = ((bf16[64,2,640]{2,1,0:T(2,128)(2,1)}), bf16[64,2,640]{2,1,0:T(2,128)(2,1)S(1)}, u32[]{:S(2)}, u32[]{:S(2)}) async-start(bf16[64,2,640]{2,1,0:T(2,128)(2,1)} %send_rows.2.after), calls=%async_computation.1 | async-start | bytes 327680 | tf_op jit(solution)/shard_map/all_to_all | solution.py:19
  29.1 15.7 %collective-permute-start.3 = (bf16[64,1024]{1,0:T(8,128)(2,1)S(1)}, bf16[64,1024]{1,0:T(8,128)(2,1)S(1)}, u32[]{:S(2)}, u32[]{:S(2)}) collective-permute-start(bf16[64,1024]{1,0:T(8,128)(2,1)S(1)} %collective-permute-done.2), channel_id=1, source_target_pairs={{0,64},{64,0},{1,65},{65,1},{2,66},{66,2},{3,67},{67,3},{4,68},{68... | collective-permute-start | bytes 393224 | tf_op jit(solution)/shard_map/ppermute | solution.py:32
  39.5 0.9 copy-start.2
  40.2 18.3 %copy-start.6 = (s32[8,64]{1,0:T(8,128)S(1)}, s32[8,64]{1,0:T(8,128)}, u32[]{:S(2)}) copy-start(s32[8,64]{1,0:T(8,128)} %get-tuple-element.55) | copy-start | bytes 6148
  41.2 12.2 %all-to-all-start.2 = ((bf16[16,8,1024]{2,1,0:T(8,128)(2,1)}), bf16[16,8,1024]{2,1,0:T(8,128)(2,1)S(1)}, u32[]{:S(2)}, u32[]{:S(2)}) async-start(bf16[16,8,1024]{2,1,0:T(8,128)(2,1)} %broadcast_in_dim.31), calls=%async_computation.2 | async-start | bytes 524288 | tf_op jit(solution)/shard_map/all_to_all | solution.py:19
  44.7 42.5 %copy-start.7 = (s32[8]{0:T(128)S(1)}, s32[8]{0:T(128)}, u32[]{:S(2)}) copy-start(s32[8]{0:T(128)} %param.14) | copy-start | bytes 100
  55.0 12.2 %all-to-all-start.3 = ((bf16[16,8,1024]{2,1,0:T(8,128)(2,1)}), bf16[16,8,1024]{2,1,0:T(8,128)(2,1)S(1)}, u32[]{:S(2)}, u32[]{:S(2)}) async-start(bf16[16,8,1024]{2,1,0:T(8,128)(2,1)} %fusion.4), calls=%async_computation.3 | async-start | bytes 524288 | tf_op jit(solution)/shard_map/all_to_all | solution.py:19
  68.8 17.3 %all-to-all-start.4 = ((f32[64,2,128]{2,1,0:T(2,128)}), f32[64,2,128]{2,1,0:T(2,128)S(1)}, u32[]{:S(2)}, u32[]{:S(2)}) async-start(f32[64,2,128]{2,1,0:T(2,128)} %copy.45), calls=%async_computation.4 | async-start | bytes 131072 | tf_op jit(solution)/shard_map/all_to_all | solution.py:19
  86.7 9.1 %copy-start.5 = (bf16[16,512]{1,0:T(8,128)(2,1)}, bf16[16,512]{1,0:T(8,128)(2,1)S(1)}, u32[]{:S(2)}) copy-start(bf16[16,512]{1,0:T(8,128)(2,1)S(1)} %fusion.5) | copy-start | bytes 49156
  87.9 6.2 %collective-permute-start.5 = (f32[16]{0:T(128)S(1)}, f32[16]{0:T(128)S(1)}, u32[]{:S(2)}, u32[]{:S(2)}) collective-permute-start(f32[16]{0:T(128)S(1)} %multiply_reduce_fusion.3), channel_id=1, source_target_pairs={{0,128},{128,0},{1,129},{129,1},{2,130},{130,2},{3,131},{131,3},{4... | collective-permute-start | bytes 200 | tf_op jit(solution)/shard_map/ppermute | solution.py:32
  88.3 7.0 %collective-permute-start.6 = (f32[16]{0:T(128)S(1)}, f32[16]{0:T(128)S(1)}, u32[]{:S(2)}, u32[]{:S(2)}) collective-permute-start(f32[16]{0:T(128)S(1)} %multiply_reduce_fusion.3), channel_id=1, source_target_pairs={{0,192},{64,128},{128,64},{192,0},{1,193},{65,129},{129,65},{193,1... | collective-permute-start | bytes 200 | tf_op jit(solution)/shard_map/ppermute | solution.py:271
  94.1 1.2 %collective-permute-start.4 = (f32[16]{0:T(128)S(1)}, f32[16]{0:T(128)S(1)}, u32[]{:S(2)}, u32[]{:S(2)}) collective-permute-start(f32[16]{0:T(128)S(1)} %multiply_reduce_fusion.3), channel_id=1, source_target_pairs={{0,64},{64,0},{1,65},{65,1},{2,66},{66,2},{3,67},{67,3},{4,68},{68... | collective-permute-start | bytes 200 | tf_op jit(solution)/shard_map/ppermute | solution.py:32
